TPU v7x, 32 devices: a whole 2x2x4 slice. The times are simulated.
32 devices in a mesh: facet: 4 (over y, x), team: 8 (over z, core).
Axes of the slice: x: 2, y: 2, z: 4, core: 2. Of those that a mesh axis runs over, the one named last changes fastest.
Arguments:
- facets: float32 [4, 2, 512, 5120], P('facet', None, 'team'), may hold values from -6 to 6
- facet_offsets: int32 [4], replicated, may hold values from 0 to 65535
- grid_offsets: int32 [8], replicated, may hold values from 0 to 65535
- taper: float32 [512], replicated, may hold values from 0.3 to 3
- kernels: float32 [16, 2, 512], replicated, may hold values from -4 to 4
- kernel_index: int32 [8, 512], P('facet', 'team'), may hold values from 0 to 15
- residual: float32 [8, 2, 512, 512], P('facet', None, 'team'), may hold values from -6 to 6
Outputs:
- facet_update: float32 [4, 2, 512, 5120], P('facet', None, 'team')
All inputs are finite; a program needn't handle non-finite values.
Results may differ from a plain program's by a relative error of at most 0.0003.
Values sent between devices are 32-bit elements; how exact they have to be, the bound alone decides.
No kernel may reach another device: no remote copies, remote signals or barrier semaphores. Data moves between devices by JAX's collectives and lax.ppermute only.
A program may use at most 64 MiB of HBM per device.

v0:
```python
import functools
import math

import jax
import jax.numpy as jnp
import numpy as np
from jax import lax
from jax.experimental import pallas as pl
from jax.experimental.pallas import tpu as pltpu
from jax.sharding import PartitionSpec as P


N_IMG = 65536
FACET_LEN = 5120
LANES = 128


def mod_product(left, right):
    low_part = right % 256
    high_part = right // 256
    return (left * low_part + left * high_part % 256 * 256) % N_IMG


def window_start(grid_offset):
    return grid_offset * FACET_LEN // N_IMG


def phase_pair(facet_offset, grid_offset, length):
    position = (grid_offset + jnp.arange(length, dtype=jnp.int32)) % N_IMG
    angle = mod_product(facet_offset, position).astype(jnp.float32) * (2.0 * math.pi / N_IMG)
    return (jnp.cos(angle), jnp.sin(angle))


def split_table(length):
    index = np.arange(length)
    angle = (index[:, None] * index[None, :] % length) * (2.0 * np.pi / length)
    table = np.concatenate([np.cos(angle), np.sin(angle)], axis=1) / math.sqrt(length)
    high = table.astype(jnp.bfloat16)
    low = (table - high.astype(np.float64)).astype(jnp.bfloat16)
    return np.stack([high, low])


def product(values, high_table, low_table):
    high = values.astype(jnp.bfloat16)
    low = (values - high.astype(jnp.float32)).astype(jnp.bfloat16)

    def dot(left, right):
        return jnp.dot(left, right, preferred_element_type=jnp.float32)

    return dot(high, high_table) + (dot(low, high_table) + dot(high, low_table))


def rotate(values, high_table, low_table, sign):
    rows = values.shape[0] // 2
    both = product(values, high_table, low_table)
    length = both.shape[1] // 2
    real = both[:rows, :length] - sign * both[rows:, length:]
    imag = both[rows:, :length] + sign * both[:rows, length:]
    return real, imag


def lane_block(index):
    return pl.ds(pl.multiple_of(index * LANES, LANES), LANES)


def begin_of(offset):
    return lax.div(offset * FACET_LEN, N_IMG)


def phase_factor(offsets, facet_offset, taper, factor):
    count, _, length = factor.shape
    row = lax.broadcasted_iota(jnp.int32, (count, length), 0)
    position = lax.broadcasted_iota(jnp.int32, (count, length), 1)
    for item in range(count):
        position = position + jnp.where(row == item, offsets[item], 0)
    position = lax.bitwise_and(position, N_IMG - 1)
    low_part = lax.bitwise_and(position, 255)
    high_part = lax.shift_right_logical(position, 8)
    high_product = lax.bitwise_and(facet_offset * high_part, 255) * 256
    product = lax.bitwise_and(facet_offset * low_part + high_product, N_IMG - 1)
    angle = product.astype(jnp.float32) * (2.0 * math.pi / N_IMG)
    real = jnp.cos(angle) * taper
    imag = jnp.sin(angle) * taper
    for item in range(count):
        factor[item, 0:1, :] = real[item : item + 1, :]
        factor[item, 1:2, :] = imag[item : item + 1, :]


def cut_windows(offsets, ids, columns, outs, buffer, sems, prepare, factor):
    count = len(outs)
    total = columns.shape[3] // LANES
    blocks = factor.shape[2] // LANES

    def copy(item, piece):
        source = lax.rem(lax.div(begin_of(offsets[ids[item]]), LANES) + piece, total)
        return pltpu.make_async_copy(
            columns.at[0, :, :, lane_block(source)],
            buffer.at[item, :, :, pl.ds(piece * LANES, LANES)],
            sems.at[item, piece],
        )

    for item in range(count):
        for piece in range(blocks + 1):
            copy(item, piece).start()
    prepare()
    lane = lax.broadcasted_iota(jnp.int32, (columns.shape[2], LANES), 1)
    for item in range(count):
        for piece in range(blocks + 1):
            copy(item, piece).wait()
        shift = lax.rem(begin_of(offsets[ids[item]]), LANES)
        back = lax.rem(LANES - shift, LANES)
        keep = lane < LANES - shift
        for piece in range(blocks):
            span = pl.ds(piece * LANES, LANES)
            after = pl.ds((piece + 1) * LANES, LANES)
            parts = []
            for part in range(2):
                first = pltpu.roll(buffer[item, part, :, span], back, 1)
                second = pltpu.roll(buffer[item, part, :, after], back, 1)
                parts.append(jnp.where(keep, first, second))
            real, imag = parts
            factor_real = factor[ids[item], 0:1, span]
            factor_imag = factor[ids[item], 1:2, span]
            outs[item][0][:, span] = real * factor_real - imag * factor_imag
            outs[item][1][:, span] = real * factor_imag + imag * factor_real


def corner_window_kernel(
    per_facet, ids, offsets_hbm, facet_offsets_hbm, taper_hbm, columns, *refs
):
    factor, planes = refs[0], refs[1:-6]
    buffer, sems, offsets, facet_offsets, taper, small_sems = refs[-6:]
    small = [
        pltpu.make_async_copy(offsets_hbm, offsets, small_sems.at[0]),
        pltpu.make_async_copy(facet_offsets_hbm, facet_offsets, small_sems.at[1]),
        pltpu.make_async_copy(taper_hbm, taper, small_sems.at[2]),
    ]
    for copy in small:
        copy.start()
    small[0].wait()
    outs = [
        (planes[2 * step].at[chunk], planes[2 * step + 1].at[chunk])
        for step in range(len(planes) // 2)
        for chunk in range(per_facet)
    ]

    def prepare():
        small[1].wait()
        small[2].wait()
        phase_factor(offsets, facet_offsets[ids[len(outs)]], taper[...], factor)

    cut_windows(offsets, ids, columns, outs, buffer, sems, prepare, factor)


def window_kernel(offsets, ids, columns, factor, *refs):
    planes, (buffer, sems) = refs[:-2], refs[-2:]
    outs = [(plane.at[0], plane.at[1]) for plane in planes]
    cut_windows(offsets, ids, columns, outs, buffer, sems, lambda: None, factor)


def join_kernel(part, chunk, term, *refs):
    received, out = refs[:-1], refs[-1]
    total = term[part]
    for corner in received:
        total = total + corner[chunk]
    out[part] = total
    out[1 - part] = term[1 - part]


def split_out(values, chip, outs):
    for distance, out in enumerate(outs):
        out[...] = values[:, :, lane_block(jnp.bitwise_xor(chip, distance))]


def first_kernel(place, table, *refs):
    scratch = refs[-1]
    chips = scratch.shape[2] // LANES
    terms, outs = refs[: -1 - chips], refs[-1 - chips : -1]
    total = terms[0][...]
    for term in terms[1:]:
        total = total + term[...]
    rows, length = total.shape[1:]
    real, imag = rotate(total.reshape(2 * rows, length), table[0], table[1], -1.0)
    scratch[0] = real
    scratch[1] = imag
    split_out(scratch, place[0], outs)


def cross_kernel(sign, place, table, *refs):
    blocks, (keep, send, gathered, partial) = refs[:-4], refs[-4:]
    chip, core = place[0], place[1]
    rows = blocks[0].shape[1]
    for distance, block in enumerate(blocks):
        spot = pl.ds(pl.multiple_of(jnp.bitwise_xor(chip, distance) * rows, rows), rows)
        gathered[0, spot, :] = block[0]
        gathered[1, spot, :] = block[1]
    values = jnp.concatenate([gathered[0].T, gathered[1].T], axis=0)

    def own(half):
        pieces = [
            table[half, pl.ds(pl.multiple_of((2 * index + core) * rows, rows), rows), :]
            for index in range(len(blocks))
        ]
        return jnp.concatenate(pieces, axis=0)

    real, imag = rotate(values, own(0), own(1), sign)
    partial[0] = real
    partial[1] = imag
    mine = pl.ds(pl.multiple_of(core * rows, rows), rows)
    other = pl.ds(pl.multiple_of((1 - core) * rows, rows), rows)
    keep[...] = partial[:, mine, :]
    send[...] = partial[:, other, :]


def correct_kernel(place, table, keep, received, residual, chosen, *refs):
    outs, scratch = refs[:-1], refs[-1]
    spectrum_real = keep[0] + received[0]
    spectrum_imag = keep[1] + received[1]
    real = residual[0] - (chosen[0] * spectrum_real - chosen[1] * spectrum_imag)
    imag = residual[1] - (chosen[0] * spectrum_imag + chosen[1] * spectrum_real)
    values = jnp.concatenate([real, imag], axis=0)
    real, imag = rotate(values, table[0], table[1], 1.0)
    scratch[0] = real
    scratch[1] = imag
    split_out(scratch, place[0], outs)


def turned_pieces(offset, factor, real_ref, imag_ref):
    rows, length = real_ref.shape
    blocks = length // LANES
    begin = begin_of(offset)
    shift = lax.rem(begin, LANES)
    lane = lax.broadcasted_iota(jnp.int32, (rows, LANES), 1)
    late = lane >= shift
    empty = jnp.zeros((rows, LANES), jnp.float32)
    earlier = [empty, empty]
    pieces = []
    for piece in range(blocks + 1):
        turned = [empty, empty]
        if piece < blocks:
            span = pl.ds(piece * LANES, LANES)
            real, imag = real_ref[:, span], imag_ref[:, span]
            factor_real, factor_imag = factor[0:1, span], factor[1:2, span]
            turned = [
                pltpu.roll(real * factor_real + imag * factor_imag, shift, 1),
                pltpu.roll(imag * factor_real - real * factor_imag, shift, 1),
            ]
        pieces.append([jnp.where(late, turned[part], earlier[part]) for part in range(2)])
        earlier = turned
    return lax.div(begin, LANES), pieces


def update_kernel(layout, offsets, ids, factor, *refs):
    arrays, (out, window) = list(refs[:-2]), refs[-2:]
    pairs = []
    for planes in layout:
        if planes == 1:
            whole = arrays.pop(0)
            pairs.append((whole.at[0], whole.at[1]))
        else:
            pairs.append((arrays.pop(0), arrays.pop(0)))
    count = len(pairs)
    total = out.shape[3] // LANES
    out[...] = jnp.zeros(out.shape, jnp.float32)
    for item in range(count):
        block, pieces = turned_pieces(
            offsets[ids[item]], factor.at[ids[item]], *pairs[item]
        )
        for piece, parts in enumerate(pieces):
            spot = lane_block(lax.rem(block + piece, total))
            for part in range(2):
                out[0, part, :, spot] += parts[part]
    block = lax.div(begin_of(offsets[ids[count]]), LANES)
    for piece in range(window.shape[2] // LANES):
        spot = lane_block(lax.rem(block + piece, total))
        window[:, :, pl.ds(piece * LANES, LANES)] = out[0, :, :, spot]


def finish_kernel(offsets, ids, factor, window, real, imag, whole, out, buffer, sems):
    total = out.shape[3] // LANES
    item = ids[0]
    block, pieces = turned_pieces(offsets[item], factor.at[item], real, imag)

    def copy(piece):
        return pltpu.make_async_copy(
            buffer.at[piece],
            out.at[0, :, :, lane_block(lax.rem(block + piece, total))],
            sems.at[piece],
        )

    for piece, parts in enumerate(pieces):
        span = pl.ds(piece * LANES, LANES)
        for part in range(2):
            buffer[piece, part] = window[part, :, span] + parts[part]
        copy(piece).start()
    for piece in range(len(pieces)):
        copy(piece).wait()


VMEM = pl.BlockSpec(memory_space=pltpu.VMEM)
SMEM = pl.BlockSpec(memory_space=pltpu.SMEM)
HBM = pl.BlockSpec(memory_space=pltpu.HBM)
MIB = 1 << 20


def call(kernel, outs, scratch, specs, limit, cost, **kwargs):
    return pl.pallas_call(
        kernel,
        out_shape=[jax.ShapeDtypeStruct(shape, jnp.float32) for shape in outs],
        in_specs=specs,
        out_specs=kwargs.pop("out_specs", [VMEM] * len(outs)),
        scratch_shapes=scratch,
        compiler_params=pltpu.CompilerParams(vmem_limit_bytes=limit),
        cost_estimate=pl.CostEstimate(flops=cost, bytes_accessed=cost // 64, transcendentals=0),
        **kwargs,
    )


def grid_of(count):
    slow = max(step for step in range(1, math.isqrt(count) + 1) if count % step == 0)
    return slow, count // slow


def tiled_device(
    facet_count, team_count, facets, facet_offsets, grid_offsets, taper, kernels, kernel_index, residual
):
    rows = facets.shape[2]
    length = taper.shape[0]
    facet_len = facets.shape[3]
    blocks = length // LANES
    chips = team_count // 2
    per_facet = residual.shape[0]
    subgrids = grid_offsets.shape[0]
    slow, fast = grid_of(facet_count)
    facet = lax.axis_index("facet")
    team = lax.axis_index("team")
    place = jnp.stack([team // 2, team % 2]).astype(jnp.int32)
    table = jnp.asarray(split_table(length))
    down, right = facet // fast, facet % fast

    def near(step, chunk):
        to = (down + step[0]) % slow * fast + (right + step[1]) % fast
        return to * per_facet + chunk

    def listed(values):
        return jnp.stack(values).astype(jnp.int32)

    def move(value, step_slow, step_fast):
        pairs = [
            (
                spot,
                (spot // fast + step_slow) % slow * fast + (spot % fast + step_fast) % fast,
            )
            for spot in range(facet_count)
        ]
        return lax.ppermute(value, "facet", pairs)

    def exchange(pieces):
        out = [pieces[0]]
        for distance in range(1, chips):
            pairs = [
                (spot, (spot // 2 ^ distance) * 2 + spot % 2) for spot in range(team_count)
            ]
            out.append(lax.ppermute(pieces[distance], "team", pairs))
        return out

    def swap(value):
        return lax.ppermute(value, "team", [(spot, spot ^ 1) for spot in range(team_count)])

    slow_steps, fast_steps = range(1, slow), range(1, fast)
    near_steps = [(0, j) for j in fast_steps] + [(i, 0) for i in slow_steps]
    corner_steps = [(i, j) for i in slow_steps for j in fast_steps]
    onehot = (kernel_index[:, :, None] == jnp.arange(kernels.shape[0], dtype=jnp.int32)).astype(
        jnp.float32
    )
    chosen = jnp.einsum("srk,kac->sarc", onehot, kernels, precision=lax.Precision.HIGHEST)
    block_shape = (2, rows, length)
    piece_shape = (2, rows, LANES)
    matmul_cost = 2 * (2 * rows) * length * (2 * length) * 3
    chunks = range(per_facet)

    def window_scratch(count):
        return [
            pltpu.VMEM((count, 2, rows, length + LANES), jnp.float32),
            pltpu.SemaphoreType.DMA((count, blocks + 1)),
        ]

    def in_hbm(value):
        return pltpu.with_memory_space_constraint(value, pltpu.HBM)

    columns = in_hbm(facets)
    corner_keys = [(step, chunk) for step in corner_steps for chunk in chunks]
    factor, *planes = call(
        functools.partial(corner_window_kernel, per_facet),
        [(subgrids, 2, length)] + [(per_facet, rows, length)] * (2 * len(corner_steps)),
        window_scratch(len(corner_keys))
        + [
            pltpu.SMEM(grid_offsets.shape, jnp.int32),
            pltpu.SMEM(facet_offsets.shape, jnp.int32),
            pltpu.VMEM((1, length), jnp.float32),
            pltpu.SemaphoreType.DMA((3,)),
        ],
        [SMEM, HBM, HBM, HBM, HBM],
        8 * MIB,
        matmul_cost // 8,
    )(
        listed([near(step, chunk) for step, chunk in corner_keys] + [facet]),
        in_hbm(grid_offsets),
        in_hbm(facet_offsets),
        in_hbm(taper.reshape(1, length)),
        columns,
    )
    by_fast, by_slow = {}, {}
    for spot, (i, j) in enumerate(corner_steps):
        by_fast[i, j] = move(planes[2 * spot], 0, j)
        by_slow[i, j] = move(planes[2 * spot + 1], i, 0)

    near_keys = [(step, chunk) for chunk in chunks for step in [(0, 0)] + near_steps]
    outs = call(
        window_kernel,
        [block_shape] * len(near_keys),
        window_scratch(len(near_keys)),
        [SMEM, SMEM, HBM, VMEM],
        12 * MIB,
        matmul_cost // 4,
    )(grid_offsets, listed([near(step, chunk) for step, chunk in near_keys]), columns, factor)
    terms = dict(zip(near_keys, outs))

    def join(term, corners, part, chunk):
        if not corners:
            return term
        (joined,) = call(
            functools.partial(join_kernel, part, chunk),
            [block_shape],
            [],
            [VMEM] * (1 + len(corners)),
            2 * MIB,
            matmul_cost // 64,
        )(term, *corners)
        return joined

    def scatter(chunk):
        received = [terms[(0, 0), chunk]]
        for i in slow_steps:
            corners = [by_fast[i, j] for j in fast_steps]
            joined = join(terms[(i, 0), chunk], corners, 0, chunk)
            received.append(move(joined, i, 0))
        for j in fast_steps:
            corners = [by_slow[i, j] for i in slow_steps]
            joined = join(terms[(0, j), chunk], corners, 1, chunk)
            received.append(move(joined, 0, j))
        return received

    def first_transform(received):
        return call(
            first_kernel,
            [piece_shape] * chips,
            [pltpu.VMEM(block_shape, jnp.float32)],
            [SMEM, VMEM] + [VMEM] * len(received),
            8 * MIB,
            matmul_cost,
        )(place, table, *received)

    def cross(pieces, sign):
        return call(
            functools.partial(cross_kernel, sign),
            [block_shape] * 2,
            [
                pltpu.VMEM((2, chips * rows, LANES), jnp.float32),
                pltpu.VMEM((2, LANES, length), jnp.float32),
            ],
            [SMEM, VMEM] + [VMEM] * chips,
            8 * MIB,
            matmul_cost,
        )(place, table, *pieces)

    def correct(keep, received, chunk):
        return call(
            correct_kernel,
            [piece_shape] * chips,
            [pltpu.VMEM(block_shape, jnp.float32)],
            [SMEM] + [VMEM] * 5,
            8 * MIB,
            matmul_cost,
        )(place, table, keep, received, residual[chunk], chosen[chunk])

    def gather(own):
        found = {(0, 0): (own,)}
        for j in fast_steps:
            found[0, j] = (move(own, 0, j),)
        for i in slow_steps:
            found[i, 0] = (move(own, i, 0),)
        for i, j in corner_steps:
            found[i, j] = (move(found[0, j][0][0], i, 0), move(found[i, 0][0][1], 0, j))
        return found

    received = [scatter(chunk) for chunk in chunks]
    pieces = [exchange(first_transform(received[chunk])) for chunk in chunks]
    halves = [cross(pieces[chunk], -1.0) for chunk in chunks]
    swapped = [swap(halves[chunk][1]) for chunk in chunks]
    pieces = [exchange(correct(halves[chunk][0], swapped[chunk], chunk)) for chunk in chunks]
    halves = [cross(pieces[chunk], 1.0) for chunk in chunks]
    ids, items = [], []
    for chunk in chunks:
        keep, sent = halves[chunk]
        own = keep + swap(sent)
        for (i, j), found in gather(own).items():
            ids.append(near((-i, -j), chunk))
            items.append(found)
    ids = listed(ids)
    *first_items, last_item = items
    if len(last_item) == 1:
        last_item = (last_item[0][0], last_item[0][1])
    arrays = [array for item in first_items for array in item]
    whole, window = call(
        functools.partial(update_kernel, tuple(len(item) for item in first_items)),
        [(1, 2, rows, facet_len), (2, rows, length + LANES)],
        [],
        [SMEM, SMEM, VMEM] + [VMEM] * len(arrays),
        16 * MIB,
        matmul_cost,
    )(grid_offsets, ids, factor, *arrays)
    (update,) = call(
        finish_kernel,
        [(1, 2, rows, facet_len)],
        [
            pltpu.VMEM((blocks + 1, 2, rows, LANES), jnp.float32),
            pltpu.SemaphoreType.DMA((blocks + 1,)),
        ],
        [SMEM, SMEM, VMEM, VMEM, VMEM, VMEM, HBM],
        8 * MIB,
        matmul_cost // 8,
        out_specs=[HBM],
        input_output_aliases={6: 0},
    )(grid_offsets, ids[-1:], factor, window, *last_item, whole)
    return update


def dft_tables(length):
    index = jnp.arange(length, dtype=jnp.int32)
    angle = (index[:, None] * index[None, :] % length).astype(jnp.float32) * (
        2.0 * math.pi / length
    )
    norm_scale = 1.0 / math.sqrt(length)
    return (jnp.cos(angle) * norm_scale, jnp.sin(angle) * norm_scale)


def transform_last(values, tables, sign):
    cosine, sine = tables
    real_part = values[:, 0]
    imag_part = values[:, 1]

    def multiply(left, right):
        return jnp.einsum("nab,bc->nac", left, right, precision=lax.Precision.HIGHEST)

    out_real = multiply(real_part, cosine) - sign * multiply(imag_part, sine)
    out_imag = multiply(imag_part, cosine) + sign * multiply(real_part, sine)
    return jnp.stack([out_real, out_imag], axis=1)


def plain_device(facets, facet_offsets, grid_offsets, taper, kernels, kernel_index, residual):
    columns = facets[0]
    length = taper.shape[0]
    facet_len = columns.shape[2]
    extended = jnp.concatenate([columns, columns[:, :, :length]], axis=2)
    facet_offset = facet_offsets[lax.axis_index("facet")]
    tables = dft_tables(length)

    def single(grid_offset):
        window = lax.dynamic_slice_in_dim(extended, window_start(grid_offset), length, 2)
        phase_real, phase_imag = phase_pair(facet_offset, grid_offset, length)
        factor_real = phase_real * taper
        factor_imag = phase_imag * taper
        return jnp.stack(
            [
                window[0] * factor_real - window[1] * factor_imag,
                window[0] * factor_imag + window[1] * factor_real,
            ]
        )

    terms = jax.vmap(single)(grid_offsets)
    summed = lax.psum_scatter(terms, "facet", scatter_dimension=0, tiled=True)
    summed = transform_last(summed, tables, -1.0)
    by_rows = lax.all_to_all(summed, "team", split_axis=3, concat_axis=2, tiled=True)
    by_rows = jnp.transpose(by_rows, (0, 1, 3, 2))
    spectrum = transform_last(by_rows, tables, -1.0)
    onehot = (kernel_index[:, :, None] == jnp.arange(kernels.shape[0], dtype=jnp.int32)).astype(
        jnp.float32
    )
    chosen = jnp.einsum("srk,kac->sarc", onehot, kernels, precision=lax.Precision.HIGHEST)
    corr_real = residual[:, 0] - (chosen[:, 0] * spectrum[:, 0] - chosen[:, 1] * spectrum[:, 1])
    corr_imag = residual[:, 1] - (chosen[:, 0] * spectrum[:, 1] + chosen[:, 1] * spectrum[:, 0])
    restored = transform_last(jnp.stack([corr_real, corr_imag], axis=1), tables, 1.0)
    restored = jnp.transpose(restored, (0, 1, 3, 2))
    by_columns = lax.all_to_all(restored, "team", split_axis=2, concat_axis=3, tiled=True)
    by_columns = transform_last(by_columns, tables, 1.0)
    initial = jnp.zeros(extended.shape, jnp.float32)
    piece = lax.all_gather(by_columns, "facet", axis=0, tiled=True)

    def add_one(item, total):
        grid_offset = grid_offsets[item]
        block = lax.dynamic_index_in_dim(piece, item, 0, keepdims=False)
        phase_real, phase_imag = phase_pair(facet_offset, grid_offset, length)
        value = jnp.stack(
            [
                (block[0] * phase_real + block[1] * phase_imag) * taper,
                (block[1] * phase_real - block[0] * phase_imag) * taper,
            ]
        )
        begin = window_start(grid_offset)
        current = lax.dynamic_slice_in_dim(total, begin, length, 2)
        return lax.dynamic_update_slice_in_dim(total, current + value, begin, 2)

    buffer = lax.fori_loop(0, piece.shape[0], add_one, initial)
    update = buffer[:, :, :facet_len].at[:, :, :length].add(buffer[:, :, facet_len:])
    return update[None]


def solution(mesh):
    facet_count, team_count = mesh.shape["facet"], mesh.shape["team"]

    def per_device(*arrays):
        rows, length, facet_len = arrays[0].shape[2], arrays[3].shape[0], arrays[0].shape[3]
        chips = team_count // 2
        tiled = (
            team_count % 2 == 0
            and chips & (chips - 1) == 0
            and 2 * rows == LANES
            and length == chips * LANES
            and facet_len % LANES == 0
            and arrays[6].shape[2] == rows
        )
        if tiled:
            return tiled_device(facet_count, team_count, *arrays)
        return plain_device(*arrays)

    return jax.shard_map(
        per_device,
        mesh=mesh,
        in_specs=(
            P("facet", None, "team", None),
            P(),
            P(),
            P(),
            P(),
            P("facet", "team"),
            P("facet", None, "team", None),
        ),
        out_specs=P("facet", None, "team", None),
        check_vma=False,
    )
```

profile of v0, /device:TPU:0, one launch (start us, length us, event | category | flops | bytes accessed | tf_op | source)
XLA Modules:
  0.0 95.7 jit_solution(2930223606375092755)
XLA Ops:
  0.1 3.6 %shard_map.82 = (f32[8,2,512]{2,1,0:T(2,128)S(1)}, f32[2,64,512]{2,1,0:T(8,128)}, f32[2,64,512]{2,1,0:T(8,128)}) custom-call(s32[3]{0:T(128)S(1)} %pad_add_fusion.ids, s32[8]{0:T(128)} %offsets.5, s32[4]{0:T(128)} %facet_offsets_hbm.1, f32[1,512]{1,0:T(1,128)} %bitcast.44, f32[1,2,64,5120]{3,2,1,0:T(8,128)} %columns.3), custom_call_target="tpu_custom_call" | custom-call | flops 50331648 | bytes 786432 | tf_op jit(solution)/shard_map/pallas_call | solution.py:393
  3.6 3.1 %collective-permute-start.2 = (f32[2,64,512]{2,1,0:T(8,128)}, f32[2,64,512]{2,1,0:T(8,128)S(1)}, u32[]{:S(2)}, u32[]{:S(2)}) collective-permute-start(f32[2,64,512]{2,1,0:T(8,128)} %get-tuple-element.45), channel_id=1, source_target_pairs={{0,16},{8,24},{16,0},{24,8},{1,17},{9,25},{17,1},{25,9},{2,18},{10... | collective-permute-start | bytes 786440 | tf_op jit(solution)/shard_map/ppermute | solution.py:356
  6.7 1.5 %collective-permute-start = (f32[2,64,512]{2,1,0:T(8,128)}, f32[2,64,512]{2,1,0:T(8,128)S(1)}, u32[]{:S(2)}, u32[]{:S(2)}) collective-permute-start(f32[2,64,512]{2,1,0:T(8,128)} %get-tuple-element.43), channel_id=1, source_target_pairs={{0,8},{8,0},{16,24},{24,16},{1,9},{9,1},{17,25},{25,17},{2,10},{10... | collective-permute-start | bytes 786440 | tf_op jit(solution)/shard_map/ppermute | solution.py:356
  8.3 3.2 %shard_map.83 = (f32[2,64,512]{2,1,0:T(8,128)S(1)}, f32[2,64,512]{2,1,0:T(8,128)S(1)}, f32[2,64,512]{2,1,0:T(8,128)S(1)}, f32[2,64,512]{2,1,0:T(8,128)S(1)}, f32...) custom-call(s32[8]{0:T(128)S(1)} %copy-done.1, s32[6]{0:T(128)S(1)} %stack.85.ids, f32[1,2,64,5120]{3,2,1,0:T(8,128)} %columns.3, ...), custom_call_target="tpu_custom_call" | custom-call | flops 100663296 | bytes 1572864 | tf_op jit(solution)/shard_map/pallas_call | solution.py:419
  11.5 1.7 %collective-permute-done.2.refs_0_ = f32[2,64,512]{2,1,0:T(8,128)S(1)} collective-permute-done((f32[2,64,512]{2,1,0:T(8,128)}, f32[2,64,512]{2,1,0:T(8,128)S(1)}, u32[]{:S(2)}, u32[]{:S(2)}) %collective-permute-start.2) | collective-permute-done | bytes 262176 | tf_op jit(solution)/shard_map/ppermute | solution.py:356
  14.0 1.7 %collective-permute-start.17 = (f32[2,64,512]{2,1,0:T(8,128)}, f32[2,64,512]{2,1,0:T(8,128)}, u32[]{:S(2)}, u32[]{:S(2)}) collective-permute-start(f32[2,64,512]{2,1,0:T(8,128)} %shard_map.91), channel_id=1, source_target_pairs={{0,8},{8,0},{16,24},{24,16},{1,9},{9,1},{17,25},{25,17},{2,10},{10... | collective-permute-start | bytes 786440 | tf_op jit(solution)/shard_map/ppermute | solution.py:356
  16.4 1.5 %collective-permute-start.16 = (f32[2,64,512]{2,1,0:T(8,128)}, f32[2,64,512]{2,1,0:T(8,128)}, u32[]{:S(2)}, u32[]{:S(2)}) collective-permute-start(f32[2,64,512]{2,1,0:T(8,128)} %shard_map.90), channel_id=1, source_target_pairs={{0,16},{8,24},{16,0},{24,8},{1,17},{9,25},{17,1},{25,9},{2,18},{10... | collective-permute-start | bytes 786440 | tf_op jit(solution)/shard_map/ppermute | solution.py:356
  19.8 3.6 %collective-permute-done.17.refs_2_ = f32[2,64,512]{2,1,0:T(8,128)} collective-permute-done((f32[2,64,512]{2,1,0:T(8,128)}, f32[2,64,512]{2,1,0:T(8,128)}, u32[]{:S(2)}, u32[]{:S(2)}) %collective-permute-start.17) | collective-permute-done | bytes 262176 | tf_op jit(solution)/shard_map/ppermute | solution.py:356
  23.5 2.5 %collective-permute-done.16.refs_1_ = f32[2,64,512]{2,1,0:T(8,128)} collective-permute-done((f32[2,64,512]{2,1,0:T(8,128)}, f32[2,64,512]{2,1,0:T(8,128)}, u32[]{:S(2)}, u32[]{:S(2)}) %collective-permute-start.16) | collective-permute-done | bytes 262176 | tf_op jit(solution)/shard_map/ppermute | solution.py:356
  25.9 1.7 %shard_map.92 = (f32[2,64,128]{2,1,0:T(8,128)S(1)}, f32[2,64,128]{2,1,0:T(8,128)S(1)}, f32[2,64,128]{2,1,0:T(8,128)S(1)}, f32[2,64,128]{2,1,0:T(8,128)S(1)}) custom-call(s32[2]{0:T(128)S(1)} %pad_add_fusion.1.place, bf16[2,512,1024]{2,1,0:T(8,128)(2,1)S(1)} %copy-done, f32[2,64,512]{2,1,0:T(8,128)S(1)} %get-tuple-element.58.refs_0_, ...), custom_call_target="tpu_custom_call" | custom-call | flops 402653184 | bytes 6291456 | tf_op jit(solution)/shard_map/pallas_call | solution.py:455
  27.6 1.6 %collective-permute-start.18 = (f32[2,64,128]{2,1,0:T(8,128)S(1)}, f32[2,64,128]{2,1,0:T(8,128)S(1)}, u32[]{:S(2)}, u32[]{:S(2)}) collective-permute-start(f32[2,64,128]{2,1,0:T(8,128)S(1)} %get-tuple-element.62), channel_id=1, source_target_pairs={{0,2},{1,3},{2,0},{3,1},{4,6},{5,7},{6,4},{7,5},{8,10},{9,11},{10,... | collective-permute-start | bytes 196616 | tf_op jit(solution)/shard_map/ppermute | solution.py:364
  29.3 2.6 %collective-permute-start.19 = (f32[2,64,128]{2,1,0:T(8,128)S(1)}, f32[2,64,128]{2,1,0:T(8,128)S(1)}, u32[]{:S(2)}, u32[]{:S(2)}) collective-permute-start(f32[2,64,128]{2,1,0:T(8,128)S(1)} %get-tuple-element.63), channel_id=1, source_target_pairs={{0,4},{1,5},{2,6},{3,7},{4,0},{5,1},{6,2},{7,3},{8,12},{9,13},{10,... | collective-permute-start | bytes 196616 | tf_op jit(solution)/shard_map/ppermute | solution.py:364
  34.0 3.5 %collective-permute-start.5 = (f32[2,64,128]{2,1,0:T(8,128)S(1)}, f32[2,64,128]{2,1,0:T(8,128)S(1)}, u32[]{:S(2)}, u32[]{:S(2)}) collective-permute-start(f32[2,64,128]{2,1,0:T(8,128)S(1)} %get-tuple-element.48), channel_id=1, source_target_pairs={{0,4},{1,5},{2,6},{3,7},{4,0},{5,1},{6,2},{7,3},{8,12},{9,13},{10,... | collective-permute-start | bytes 196616 | tf_op jit(solution)/shard_map/ppermute | solution.py:364
  38.2 1.2 %shard_map.93 = (f32[2,64,512]{2,1,0:T(8,128)S(1)}, f32[2,64,512]{2,1,0:T(8,128)S(1)}) custom-call(s32[2]{0:T(128)S(1)} %pad_add_fusion.1.place, bf16[2,512,1024]{2,1,0:T(8,128)(2,1)S(1)} %copy-done, f32[2,64,128]{2,1,0:T(8,128)S(1)} %get-tuple-element.61.refs_0_, f32[2,64,128]{2,1,0:T(8,128)S(1)} %collective-permute-done.18.refs_1_, ...), custom_call_target="tpu_custom_call" | custom-call | flops 402653184 | bytes 6291456 | tf_op jit(solution)/shard_map/pallas_call | solution.py:465
  40.4 3.1 %collective-permute-done.6.refs_3_ = f32[2,64,128]{2,1,0:T(8,128)S(1)} collective-permute-done((f32[2,64,128]{2,1,0:T(8,128)S(1)}, f32[2,64,128]{2,1,0:T(8,128)S(1)}, u32[]{:S(2)}, u32[]{:S(2)}) %collective-permute-start.6) | collective-permute-done | bytes 65568 | tf_op jit(solution)/shard_map/ppermute | solution.py:364
  43.5 1.2 %shard_map.87 = (f32[2,64,512]{2,1,0:T(8,128)S(1)}, f32[2,64,512]{2,1,0:T(8,128)S(1)}) custom-call(s32[2]{0:T(128)S(1)} %pad_add_fusion.1.place, bf16[2,512,1024]{2,1,0:T(8,128)(2,1)S(1)} %copy-done, f32[2,64,128]{2,1,0:T(8,128)S(1)} %get-tuple-element.46.refs_0_, f32[2,64,128]{2,1,0:T(8,128)S(1)} %collective-permute-done.4.refs_1_, ...), custom_call_target="tpu_custom_call" | custom-call | flops 402653184 | bytes 6291456 | tf_op jit(solution)/shard_map/pallas_call | solution.py:465
  46.2 1.3 %collective-permute-start.23 = (f32[2,64,128]{2,1,0:T(8,128)S(1)}, f32[2,64,128]{2,1,0:T(8,128)S(1)}, u32[]{:S(2)}, u32[]{:S(2)}) collective-permute-start(f32[2,64,128]{2,1,0:T(8,128)S(1)} %get-tuple-element.69), channel_id=1, source_target_pairs={{0,4},{1,5},{2,6},{3,7},{4,0},{5,1},{6,2},{7,3},{8,12},{9,13},{10,... | collective-permute-start | bytes 196616 | tf_op jit(solution)/shard_map/ppermute | solution.py:364
  47.5 3.1 %collective-permute-start.24 = (f32[2,64,128]{2,1,0:T(8,128)S(1)}, f32[2,64,128]{2,1,0:T(8,128)S(1)}, u32[]{:S(2)}, u32[]{:S(2)}) collective-permute-start(f32[2,64,128]{2,1,0:T(8,128)S(1)} %get-tuple-element.70), channel_id=1, source_target_pairs={{0,6},{1,7},{2,4},{3,5},{4,2},{5,3},{6,0},{7,1},{8,14},{9,15},{10,... | collective-permute-start | bytes 196616 | tf_op jit(solution)/shard_map/ppermute | solution.py:364
  51.8 3.2 %collective-permute-done.23.refs_2_ = f32[2,64,128]{2,1,0:T(8,128)S(1)} collective-permute-done((f32[2,64,128]{2,1,0:T(8,128)S(1)}, f32[2,64,128]{2,1,0:T(8,128)S(1)}, u32[]{:S(2)}, u32[]{:S(2)}) %collective-permute-start.23) | collective-permute-done | bytes 65568 | tf_op jit(solution)/shard_map/ppermute | solution.py:364
  57.5 1.5 %collective-permute-start.8 = (f32[2,64,128]{2,1,0:T(8,128)S(1)}, f32[2,64,128]{2,1,0:T(8,128)S(1)}, u32[]{:S(2)}, u32[]{:S(2)}) collective-permute-start(f32[2,64,128]{2,1,0:T(8,128)S(1)} %get-tuple-element.53), channel_id=1, source_target_pairs={{0,2},{1,3},{2,0},{3,1},{4,6},{5,7},{6,4},{7,5},{8,10},{9,11},{10,... | collective-permute-start | bytes 196616 | tf_op jit(solution)/shard_map/ppermute | solution.py:364
  59.8 2.1 %collective-permute-start.10 = (f32[2,64,128]{2,1,0:T(8,128)S(1)}, f32[2,64,128]{2,1,0:T(8,128)S(1)}, u32[]{:S(2)}, u32[]{:S(2)}) collective-permute-start(f32[2,64,128]{2,1,0:T(8,128)S(1)} %get-tuple-element.55), channel_id=1, source_target_pairs={{0,6},{1,7},{2,4},{3,5},{4,2},{5,3},{6,0},{7,1},{8,14},{9,15},{10,... | collective-permute-start | bytes 196616 | tf_op jit(solution)/shard_map/ppermute | solution.py:364
  62.0 5.1 %collective-permute-done.9.refs_2_ = f32[2,64,128]{2,1,0:T(8,128)S(1)} collective-permute-done((f32[2,64,128]{2,1,0:T(8,128)S(1)}, f32[2,64,128]{2,1,0:T(8,128)S(1)}, u32[]{:S(2)}, u32[]{:S(2)}) %collective-permute-start.9) | collective-permute-done | bytes 65568 | tf_op jit(solution)/shard_map/ppermute | solution.py:364
  68.6 1.6 %collective-permute-start.27 = (f32[2,64,512]{2,1,0:T(8,128)S(1)}, f32[2,64,512]{2,1,0:T(8,128)S(1)}, u32[]{:S(2)}, u32[]{:S(2)}) collective-permute-start(f32[2,64,512]{2,1,0:T(8,128)S(1)} %add.162.refs_5_), channel_id=1, source_target_pairs={{0,16},{8,24},{16,0},{24,8},{1,17},{9,25},{17,1},{25,9},{2,18},{10... | collective-permute-start | bytes 786440 | tf_op jit(solution)/shard_map/ppermute | solution.py:356
  70.2 1.5 %collective-permute-start.13 = (f32[2,64,512]{2,1,0:T(8,128)S(1)}, f32[2,64,512]{2,1,0:T(8,128)S(1)}, u32[]{:S(2)}, u32[]{:S(2)}) collective-permute-start(f32[2,64,512]{2,1,0:T(8,128)S(1)} %add.161.refs_0_), channel_id=1, source_target_pairs={{0,16},{8,24},{16,0},{24,8},{1,17},{9,25},{17,1},{25,9},{2,18},{10... | collective-permute-start | bytes 786440 | tf_op jit(solution)/shard_map/ppermute | solution.py:356
  72.2 1.5 %collective-permute-start.12 = (f32[2,64,512]{2,1,0:T(8,128)S(1)}, f32[2,64,512]{2,1,0:T(8,128)S(1)}, u32[]{:S(2)}, u32[]{:S(2)}) collective-permute-start(f32[2,64,512]{2,1,0:T(8,128)S(1)} %add.161.refs_0_), channel_id=1, source_target_pairs={{0,8},{8,0},{16,24},{24,16},{1,9},{9,1},{17,25},{25,17},{2,10},{10... | collective-permute-start | bytes 786440 | tf_op jit(solution)/shard_map/ppermute | solution.py:356
  73.7 4.1 %collective-permute-done.27.refs_7_ = f32[2,64,512]{2,1,0:T(8,128)S(1)} collective-permute-done((f32[2,64,512]{2,1,0:T(8,128)S(1)}, f32[2,64,512]{2,1,0:T(8,128)S(1)}, u32[]{:S(2)}, u32[]{:S(2)}) %collective-permute-start.27) | collective-permute-done | bytes 262176 | tf_op jit(solution)/shard_map/ppermute | solution.py:356
  78.4 4.5 %collective-permute-done.13.refs_2_ = f32[2,64,512]{2,1,0:T(8,128)S(1)} collective-permute-done((f32[2,64,512]{2,1,0:T(8,128)S(1)}, f32[2,64,512]{2,1,0:T(8,128)S(1)}, u32[]{:S(2)}, u32[]{:S(2)}) %collective-permute-start.13) | collective-permute-done | bytes 262176 | tf_op jit(solution)/shard_map/ppermute | solution.py:356
  83.5 2.9 %collective-permute-done.12.refs_1_ = f32[2,64,512]{2,1,0:T(8,128)S(1)} collective-permute-done((f32[2,64,512]{2,1,0:T(8,128)S(1)}, f32[2,64,512]{2,1,0:T(8,128)S(1)}, u32[]{:S(2)}, u32[]{:S(2)}) %collective-permute-start.12) | collective-permute-done | bytes 262176 | tf_op jit(solution)/shard_map/ppermute | solution.py:356
  87.2 1.5 %collective-permute-start.28 = (f32[64,512]{1,0:T(8,128)S(1)}, f32[64,512]{1,0:T(8,128)S(1)}, u32[]{:S(2)}, u32[]{:S(2)}) collective-permute-start(f32[64,512]{1,0:T(8,128)S(1)} %slice_bitcast_fusion.5), channel_id=1, source_target_pairs={{0,16},{8,24},{16,0},{24,8},{1,17},{9,25},{17,1},{25,9},{2,18},{10... | collective-permute-start | bytes 393224 | tf_op jit(solution)/shard_map/ppermute | solution.py:356
  88.7 2.2 %collective-permute-done.15.refs_4_ = f32[64,512]{1,0:T(8,128)S(1)} collective-permute-done((f32[64,512]{1,0:T(8,128)S(1)}, f32[64,512]{1,0:T(8,128)S(1)}, u32[]{:S(2)}, u32[]{:S(2)}) %collective-permute-start.15) | collective-permute-done | bytes 131104 | tf_op jit(solution)/shard_map/ppermute | solution.py:356
  91.5 2.8 %shard_map.96 = (f32[1,2,64,5120]{3,2,1,0:T(8,128)}, f32[2,64,640]{2,1,0:T(8,128)S(1)}) custom-call(s32[8]{0:T(128)S(1)} %copy-done.1, s32[8]{0:T(128)S(1)} %stack.77.ids, f32[8,2,512]{2,1,0:T(2,128)S(1)} %get-tuple-element.40.factor, f32[2,64,512]{2,1,0:T(8,128)S(1)} %add.161.refs_0_, f32[2,64,512]{2,1,0:T(8,128)S(1)} %collective-permute-done.12.refs_1_, ...), custom_call_target="tpu_custom_call" | custom-call | flops 402653184 | bytes 6291456 | tf_op jit(solution)/shard_map/pallas_call | solution.py:515
  94.3 1.4 %shard_map.97 = f32[1,2,64,5120]{3,2,1,0:T(8,128)} custom-call(s32[8]{0:T(128)S(1)} %copy-done.1, s32[1]{0:T(128)} %bitcast.ids, f32[8,2,512]{2,1,0:T(2,128)S(1)} %get-tuple-element.40.factor, f32[2,64,640]{2,1,0:T(8,128)S(1)} %get-tuple-element.73.window, f32[64,512]{1,0:T(8,128)S(1)} %collective-permute-done.28.real, ...), custom_call_target="tpu_custom_call", output_to_operand_aliasing={{}: (6, {})} | custom-call | flops 50331648 | bytes 786432 | tf_op jit(solution)/shard_map/pallas_call | solution.py:523
  (66 shorter events, 17.7 us)
Async XLA Ops:
  3.6 9.6 %collective-permute-start.2 = (f32[2,64,512]{2,1,0:T(8,128)}, f32[2,64,512]{2,1,0:T(8,128)S(1)}, u32[]{:S(2)}, u32[]{:S(2)}) collective-permute-start(f32[2,64,512]{2,1,0:T(8,128)} %get-tuple-element.45), channel_id=1, source_target_pairs={{0,16},{8,24},{16,0},{24,8},{1,17},{9,25},{17,1},{25,9},{2,18},{10... | collective-permute-start | bytes 786440 | tf_op jit(solution)/shard_map/ppermute | solution.py:356
  6.7 9.0 %collective-permute-start = (f32[2,64,512]{2,1,0:T(8,128)}, f32[2,64,512]{2,1,0:T(8,128)S(1)}, u32[]{:S(2)}, u32[]{:S(2)}) collective-permute-start(f32[2,64,512]{2,1,0:T(8,128)} %get-tuple-element.43), channel_id=1, source_target_pairs={{0,8},{8,0},{16,24},{24,16},{1,9},{9,1},{17,25},{25,17},{2,10},{10... | collective-permute-start | bytes 786440 | tf_op jit(solution)/shard_map/ppermute | solution.py:356
  8.3 17.6 %copy-start = (bf16[2,512,1024]{2,1,0:T(8,128)(2,1)S(1)}, bf16[2,512,1024]{2,1,0:T(8,128)(2,1)}, u32[]{:S(2)}) copy-start(bf16[2,512,1024]{2,1,0:T(8,128)(2,1)} %constant.123.clone.table) | copy-start | bytes 6291460
  14.0 9.5 %collective-permute-start.17 = (f32[2,64,512]{2,1,0:T(8,128)}, f32[2,64,512]{2,1,0:T(8,128)}, u32[]{:S(2)}, u32[]{:S(2)}) collective-permute-start(f32[2,64,512]{2,1,0:T(8,128)} %shard_map.91), channel_id=1, source_target_pairs={{0,8},{8,0},{16,24},{24,16},{1,9},{9,1},{17,25},{25,17},{2,10},{10... | collective-permute-start | bytes 786440 | tf_op jit(solution)/shard_map/ppermute | solution.py:356
  16.4 9.5 %collective-permute-start.16 = (f32[2,64,512]{2,1,0:T(8,128)}, f32[2,64,512]{2,1,0:T(8,128)}, u32[]{:S(2)}, u32[]{:S(2)}) collective-permute-start(f32[2,64,512]{2,1,0:T(8,128)} %shard_map.90), channel_id=1, source_target_pairs={{0,16},{8,24},{16,0},{24,8},{1,17},{9,25},{17,1},{25,9},{2,18},{10... | collective-permute-start | bytes 786440 | tf_op jit(solution)/shard_map/ppermute | solution.py:356
  18.0 14.1 %collective-permute-start.3 = (f32[2,64,512]{2,1,0:T(8,128)S(1)}, f32[2,64,512]{2,1,0:T(8,128)S(1)}, u32[]{:S(2)}, u32[]{:S(2)}) collective-permute-start(f32[2,64,512]{2,1,0:T(8,128)S(1)} %shard_map.85), channel_id=1, source_target_pairs={{0,8},{8,0},{16,24},{24,16},{1,9},{9,1},{17,25},{25,17},{2,10},{10... | collective-permute-start | bytes 786440 | tf_op jit(solution)/shard_map/ppermute | solution.py:356
  19.3 12.8 %collective-permute-start.1 = (f32[2,64,512]{2,1,0:T(8,128)}, f32[2,64,512]{2,1,0:T(8,128)S(1)}, u32[]{:S(2)}, u32[]{:S(2)}) collective-permute-start(f32[2,64,512]{2,1,0:T(8,128)} %shard_map.84), channel_id=1, source_target_pairs={{0,16},{8,24},{16,0},{24,8},{1,17},{9,25},{17,1},{25,9},{2,18},{10... | collective-permute-start | bytes 786440 | tf_op jit(solution)/shard_map/ppermute | solution.py:356
  25.9 11.8 %copy-start.4 = (s32[2,64]{1,0:T(2,128)S(1)}, s32[2,64]{1,0:T(2,128)}, u32[]{:S(2)}) copy-start(s32[2,64]{1,0:T(2,128)} %param.13) | copy-start | bytes 1540
  27.6 9.9 %collective-permute-start.18 = (f32[2,64,128]{2,1,0:T(8,128)S(1)}, f32[2,64,128]{2,1,0:T(8,128)S(1)}, u32[]{:S(2)}, u32[]{:S(2)}) collective-permute-start(f32[2,64,128]{2,1,0:T(8,128)S(1)} %get-tuple-element.62), channel_id=1, source_target_pairs={{0,2},{1,3},{2,0},{3,1},{4,6},{5,7},{6,4},{7,5},{8,10},{9,11},{10,... | collective-permute-start | bytes 196616 | tf_op jit(solution)/shard_map/ppermute | solution.py:364
  29.3 8.9 %collective-permute-start.19 = (f32[2,64,128]{2,1,0:T(8,128)S(1)}, f32[2,64,128]{2,1,0:T(8,128)S(1)}, u32[]{:S(2)}, u32[]{:S(2)}) collective-permute-start(f32[2,64,128]{2,1,0:T(8,128)S(1)} %get-tuple-element.63), channel_id=1, source_target_pairs={{0,4},{1,5},{2,6},{3,7},{4,0},{5,1},{6,2},{7,3},{8,12},{9,13},{10,... | collective-permute-start | bytes 196616 | tf_op jit(solution)/shard_map/ppermute | solution.py:364
  31.9 6.3 %collective-permute-start.20 = (f32[2,64,128]{2,1,0:T(8,128)S(1)}, f32[2,64,128]{2,1,0:T(8,128)S(1)}, u32[]{:S(2)}, u32[]{:S(2)}) collective-permute-start(f32[2,64,128]{2,1,0:T(8,128)S(1)} %get-tuple-element.64), channel_id=1, source_target_pairs={{0,6},{1,7},{2,4},{3,5},{4,2},{5,3},{6,0},{7,1},{8,14},{9,15},{10,... | collective-permute-start | bytes 196616 | tf_op jit(solution)/shard_map/ppermute | solution.py:364
  33.2 6.2 %collective-permute-start.4 = (f32[2,64,128]{2,1,0:T(8,128)S(1)}, f32[2,64,128]{2,1,0:T(8,128)S(1)}, u32[]{:S(2)}, u32[]{:S(2)}) collective-permute-start(f32[2,64,128]{2,1,0:T(8,128)S(1)} %get-tuple-element.47), channel_id=1, source_target_pairs={{0,2},{1,3},{2,0},{3,1},{4,6},{5,7},{6,4},{7,5},{8,10},{9,11},{10,... | collective-permute-start | bytes 196616 | tf_op jit(solution)/shard_map/ppermute | solution.py:364
  34.0 6.4 %collective-permute-start.5 = (f32[2,64,128]{2,1,0:T(8,128)S(1)}, f32[2,64,128]{2,1,0:T(8,128)S(1)}, u32[]{:S(2)}, u32[]{:S(2)}) collective-permute-start(f32[2,64,128]{2,1,0:T(8,128)S(1)} %get-tuple-element.48), channel_id=1, source_target_pairs={{0,4},{1,5},{2,6},{3,7},{4,0},{5,1},{6,2},{7,3},{8,12},{9,13},{10,... | collective-permute-start | bytes 196616 | tf_op jit(solution)/shard_map/ppermute | solution.py:364
  37.5 6.1 %collective-permute-start.6 = (f32[2,64,128]{2,1,0:T(8,128)S(1)}, f32[2,64,128]{2,1,0:T(8,128)S(1)}, u32[]{:S(2)}, u32[]{:S(2)}) collective-permute-start(f32[2,64,128]{2,1,0:T(8,128)S(1)} %get-tuple-element.49), channel_id=1, source_target_pairs={{0,6},{1,7},{2,4},{3,5},{4,2},{5,3},{6,0},{7,1},{8,14},{9,15},{10,... | collective-permute-start | bytes 196616 | tf_op jit(solution)/shard_map/ppermute | solution.py:364
  39.4 5.6 %collective-permute-start.21 = (f32[2,64,512]{2,1,0:T(8,128)S(1)}, f32[2,64,512]{2,1,0:T(8,128)S(1)}, u32[]{:S(2)}, u32[]{:S(2)}) collective-permute-start(f32[2,64,512]{2,1,0:T(8,128)S(1)} %get-tuple-element.66), channel_id=1, source_target_pairs={{0,1},{1,0},{2,3},{3,2},{4,5},{5,4},{6,7},{7,6},{8,9},{9,8},{10,11... | collective-permute-start | bytes 786440 | tf_op jit(solution)/shard_map/ppermute | solution.py:368
  44.8 11.5 %collective-permute-start.7 = (f32[2,64,512]{2,1,0:T(8,128)S(1)}, f32[2,64,512]{2,1,0:T(8,128)S(1)}, u32[]{:S(2)}, u32[]{:S(2)}) collective-permute-start(f32[2,64,512]{2,1,0:T(8,128)S(1)} %get-tuple-element.51), channel_id=1, source_target_pairs={{0,1},{1,0},{2,3},{3,2},{4,5},{5,4},{6,7},{7,6},{8,9},{9,8},{10,11... | collective-permute-start | bytes 786440 | tf_op jit(solution)/shard_map/ppermute | solution.py:368
  46.2 5.6 %collective-permute-start.22 = (f32[2,64,128]{2,1,0:T(8,128)S(1)}, f32[2,64,128]{2,1,0:T(8,128)S(1)}, u32[]{:S(2)}, u32[]{:S(2)}) collective-permute-start(f32[2,64,128]{2,1,0:T(8,128)S(1)} %get-tuple-element.68), channel_id=1, source_target_pairs={{0,2},{1,3},{2,0},{3,1},{4,6},{5,7},{6,4},{7,5},{8,10},{9,11},{10,... | collective-permute-start | bytes 196616 | tf_op jit(solution)/shard_map/ppermute | solution.py:364
  46.2 8.7 %collective-permute-start.23 = (f32[2,64,128]{2,1,0:T(8,128)S(1)}, f32[2,64,128]{2,1,0:T(8,128)S(1)}, u32[]{:S(2)}, u32[]{:S(2)}) collective-permute-start(f32[2,64,128]{2,1,0:T(8,128)S(1)} %get-tuple-element.69), channel_id=1, source_target_pairs={{0,4},{1,5},{2,6},{3,7},{4,0},{5,1},{6,2},{7,3},{8,12},{9,13},{10,... | collective-permute-start | bytes 196616 | tf_op jit(solution)/shard_map/ppermute | solution.py:364
  47.5 7.5 %collective-permute-start.24 = (f32[2,64,128]{2,1,0:T(8,128)S(1)}, f32[2,64,128]{2,1,0:T(8,128)S(1)}, u32[]{:S(2)}, u32[]{:S(2)}) collective-permute-start(f32[2,64,128]{2,1,0:T(8,128)S(1)} %get-tuple-element.70), channel_id=1, source_target_pairs={{0,6},{1,7},{2,4},{3,5},{4,2},{5,3},{6,0},{7,1},{8,14},{9,15},{10,... | collective-permute-start | bytes 196616 | tf_op jit(solution)/shard_map/ppermute | solution.py:364
  56.2 12.3 %collective-permute-start.25 = (f32[2,64,512]{2,1,0:T(8,128)S(1)}, f32[2,64,512]{2,1,0:T(8,128)S(1)}, u32[]{:S(2)}, u32[]{:S(2)}) collective-permute-start(f32[2,64,512]{2,1,0:T(8,128)S(1)} %get-tuple-element.72), channel_id=1, source_target_pairs={{0,1},{1,0},{2,3},{3,2},{4,5},{5,4},{6,7},{7,6},{8,9},{9,8},{10,11... | collective-permute-start | bytes 786440 | tf_op jit(solution)/shard_map/ppermute | solution.py:368
  57.5 4.5 %collective-permute-start.8 = (f32[2,64,128]{2,1,0:T(8,128)S(1)}, f32[2,64,128]{2,1,0:T(8,128)S(1)}, u32[]{:S(2)}, u32[]{:S(2)}) collective-permute-start(f32[2,64,128]{2,1,0:T(8,128)S(1)} %get-tuple-element.53), channel_id=1, source_target_pairs={{0,2},{1,3},{2,0},{3,1},{4,6},{5,7},{6,4},{7,5},{8,10},{9,11},{10,... | collective-permute-start | bytes 196616 | tf_op jit(solution)/shard_map/ppermute | solution.py:364
  59.0 8.1 %collective-permute-start.9 = (f32[2,64,128]{2,1,0:T(8,128)S(1)}, f32[2,64,128]{2,1,0:T(8,128)S(1)}, u32[]{:S(2)}, u32[]{:S(2)}) collective-permute-start(f32[2,64,128]{2,1,0:T(8,128)S(1)} %get-tuple-element.54), channel_id=1, source_target_pairs={{0,4},{1,5},{2,6},{3,7},{4,0},{5,1},{6,2},{7,3},{8,12},{9,13},{10,... | collective-permute-start | bytes 196616 | tf_op jit(solution)/shard_map/ppermute | solution.py:364
  59.8 7.4 %collective-permute-start.10 = (f32[2,64,128]{2,1,0:T(8,128)S(1)}, f32[2,64,128]{2,1,0:T(8,128)S(1)}, u32[]{:S(2)}, u32[]{:S(2)}) collective-permute-start(f32[2,64,128]{2,1,0:T(8,128)S(1)} %get-tuple-element.55), channel_id=1, source_target_pairs={{0,6},{1,7},{2,4},{3,5},{4,2},{5,3},{6,0},{7,1},{8,14},{9,15},{10,... | collective-permute-start | bytes 196616 | tf_op jit(solution)/shard_map/ppermute | solution.py:364
  68.4 1.7 %collective-permute-start.11 = (f32[2,64,512]{2,1,0:T(8,128)S(1)}, f32[2,64,512]{2,1,0:T(8,128)S(1)}, u32[]{:S(2)}, u32[]{:S(2)}) collective-permute-start(f32[2,64,512]{2,1,0:T(8,128)S(1)} %get-tuple-element.57), channel_id=1, source_target_pairs={{0,1},{1,0},{2,3},{3,2},{4,5},{5,4},{6,7},{7,6},{8,9},{9,8},{10,11... | collective-permute-start | bytes 786440 | tf_op jit(solution)/shard_map/ppermute | solution.py:368
  68.6 9.2 %collective-permute-start.27 = (f32[2,64,512]{2,1,0:T(8,128)S(1)}, f32[2,64,512]{2,1,0:T(8,128)S(1)}, u32[]{:S(2)}, u32[]{:S(2)}) collective-permute-start(f32[2,64,512]{2,1,0:T(8,128)S(1)} %add.162.refs_5_), channel_id=1, source_target_pairs={{0,16},{8,24},{16,0},{24,8},{1,17},{9,25},{17,1},{25,9},{2,18},{10... | collective-permute-start | bytes 786440 | tf_op jit(solution)/shard_map/ppermute | solution.py:356
  70.2 12.8 %collective-permute-start.13 = (f32[2,64,512]{2,1,0:T(8,128)S(1)}, f32[2,64,512]{2,1,0:T(8,128)S(1)}, u32[]{:S(2)}, u32[]{:S(2)}) collective-permute-start(f32[2,64,512]{2,1,0:T(8,128)S(1)} %add.161.refs_0_), channel_id=1, source_target_pairs={{0,16},{8,24},{16,0},{24,8},{1,17},{9,25},{17,1},{25,9},{2,18},{10... | collective-permute-start | bytes 786440 | tf_op jit(solution)/shard_map/ppermute | solution.py:356
  71.6 15.5 %collective-permute-start.26 = (f32[2,64,512]{2,1,0:T(8,128)S(1)}, f32[2,64,512]{2,1,0:T(8,128)S(1)}, u32[]{:S(2)}, u32[]{:S(2)}) collective-permute-start(f32[2,64,512]{2,1,0:T(8,128)S(1)} %add.162.refs_5_), channel_id=1, source_target_pairs={{0,8},{8,0},{16,24},{24,16},{1,9},{9,1},{17,25},{25,17},{2,10},{10... | collective-permute-start | bytes 786440 | tf_op jit(solution)/shard_map/ppermute | solution.py:356
  72.2 14.3 %collective-permute-start.12 = (f32[2,64,512]{2,1,0:T(8,128)S(1)}, f32[2,64,512]{2,1,0:T(8,128)S(1)}, u32[]{:S(2)}, u32[]{:S(2)}) collective-permute-start(f32[2,64,512]{2,1,0:T(8,128)S(1)} %add.161.refs_0_), channel_id=1, source_target_pairs={{0,8},{8,0},{16,24},{24,16},{1,9},{9,1},{17,25},{25,17},{2,10},{10... | collective-permute-start | bytes 786440 | tf_op jit(solution)/shard_map/ppermute | solution.py:356
  77.8 16.5 %collective-permute-start.29 = (f32[64,512]{1,0:T(8,128)S(1)}, f32[64,512]{1,0:T(8,128)S(1)}, u32[]{:S(2)}, u32[]{:S(2)}) collective-permute-start(f32[64,512]{1,0:T(8,128)S(1)} %slice_bitcast_fusion.4), channel_id=1, source_target_pairs={{0,8},{8,0},{16,24},{24,16},{1,9},{9,1},{17,25},{25,17},{2,10},{10... | collective-permute-start | bytes 393224 | tf_op jit(solution)/shard_map/ppermute | solution.py:356
  82.9 8.0 %collective-permute-start.15 = (f32[64,512]{1,0:T(8,128)S(1)}, f32[64,512]{1,0:T(8,128)S(1)}, u32[]{:S(2)}, u32[]{:S(2)}) collective-permute-start(f32[64,512]{1,0:T(8,128)S(1)} %slice_bitcast_fusion.6), channel_id=1, source_target_pairs={{0,8},{8,0},{16,24},{24,16},{1,9},{9,1},{17,25},{25,17},{2,10},{10... | collective-permute-start | bytes 393224 | tf_op jit(solution)/shard_map/ppermute | solution.py:356
  86.5 5.0 %collective-permute-start.14 = (f32[64,512]{1,0:T(8,128)S(1)}, f32[64,512]{1,0:T(8,128)S(1)}, u32[]{:S(2)}, u32[]{:S(2)}) collective-permute-start(f32[64,512]{1,0:T(8,128)S(1)} %slice_bitcast_fusion.7), channel_id=1, source_target_pairs={{0,16},{8,24},{16,0},{24,8},{1,17},{9,25},{17,1},{25,9},{2,18},{10... | collective-permute-start | bytes 393224 | tf_op jit(solution)/shard_map/ppermute | solution.py:356
  87.2 7.2 %collective-permute-start.28 = (f32[64,512]{1,0:T(8,128)S(1)}, f32[64,512]{1,0:T(8,128)S(1)}, u32[]{:S(2)}, u32[]{:S(2)}) collective-permute-start(f32[64,512]{1,0:T(8,128)S(1)} %slice_bitcast_fusion.5), channel_id=1, source_target_pairs={{0,16},{8,24},{16,0},{24,8},{1,17},{9,25},{17,1},{25,9},{2,18},{10... | collective-permute-start | bytes 393224 | tf_op jit(solution)/shard_map/ppermute | solution.py:356
  (3 other events, 27.4 us)
where the time goes:
time: 95.9 us; the launch traced here: 95.7 us
  waiting for transfers between devices  35.8 us (37%)
  starting transfers between devices  35.3 us (37%)
  Pallas kernels  23.3 us (24%)
    ppermute x14, waiting for transfers between devices, move(): return lax.ppermute(value, 'facet', pairs)  22.1 us
    ppermute x12, starting transfers between devices, exchange(): out.append(lax.ppermute(pieces[distance], 'team', pairs))  17.8 us
    ppermute x14, starting transfers between devices, move(): return lax.ppermute(value, 'facet', pairs)  17.2 us
    ppermute x12, waiting for transfers between devices, exchange(): out.append(lax.ppermute(pieces[distance], 'team', pairs))  13.7 us
    pallas_call x4, Pallas kernels, cross(): call(functools.partial(cross_kernel, sign), [block_shape] * 2, [pltpu.VME...  4.89 us
    pallas_call x1, Pallas kernels, tiled_device(): call(functools.partial(corner_window_kernel, per_facet), [(subgrids, 2, l...  3.56 us
    pallas_call x1, Pallas kernels, tiled_device(): call(window_kernel, [block_shape] * len(near_keys), window_scratch(len(ne...  3.21 us
    pallas_call x2, Pallas kernels, first_transform(): call(first_kernel, [piece_shape] * chips, [pltpu.VMEM(block_shape, jnp.fl...  2.85 us
  transfers between devices with their start and end apart: 30, of which 14 were waited for; matrix products, arithmetic and copies ran while one was open for 1% of the time, Pallas kernels for 19%

commit v1 on v0

--- a/solution.py
+++ b/solution.py
@@ -13,6 +13,7 @@
 N_IMG = 65536
 FACET_LEN = 5120
 LANES = 128
+CHIP, CORE, FACET = range(3)
 
 
 def mod_product(left, right):
@@ -84,6 +85,18 @@
     for item in range(count):
         factor[item, 0:1, :] = real[item : item + 1, :]
         factor[item, 1:2, :] = imag[item : item + 1, :]
+
+
+def pairs_of(layout, refs):
+    refs = list(refs)
+    pairs = []
+    for planes in layout:
+        if planes == 1:
+            whole = refs.pop(0)
+            pairs.append((whole.at[0], whole.at[1]))
+        else:
+            pairs.append((refs.pop(0), refs.pop(0)))
+    return pairs
 
 
 def cut_windows(offsets, ids, columns, outs, buffer, sems, prepare, factor):
@@ -126,7 +139,7 @@
 
 
 def corner_window_kernel(
-    per_facet, ids, offsets_hbm, facet_offsets_hbm, taper_hbm, columns, *refs
+    per_facet, spots, info, offsets_hbm, facet_offsets_hbm, taper_hbm, columns, *refs
 ):
     factor, planes = refs[0], refs[1:-6]
     buffer, sems, offsets, facet_offsets, taper, small_sems = refs[-6:]
@@ -147,24 +160,45 @@
     def prepare():
         small[1].wait()
         small[2].wait()
-        phase_factor(offsets, facet_offsets[ids[len(outs)]], taper[...], factor)
-
+        phase_factor(offsets, facet_offsets[info[FACET]], taper[...], factor)
+
+    ids = [info[spot] for spot in spots]
     cut_windows(offsets, ids, columns, outs, buffer, sems, prepare, factor)
 
 
-def window_kernel(offsets, ids, columns, factor, *refs):
+def window_kernel(layout, spots, info, offsets, columns, factor, *refs):
     planes, (buffer, sems) = refs[:-2], refs[-2:]
-    outs = [(plane.at[0], plane.at[1]) for plane in planes]
+    outs = pairs_of(layout, planes)
+    ids = [info[spot] for spot in spots]
     cut_windows(offsets, ids, columns, outs, buffer, sems, lambda: None, factor)
 
 
-def join_kernel(part, chunk, term, *refs):
+def join_kernel(part, chunk, whole, term, *refs):
     received, out = refs[:-1], refs[-1]
-    total = term[part]
+    if not whole:
+        total = term[...]
+    else:
+        total = term[part]
+        out[1 - part] = term[1 - part]
     for corner in received:
         total = total + corner[chunk]
-    out[part] = total
-    out[1 - part] = term[1 - part]
+    if whole:
+        out[part] = total
+    else:
+        out[...] = total
+
+
+def choose_kernel(index, kernels, out):
+    chunks, _, rows, _ = out.shape
+    for chunk in range(chunks):
+
+        def step(row, carry):
+            found = kernels[index[chunk, row]]
+            out[chunk, 0, pl.ds(row, 1), :] = found[0:1]
+            out[chunk, 1, pl.ds(row, 1), :] = found[1:2]
+            return carry
+
+        lax.fori_loop(0, rows, step, 0, unroll=8)
 
 
 def split_out(values, chip, outs):
@@ -172,23 +206,26 @@
         out[...] = values[:, :, lane_block(jnp.bitwise_xor(chip, distance))]
 
 
-def first_kernel(place, table, *refs):
+def first_kernel(layout, info, table, *refs):
     scratch = refs[-1]
     chips = scratch.shape[2] // LANES
     terms, outs = refs[: -1 - chips], refs[-1 - chips : -1]
-    total = terms[0][...]
-    for term in terms[1:]:
-        total = total + term[...]
-    rows, length = total.shape[1:]
-    real, imag = rotate(total.reshape(2 * rows, length), table[0], table[1], -1.0)
+    pairs = pairs_of(layout, terms)
+    sums = []
+    for part in range(2):
+        total = pairs[0][part][...]
+        for pair in pairs[1:]:
+            total = total + pair[part][...]
+        sums.append(total)
+    real, imag = rotate(jnp.concatenate(sums, axis=0), table[0], table[1], -1.0)
     scratch[0] = real
     scratch[1] = imag
-    split_out(scratch, place[0], outs)
-
-
-def cross_kernel(sign, place, table, *refs):
+    split_out(scratch, info[CHIP], outs)
+
+
+def cross_kernel(sign, info, table, *refs):
     blocks, (keep, send, gathered, partial) = refs[:-4], refs[-4:]
-    chip, core = place[0], place[1]
+    chip, core = info[CHIP], info[CORE]
     rows = blocks[0].shape[1]
     for distance, block in enumerate(blocks):
         spot = pl.ds(pl.multiple_of(jnp.bitwise_xor(chip, distance) * rows, rows), rows)
@@ -212,8 +249,9 @@
     send[...] = partial[:, other, :]
 
 
-def correct_kernel(place, table, keep, received, residual, chosen, *refs):
+def correct_kernel(chunk, info, table, keep, received, residuals, chosens, *refs):
     outs, scratch = refs[:-1], refs[-1]
+    residual, chosen = residuals.at[chunk], chosens.at[chunk]
     spectrum_real = keep[0] + received[0]
     spectrum_imag = keep[1] + received[1]
     real = residual[0] - (chosen[0] * spectrum_real - chosen[1] * spectrum_imag)
@@ -222,7 +260,7 @@
     real, imag = rotate(values, table[0], table[1], 1.0)
     scratch[0] = real
     scratch[1] = imag
-    split_out(scratch, place[0], outs)
+    split_out(scratch, info[CHIP], outs)
 
 
 def turned_pieces(offset, factor, real_ref, imag_ref):
@@ -250,15 +288,10 @@
     return lax.div(begin, LANES), pieces
 
 
-def update_kernel(layout, offsets, ids, factor, *refs):
-    arrays, (out, window) = list(refs[:-2]), refs[-2:]
-    pairs = []
-    for planes in layout:
-        if planes == 1:
-            whole = arrays.pop(0)
-            pairs.append((whole.at[0], whole.at[1]))
-        else:
-            pairs.append((arrays.pop(0), arrays.pop(0)))
+def update_kernel(layout, spots, info, offsets, factor, *refs):
+    arrays, (out, window) = refs[:-2], refs[-2:]
+    pairs = pairs_of(layout, arrays)
+    ids = [info[spot] for spot in spots]
     count = len(pairs)
     total = out.shape[3] // LANES
     out[...] = jnp.zeros(out.shape, jnp.float32)
@@ -276,9 +309,9 @@
         window[:, :, pl.ds(piece * LANES, LANES)] = out[0, :, :, spot]
 
 
-def finish_kernel(offsets, ids, factor, window, real, imag, whole, out, buffer, sems):
+def finish_kernel(spot, info, offsets, factor, window, real, imag, whole, out, buffer, sems):
     total = out.shape[3] // LANES
-    item = ids[0]
+    item = info[spot]
     block, pieces = turned_pieces(offsets[item], factor.at[item], real, imag)
 
     def copy(piece):
@@ -314,6 +347,10 @@
         cost_estimate=pl.CostEstimate(flops=cost, bytes_accessed=cost // 64, transcendentals=0),
         **kwargs,
     )
+
+
+def jump_order(chips):
+    return list(range(chips - 1, 0, -1))
 
 
 def grid_of(count):
@@ -334,16 +371,12 @@
     slow, fast = grid_of(facet_count)
     facet = lax.axis_index("facet")
     team = lax.axis_index("team")
-    place = jnp.stack([team // 2, team % 2]).astype(jnp.int32)
     table = jnp.asarray(split_table(length))
     down, right = facet // fast, facet % fast
 
     def near(step, chunk):
         to = (down + step[0]) % slow * fast + (right + step[1]) % fast
         return to * per_facet + chunk
-
-    def listed(values):
-        return jnp.stack(values).astype(jnp.int32)
 
     def move(value, step_slow, step_fast):
         pairs = [
@@ -356,12 +389,12 @@
         return lax.ppermute(value, "facet", pairs)
 
     def exchange(pieces):
-        out = [pieces[0]]
-        for distance in range(1, chips):
+        out = [pieces[0]] + [None] * (chips - 1)
+        for distance in jump_order(chips):
             pairs = [
                 (spot, (spot // 2 ^ distance) * 2 + spot % 2) for spot in range(team_count)
             ]
-            out.append(lax.ppermute(pieces[distance], "team", pairs))
+            out[distance] = lax.ppermute(pieces[distance], "team", pairs)
         return out
 
     def swap(value):
@@ -370,10 +403,7 @@
     slow_steps, fast_steps = range(1, slow), range(1, fast)
     near_steps = [(0, j) for j in fast_steps] + [(i, 0) for i in slow_steps]
     corner_steps = [(i, j) for i in slow_steps for j in fast_steps]
-    onehot = (kernel_index[:, :, None] == jnp.arange(kernels.shape[0], dtype=jnp.int32)).astype(
-        jnp.float32
-    )
-    chosen = jnp.einsum("srk,kac->sarc", onehot, kernels, precision=lax.Precision.HIGHEST)
+    plane = (rows, length)
     block_shape = (2, rows, length)
     piece_shape = (2, rows, LANES)
     matmul_cost = 2 * (2 * rows) * length * (2 * length) * 3
@@ -385,13 +415,24 @@
             pltpu.SemaphoreType.DMA((count, blocks + 1)),
         ]
 
+    last = per_facet - 1
+    corner_keys = [(step, chunk) for step in corner_steps for chunk in chunks]
+    near_keys = [(step, chunk) for chunk in chunks for step in [(0, 0)] + near_steps]
+    gather_keys = [
+        ((-i, -j), chunk) for chunk in chunks for i, j in [(0, 0)] + near_steps + corner_steps
+    ]
+    spots, numbers = {}, [team // 2, team % 2, facet]
+    for key in corner_keys + near_keys + gather_keys:
+        spots[key] = len(numbers)
+        numbers.append(near(*key))
+    info = jnp.stack(numbers).astype(jnp.int32)
+
     def in_hbm(value):
         return pltpu.with_memory_space_constraint(value, pltpu.HBM)
 
     columns = in_hbm(facets)
-    corner_keys = [(step, chunk) for step in corner_steps for chunk in chunks]
     factor, *planes = call(
-        functools.partial(corner_window_kernel, per_facet),
+        functools.partial(corner_window_kernel, per_facet, [spots[key] for key in corner_keys]),
         [(subgrids, 2, length)] + [(per_facet, rows, length)] * (2 * len(corner_steps)),
         window_scratch(len(corner_keys))
         + [
@@ -404,7 +445,7 @@
         8 * MIB,
         matmul_cost // 8,
     )(
-        listed([near(step, chunk) for step, chunk in corner_keys] + [facet]),
+        info,
         in_hbm(grid_offsets),
         in_hbm(facet_offsets),
         in_hbm(taper.reshape(1, length)),
@@ -415,23 +456,29 @@
         by_fast[i, j] = move(planes[2 * spot], 0, j)
         by_slow[i, j] = move(planes[2 * spot + 1], i, 0)
 
-    near_keys = [(step, chunk) for chunk in chunks for step in [(0, 0)] + near_steps]
+    near_layout = [2 if chunk == 0 and step != (0, 0) else 1 for step, chunk in near_keys]
     outs = call(
-        window_kernel,
-        [block_shape] * len(near_keys),
+        functools.partial(window_kernel, near_layout, [spots[key] for key in near_keys]),
+        [shape for count in near_layout for shape in ([block_shape], [plane] * 2)[count - 1]],
         window_scratch(len(near_keys)),
         [SMEM, SMEM, HBM, VMEM],
         12 * MIB,
         matmul_cost // 4,
-    )(grid_offsets, listed([near(step, chunk) for step, chunk in near_keys]), columns, factor)
-    terms = dict(zip(near_keys, outs))
+    )(info, grid_offsets, columns, factor)
+    terms = {}
+    for key, count in zip(near_keys, near_layout):
+        terms[key], outs = tuple(outs[:count]), outs[count:]
+
+    (chosen,) = call(
+        choose_kernel, [residual.shape], [], [SMEM, VMEM], 4 * MIB, matmul_cost // 8
+    )(kernel_index, kernels)
 
     def join(term, corners, part, chunk):
         if not corners:
             return term
         (joined,) = call(
-            functools.partial(join_kernel, part, chunk),
-            [block_shape],
+            functools.partial(join_kernel, part, chunk, term.ndim == 3),
+            [term.shape],
             [],
             [VMEM] * (1 + len(corners)),
             2 * MIB,
@@ -441,25 +488,35 @@
 
     def scatter(chunk):
         received = [terms[(0, 0), chunk]]
-        for i in slow_steps:
-            corners = [by_fast[i, j] for j in fast_steps]
-            joined = join(terms[(i, 0), chunk], corners, 0, chunk)
-            received.append(move(joined, i, 0))
-        for j in fast_steps:
-            corners = [by_slow[i, j] for i in slow_steps]
-            joined = join(terms[(0, j), chunk], corners, 1, chunk)
-            received.append(move(joined, 0, j))
+        for i, j in near_steps:
+            axis = "slow" if i else "fast"
+            part = 0 if i else 1
+            if i:
+                corners = [by_fast[i, j] for j in fast_steps]
+            else:
+                corners = [by_slow[i, j] for i in slow_steps]
+            i, j = (i, 0) if axis == "slow" else (0, j)
+            term = terms[(i, j), chunk]
+            if len(term) == 1:
+                joined = join(term[0], corners, part, chunk)
+                received.append((move(joined, i, j),))
+            else:
+                early = move(term[1 - part], i, j)
+                joined = join(term[part], corners, part, chunk)
+                late = move(joined, i, j)
+                received.append((late, early) if part == 0 else (early, late))
         return received
 
     def first_transform(received):
+        arrays = [array for item in received for array in item]
         return call(
-            first_kernel,
+            functools.partial(first_kernel, [len(item) for item in received]),
             [piece_shape] * chips,
             [pltpu.VMEM(block_shape, jnp.float32)],
-            [SMEM, VMEM] + [VMEM] * len(received),
+            [SMEM, VMEM] + [VMEM] * len(arrays),
             8 * MIB,
             matmul_cost,
-        )(place, table, *received)
+        )(info, table, *arrays)
 
     def cross(pieces, sign):
         return call(
@@ -472,26 +529,36 @@
             [SMEM, VMEM] + [VMEM] * chips,
             8 * MIB,
             matmul_cost,
-        )(place, table, *pieces)
+        )(info, table, *pieces)
 
     def correct(keep, received, chunk):
         return call(
-            correct_kernel,
+            functools.partial(correct_kernel, chunk),
             [piece_shape] * chips,
             [pltpu.VMEM(block_shape, jnp.float32)],
             [SMEM] + [VMEM] * 5,
             8 * MIB,
             matmul_cost,
-        )(place, table, keep, received, residual[chunk], chosen[chunk])
-
-    def gather(own):
+        )(info, table, keep, received, residual, chosen)
+
+    def gather(own, chunk):
         found = {(0, 0): (own,)}
-        for j in fast_steps:
-            found[0, j] = (move(own, 0, j),)
-        for i in slow_steps:
-            found[i, 0] = (move(own, i, 0),)
+        split = chunk == last
+        for i, j in near_steps:
+            if split:
+                part = 1 if i else 0
+                early = move(own[part], i, j)
+                late = move(own[1 - part], i, j)
+                found[i, j] = (late, early) if part else (early, late)
+            else:
+                whole = move(own, i, j)
+                found[i, j] = (whole,)
+
+        def part_of(item, part):
+            return item[part] if len(item) == 2 else item[0][part]
+
         for i, j in corner_steps:
-            found[i, j] = (move(found[0, j][0][0], i, 0), move(found[i, 0][0][1], 0, j))
+            found[i, j] = (move(part_of(found[0, j], 0), i, 0), move(part_of(found[i, 0], 1), 0, j))
         return found
 
     received = [scatter(chunk) for chunk in chunks]
@@ -500,28 +567,27 @@
     swapped = [swap(halves[chunk][1]) for chunk in chunks]
     pieces = [exchange(correct(halves[chunk][0], swapped[chunk], chunk)) for chunk in chunks]
     halves = [cross(pieces[chunk], 1.0) for chunk in chunks]
-    ids, items = [], []
+    keys, items = [], []
     for chunk in chunks:
         keep, sent = halves[chunk]
         own = keep + swap(sent)
-        for (i, j), found in gather(own).items():
-            ids.append(near((-i, -j), chunk))
+        for (i, j), found in gather(own, chunk).items():
+            keys.append(spots[(-i, -j), chunk])
             items.append(found)
-    ids = listed(ids)
     *first_items, last_item = items
     if len(last_item) == 1:
         last_item = (last_item[0][0], last_item[0][1])
     arrays = [array for item in first_items for array in item]
     whole, window = call(
-        functools.partial(update_kernel, tuple(len(item) for item in first_items)),
+        functools.partial(update_kernel, [len(item) for item in first_items], keys),
         [(1, 2, rows, facet_len), (2, rows, length + LANES)],
         [],
         [SMEM, SMEM, VMEM] + [VMEM] * len(arrays),
         16 * MIB,
         matmul_cost,
-    )(grid_offsets, ids, factor, *arrays)
+    )(info, grid_offsets, factor, *arrays)
     (update,) = call(
-        finish_kernel,
+        functools.partial(finish_kernel, keys[-1]),
         [(1, 2, rows, facet_len)],
         [
             pltpu.VMEM((blocks + 1, 2, rows, LANES), jnp.float32),
@@ -532,7 +598,7 @@
         matmul_cost // 8,
         out_specs=[HBM],
         input_output_aliases={6: 0},
-    )(grid_offsets, ids[-1:], factor, window, *last_item, whole)
+    )(info, grid_offsets, factor, window, *last_item, whole)
     return update
 
 

time: 95.9 us -> 85.5 us (0.89)
  waiting for transfers between devices: 35.8 us -> 21.5 us
  starting transfers between devices: 35.3 us -> 42.3 us
  Pallas kernels: 23.3 us -> 21 us
    ppermute x14 -> x18, waiting for transfers between devices: 22.1 us -> 14 us  [move(): return lax.ppermute(value, 'facet', pairs)]
    ppermute x14 -> x18, starting transfers between devices: 17.2 us -> 24.3 us  [move(): return lax.ppermute(value, 'facet', pairs)]
    ppermute x12, waiting for transfers between devices: 13.7 us -> 7.48 us  [exchange(): out[distance] = lax.ppermute(pieces[distance], 'team', pairs)]
    pallas_call x12 -> x13, Pallas kernels: 18.5 us -> 16 us  [the longest x1 3.21 us: tiled_device(): call(functools.partial(window_kernel, near_layout, [spots[key] for key in...]
  transfers between devices with their start and end apart: 30 -> 34, of which waited for: 14 -> 10; matrix products, arithmetic and copies ran while one was open for 1% -> 0% of each run, Pallas kernels for 19% -> 20%
where the time goes in v1:
time: 85.5 us; the launch traced here: 85.3 us
  starting transfers between devices  42.3 us (49%)
  waiting for transfers between devices  21.5 us (25%)
  Pallas kernels  21 us (25%)
    ppermute x18, starting transfers between devices, move(): return lax.ppermute(value, 'facet', pairs)  24.3 us
    ppermute x12, starting transfers between devices, exchange(): out[distance] = lax.ppermute(pieces[distance], 'team', pairs)  17.8 us
    ppermute x18, waiting for transfers between devices, move(): return lax.ppermute(value, 'facet', pairs)  14 us
    ppermute x12, waiting for transfers between devices, exchange(): out[distance] = lax.ppermute(pieces[distance], 'team', pairs)  7.48 us
    pallas_call x4, Pallas kernels, cross(): call(functools.partial(cross_kernel, sign), [block_shape] * 2, [pltpu.VME...  4.91 us
    pallas_call x1, Pallas kernels, tiled_device(): call(functools.partial(window_kernel, near_layout, [spots[key] for key in...  3.21 us
    pallas_call x1, Pallas kernels, tiled_device(): call(functools.partial(update_kernel, [len(item) for item in first_items]...  2.85 us
    pallas_call x1, Pallas kernels, tiled_device(): call(functools.partial(corner_window_kernel, per_facet, [spots[key] for k...  2.76 us
  transfers between devices with their start and end apart: 34, of which 10 were waited for; matrix products, arithmetic and copies ran while one was open for 0% of the time, Pallas kernels for 20%

profile of v1, /device:TPU:0, one launch (start us, length us, event | category | flops | bytes accessed | tf_op | source)
XLA Modules:
  0.0 85.3 jit_solution(3155160457044472048)
XLA Ops:
  0.1 2.8 %shard_map.82 = (f32[8,2,512]{2,1,0:T(2,128)S(1)}, f32[2,64,512]{2,1,0:T(8,128)S(1)}, f32[2,64,512]{2,1,0:T(8,128)S(1)}) custom-call(s32[19]{0:T(128)S(1)} %stack.73.info, s32[8]{0:T(128)} %offsets.5, s32[4]{0:T(128)} %facet_offsets_hbm.1, f32[1,512]{1,0:T(1,128)} %bitcast.26, f32[1,2,64,5120]{3,2,1,0:T(8,128)} %columns.3), custom_call_target="tpu_custom_call" | custom-call | flops 50331648 | bytes 786432 | tf_op jit(solution)/shard_map/pallas_call | solution.py:434
  2.9 3.0 %collective-permute-start.3 = (f32[2,64,512]{2,1,0:T(8,128)S(1)}, f32[2,64,512]{2,1,0:T(8,128)S(1)}, u32[]{:S(2)}, u32[]{:S(2)}) collective-permute-start(f32[2,64,512]{2,1,0:T(8,128)S(1)} %get-tuple-element.48), channel_id=1, source_target_pairs={{0,8},{8,0},{16,24},{24,16},{1,9},{9,1},{17,25},{25,17},{2,10},{10... | collective-permute-start | bytes 786440 | tf_op jit(solution)/shard_map/ppermute | solution.py:389
  5.9 1.5 %collective-permute-start.1 = (f32[2,64,512]{2,1,0:T(8,128)S(1)}, f32[2,64,512]{2,1,0:T(8,128)S(1)}, u32[]{:S(2)}, u32[]{:S(2)}) collective-permute-start(f32[2,64,512]{2,1,0:T(8,128)S(1)} %get-tuple-element.46), channel_id=1, source_target_pairs={{0,16},{8,24},{16,0},{24,8},{1,17},{9,25},{17,1},{25,9},{2,18},{10... | collective-permute-start | bytes 786440 | tf_op jit(solution)/shard_map/ppermute | solution.py:389
  7.4 3.2 %shard_map.83 = (f32[2,64,512]{2,1,0:T(8,128)S(1)}, f32[64,512]{1,0:T(8,128)S(1)}, f32[64,512]{1,0:T(8,128)S(1)}, f32[64,512]{1,0:T(8,128)S(1)}, f32[64,512]{1,0...) custom-call(s32[19]{0:T(128)S(1)} %stack.73.info, s32[8]{0:T(128)S(1)} %copy-done.3, ...), custom_call_target="tpu_custom_call" | custom-call | flops 100663296 | bytes 1572864 | tf_op jit(solution)/shard_map/pallas_call | solution.py:460
  12.3 2.6 %collective-permute-start.19 = (f32[2,64,512]{2,1,0:T(8,128)S(1)}, f32[2,64,512]{2,1,0:T(8,128)S(1)}, u32[]{:S(2)}, u32[]{:S(2)}) collective-permute-start(f32[2,64,512]{2,1,0:T(8,128)S(1)} %shard_map.92), channel_id=1, source_target_pairs={{0,16},{8,24},{16,0},{24,8},{1,17},{9,25},{17,1},{25,9},{2,18},{10... | collective-permute-start | bytes 786440 | tf_op jit(solution)/shard_map/ppermute | solution.py:389
  15.0 1.8 %collective-permute-start.18 = (f32[2,64,512]{2,1,0:T(8,128)S(1)}, f32[2,64,512]{2,1,0:T(8,128)S(1)}, u32[]{:S(2)}, u32[]{:S(2)}) collective-permute-start(f32[2,64,512]{2,1,0:T(8,128)S(1)} %shard_map.91), channel_id=1, source_target_pairs={{0,8},{8,0},{16,24},{24,16},{1,9},{9,1},{17,25},{25,17},{2,10},{10... | collective-permute-start | bytes 786440 | tf_op jit(solution)/shard_map/ppermute | solution.py:389
  17.0 1.9 %collective-permute-start.4 = (f32[64,512]{1,0:T(8,128)S(1)}, f32[64,512]{1,0:T(8,128)S(1)}, u32[]{:S(2)}, u32[]{:S(2)}) collective-permute-start(f32[64,512]{1,0:T(8,128)S(1)} %shard_map.85), channel_id=1, source_target_pairs={{0,16},{8,24},{16,0},{24,8},{1,17},{9,25},{17,1},{25,9},{2,18},{10... | collective-permute-start | bytes 393224 | tf_op jit(solution)/shard_map/ppermute | solution.py:389
  19.3 4.7 %collective-permute-done.5.refs_4_ = f32[64,512]{1,0:T(8,128)S(1)} collective-permute-done((f32[64,512]{1,0:T(8,128)S(1)}, f32[64,512]{1,0:T(8,128)S(1)}, u32[]{:S(2)}, u32[]{:S(2)}) %collective-permute-start.5) | collective-permute-done | bytes 131104 | tf_op jit(solution)/shard_map/ppermute | solution.py:389
  24.0 1.4 %collective-permute-done.4.refs_3_ = f32[64,512]{1,0:T(8,128)S(1)} collective-permute-done((f32[64,512]{1,0:T(8,128)S(1)}, f32[64,512]{1,0:T(8,128)S(1)}, u32[]{:S(2)}, u32[]{:S(2)}) %collective-permute-start.4) | collective-permute-done | bytes 131104 | tf_op jit(solution)/shard_map/ppermute | solution.py:389
  26.6 1.6 %collective-permute-start.6 = (f32[2,64,128]{2,1,0:T(8,128)S(1)}, f32[2,64,128]{2,1,0:T(8,128)S(1)}, u32[]{:S(2)}, u32[]{:S(2)}) collective-permute-start(f32[2,64,128]{2,1,0:T(8,128)S(1)} %get-tuple-element.51), channel_id=1, source_target_pairs={{0,2},{1,3},{2,0},{3,1},{4,6},{5,7},{6,4},{7,5},{8,10},{9,11},{10,... | collective-permute-start | bytes 196616 | tf_op jit(solution)/shard_map/ppermute | solution.py:397
  28.2 2.6 %collective-permute-start.7 = (f32[2,64,128]{2,1,0:T(8,128)S(1)}, f32[2,64,128]{2,1,0:T(8,128)S(1)}, u32[]{:S(2)}, u32[]{:S(2)}) collective-permute-start(f32[2,64,128]{2,1,0:T(8,128)S(1)} %get-tuple-element.52), channel_id=1, source_target_pairs={{0,4},{1,5},{2,6},{3,7},{4,0},{5,1},{6,2},{7,3},{8,12},{9,13},{10,... | collective-permute-start | bytes 196616 | tf_op jit(solution)/shard_map/ppermute | solution.py:397
  32.9 3.5 %collective-permute-start.21 = (f32[2,64,128]{2,1,0:T(8,128)S(1)}, f32[2,64,128]{2,1,0:T(8,128)S(1)}, u32[]{:S(2)}, u32[]{:S(2)}) collective-permute-start(f32[2,64,128]{2,1,0:T(8,128)S(1)} %get-tuple-element.67), channel_id=1, source_target_pairs={{0,4},{1,5},{2,6},{3,7},{4,0},{5,1},{6,2},{7,3},{8,12},{9,13},{10,... | collective-permute-start | bytes 196616 | tf_op jit(solution)/shard_map/ppermute | solution.py:397
  38.3 2.0 %collective-permute-done.21.refs_2_ = f32[2,64,128]{2,1,0:T(8,128)S(1)} collective-permute-done((f32[2,64,128]{2,1,0:T(8,128)S(1)}, f32[2,64,128]{2,1,0:T(8,128)S(1)}, u32[]{:S(2)}, u32[]{:S(2)}) %collective-permute-start.21) | collective-permute-done | bytes 65568 | tf_op jit(solution)/shard_map/ppermute | solution.py:397
  40.2 2.3 %collective-permute-done.22.refs_3_ = f32[2,64,128]{2,1,0:T(8,128)S(1)} collective-permute-done((f32[2,64,128]{2,1,0:T(8,128)S(1)}, f32[2,64,128]{2,1,0:T(8,128)S(1)}, u32[]{:S(2)}, u32[]{:S(2)}) %collective-permute-start.22) | collective-permute-done | bytes 65568 | tf_op jit(solution)/shard_map/ppermute | solution.py:397
  42.5 1.2 %shard_map.94 = (f32[2,64,512]{2,1,0:T(8,128)S(1)}, f32[2,64,512]{2,1,0:T(8,128)S(1)}) custom-call(s32[19]{0:T(128)S(1)} %stack.73.info, bf16[2,512,1024]{2,1,0:T(8,128)(2,1)S(1)} %copy-done, f32[2,64,128]{2,1,0:T(8,128)S(1)} %get-tuple-element.65.refs_0_, f32[2,64,128]{2,1,0:T(8,128)S(1)} %collective-permute-done.20.refs_1_, ...), custom_call_target="tpu_custom_call" | custom-call | flops 402653184 | bytes 6291456 | tf_op jit(solution)/shard_map/pallas_call | solution.py:522
  46.2 1.3 %collective-permute-start.11 = (f32[2,64,128]{2,1,0:T(8,128)S(1)}, f32[2,64,128]{2,1,0:T(8,128)S(1)}, u32[]{:S(2)}, u32[]{:S(2)}) collective-permute-start(f32[2,64,128]{2,1,0:T(8,128)S(1)} %get-tuple-element.58), channel_id=1, source_target_pairs={{0,4},{1,5},{2,6},{3,7},{4,0},{5,1},{6,2},{7,3},{8,12},{9,13},{10,... | collective-permute-start | bytes 196616 | tf_op jit(solution)/shard_map/ppermute | solution.py:397
  47.5 3.0 %collective-permute-start.12 = (f32[2,64,128]{2,1,0:T(8,128)S(1)}, f32[2,64,128]{2,1,0:T(8,128)S(1)}, u32[]{:S(2)}, u32[]{:S(2)}) collective-permute-start(f32[2,64,128]{2,1,0:T(8,128)S(1)} %get-tuple-element.59), channel_id=1, source_target_pairs={{0,6},{1,7},{2,4},{3,5},{4,2},{5,3},{6,0},{7,1},{8,14},{9,15},{10,... | collective-permute-start | bytes 196616 | tf_op jit(solution)/shard_map/ppermute | solution.py:397
  51.8 1.3 %collective-permute-start.25 = (f32[2,64,128]{2,1,0:T(8,128)S(1)}, f32[2,64,128]{2,1,0:T(8,128)S(1)}, u32[]{:S(2)}, u32[]{:S(2)}) collective-permute-start(f32[2,64,128]{2,1,0:T(8,128)S(1)} %get-tuple-element.73), channel_id=1, source_target_pairs={{0,4},{1,5},{2,6},{3,7},{4,0},{5,1},{6,2},{7,3},{8,12},{9,13},{10,... | collective-permute-start | bytes 196616 | tf_op jit(solution)/shard_map/ppermute | solution.py:397
  53.2 3.0 %collective-permute-start.26 = (f32[2,64,128]{2,1,0:T(8,128)S(1)}, f32[2,64,128]{2,1,0:T(8,128)S(1)}, u32[]{:S(2)}, u32[]{:S(2)}) collective-permute-start(f32[2,64,128]{2,1,0:T(8,128)S(1)} %get-tuple-element.74), channel_id=1, source_target_pairs={{0,6},{1,7},{2,4},{3,5},{4,2},{5,3},{6,0},{7,1},{8,14},{9,15},{10,... | collective-permute-start | bytes 196616 | tf_op jit(solution)/shard_map/ppermute | solution.py:397
  57.5 3.0 %collective-permute-done.25.refs_2_ = f32[2,64,128]{2,1,0:T(8,128)S(1)} collective-permute-done((f32[2,64,128]{2,1,0:T(8,128)S(1)}, f32[2,64,128]{2,1,0:T(8,128)S(1)}, u32[]{:S(2)}, u32[]{:S(2)}) %collective-permute-start.25) | collective-permute-done | bytes 65568 | tf_op jit(solution)/shard_map/ppermute | solution.py:397
  60.5 1.2 %shard_map.96 = (f32[2,64,512]{2,1,0:T(8,128)S(1)}, f32[2,64,512]{2,1,0:T(8,128)S(1)}) custom-call(s32[19]{0:T(128)S(1)} %stack.73.info, bf16[2,512,1024]{2,1,0:T(8,128)(2,1)S(1)} %copy-done, f32[2,64,128]{2,1,0:T(8,128)S(1)} %get-tuple-element.71.refs_0_, f32[2,64,128]{2,1,0:T(8,128)S(1)} %collective-permute-done.24.refs_1_, ...), custom_call_target="tpu_custom_call" | custom-call | flops 402653184 | bytes 6291456 | tf_op jit(solution)/shard_map/pallas_call | solution.py:522
  61.9 1.6 %collective-permute-start.15 = (f32[2,64,512]{2,1,0:T(8,128)S(1)}, f32[2,64,512]{2,1,0:T(8,128)S(1)}, u32[]{:S(2)}, u32[]{:S(2)}) collective-permute-start(f32[2,64,512]{2,1,0:T(8,128)S(1)} %add.161.refs_0_), channel_id=1, source_target_pairs={{0,16},{8,24},{16,0},{24,8},{1,17},{9,25},{17,1},{25,9},{2,18},{10... | collective-permute-start | bytes 786440 | tf_op jit(solution)/shard_map/ppermute | solution.py:389
  63.5 1.5 %collective-permute-start.14 = (f32[2,64,512]{2,1,0:T(8,128)S(1)}, f32[2,64,512]{2,1,0:T(8,128)S(1)}, u32[]{:S(2)}, u32[]{:S(2)}) collective-permute-start(f32[2,64,512]{2,1,0:T(8,128)S(1)} %add.161.refs_0_), channel_id=1, source_target_pairs={{0,8},{8,0},{16,24},{24,16},{1,9},{9,1},{17,25},{25,17},{2,10},{10... | collective-permute-start | bytes 786440 | tf_op jit(solution)/shard_map/ppermute | solution.py:389
  67.7 3.5 %collective-permute-done.15.refs_2_ = f32[2,64,512]{2,1,0:T(8,128)S(1)} collective-permute-done((f32[2,64,512]{2,1,0:T(8,128)S(1)}, f32[2,64,512]{2,1,0:T(8,128)S(1)}, u32[]{:S(2)}, u32[]{:S(2)}) %collective-permute-start.15) | collective-permute-done | bytes 262176 | tf_op jit(solution)/shard_map/ppermute | solution.py:389
  71.1 1.5 %collective-permute-start.28 = (f32[64,512]{1,0:T(8,128)S(1)}, f32[64,512]{1,0:T(8,128)S(1)}, u32[]{:S(2)}, u32[]{:S(2)}) collective-permute-start(f32[64,512]{1,0:T(8,128)S(1)} %get-tuple-element.80), channel_id=1, source_target_pairs={{0,8},{8,0},{16,24},{24,16},{1,9},{9,1},{17,25},{25,17},{2,10},{10... | collective-permute-start | bytes 393224 | tf_op jit(solution)/shard_map/ppermute | solution.py:389
  72.6 1.5 %collective-permute-start.17 = (f32[64,512]{1,0:T(8,128)S(1)}, f32[64,512]{1,0:T(8,128)S(1)}, u32[]{:S(2)}, u32[]{:S(2)}) collective-permute-start(f32[64,512]{1,0:T(8,128)S(1)} %slice_bitcast_fusion.2), channel_id=1, source_target_pairs={{0,8},{8,0},{16,24},{24,16},{1,9},{9,1},{17,25},{25,17},{2,10},{10... | collective-permute-start | bytes 393224 | tf_op jit(solution)/shard_map/ppermute | solution.py:389
  74.2 1.3 %collective-permute-start.16 = (f32[64,512]{1,0:T(8,128)S(1)}, f32[64,512]{1,0:T(8,128)S(1)}, u32[]{:S(2)}, u32[]{:S(2)}) collective-permute-start(f32[64,512]{1,0:T(8,128)S(1)} %slice_bitcast_fusion.3), channel_id=1, source_target_pairs={{0,16},{8,24},{16,0},{24,8},{1,17},{9,25},{17,1},{25,9},{2,18},{10... | collective-permute-start | bytes 393224 | tf_op jit(solution)/shard_map/ppermute | solution.py:389
  75.5 1.5 %collective-permute-start.33 = (f32[64,512]{1,0:T(8,128)S(1)}, f32[64,512]{1,0:T(8,128)S(1)}, u32[]{:S(2)}, u32[]{:S(2)}) collective-permute-start(f32[64,512]{1,0:T(8,128)S(1)} %collective-permute-done.31.refs_9_), channel_id=1, source_target_pairs={{0,8},{8,0},{16,24},{24,16},{1,9},{9,1},{17,25},{25,17},{2,10},{10... | collective-permute-start | bytes 393224 | tf_op jit(solution)/shard_map/ppermute | solution.py:389
  77.0 1.3 %collective-permute-done.28.refs_6_ = f32[64,512]{1,0:T(8,128)S(1)} collective-permute-done((f32[64,512]{1,0:T(8,128)S(1)}, f32[64,512]{1,0:T(8,128)S(1)}, u32[]{:S(2)}, u32[]{:S(2)}) %collective-permute-start.28) | collective-permute-done | bytes 131104 | tf_op jit(solution)/shard_map/ppermute | solution.py:389
  79.0 2.1 %collective-permute-done.17.refs_4_ = f32[64,512]{1,0:T(8,128)S(1)} collective-permute-done((f32[64,512]{1,0:T(8,128)S(1)}, f32[64,512]{1,0:T(8,128)S(1)}, u32[]{:S(2)}, u32[]{:S(2)}) %collective-permute-start.17) | collective-permute-done | bytes 131104 | tf_op jit(solution)/shard_map/ppermute | solution.py:389
  81.1 2.9 %shard_map.97 = (f32[1,2,64,5120]{3,2,1,0:T(8,128)}, f32[2,64,640]{2,1,0:T(8,128)S(1)}) custom-call(s32[19]{0:T(128)S(1)} %stack.73.info, s32[8]{0:T(128)S(1)} %copy-done.3, f32[8,2,512]{2,1,0:T(2,128)S(1)} %get-tuple-element.42.factor, f32[2,64,512]{2,1,0:T(8,128)S(1)} %add.161.refs_0_, f32[2,64,512]{2,1,0:T(8,128)S(1)} %collective-permute-done.14.refs_1_, ...), custom_call_target="tpu_custom_call" | custom-call | flops 402653184 | bytes 6291456 | tf_op jit(solution)/shard_map/pallas_call | solution.py:581
  83.9 1.4 %shard_map.98 = f32[1,2,64,5120]{3,2,1,0:T(8,128)} custom-call(s32[19]{0:T(128)S(1)} %stack.73.info, s32[8]{0:T(128)S(1)} %copy-done.3, f32[8,2,512]{2,1,0:T(2,128)S(1)} %get-tuple-element.42.factor, f32[2,64,640]{2,1,0:T(8,128)S(1)} %get-tuple-element.77.window, f32[64,512]{1,0:T(8,128)S(1)} %collective-permute-done.32.real, ...), custom_call_target="tpu_custom_call", output_to_operand_aliasing={{}: (6, {})} | custom-call | flops 50331648 | bytes 786432 | tf_op jit(solution)/shard_map/pallas_call | solution.py:589
  (69 shorter events, 16.1 us)
Async XLA Ops:
  2.9 9.4 %collective-permute-start.3 = (f32[2,64,512]{2,1,0:T(8,128)S(1)}, f32[2,64,512]{2,1,0:T(8,128)S(1)}, u32[]{:S(2)}, u32[]{:S(2)}) collective-permute-start(f32[2,64,512]{2,1,0:T(8,128)S(1)} %get-tuple-element.48), channel_id=1, source_target_pairs={{0,8},{8,0},{16,24},{24,16},{1,9},{9,1},{17,25},{25,17},{2,10},{10... | collective-permute-start | bytes 786440 | tf_op jit(solution)/shard_map/ppermute | solution.py:389
  5.9 9.1 %collective-permute-start.1 = (f32[2,64,512]{2,1,0:T(8,128)S(1)}, f32[2,64,512]{2,1,0:T(8,128)S(1)}, u32[]{:S(2)}, u32[]{:S(2)}) collective-permute-start(f32[2,64,512]{2,1,0:T(8,128)S(1)} %get-tuple-element.46), channel_id=1, source_target_pairs={{0,16},{8,24},{16,0},{24,8},{1,17},{9,25},{17,1},{25,9},{2,18},{10... | collective-permute-start | bytes 786440 | tf_op jit(solution)/shard_map/ppermute | solution.py:389
  10.6 8.3 %collective-permute-start = (f32[64,512]{1,0:T(8,128)S(1)}, f32[64,512]{1,0:T(8,128)S(1)}, u32[]{:S(2)}, u32[]{:S(2)}) collective-permute-start(f32[64,512]{1,0:T(8,128)S(1)} %get-tuple-element.44), channel_id=1, source_target_pairs={{0,8},{8,0},{16,24},{24,16},{1,9},{9,1},{17,25},{25,17},{2,10},{10... | collective-permute-start | bytes 393224 | tf_op jit(solution)/shard_map/ppermute | solution.py:389
  12.3 18.7 %collective-permute-start.19 = (f32[2,64,512]{2,1,0:T(8,128)S(1)}, f32[2,64,512]{2,1,0:T(8,128)S(1)}, u32[]{:S(2)}, u32[]{:S(2)}) collective-permute-start(f32[2,64,512]{2,1,0:T(8,128)S(1)} %shard_map.92), channel_id=1, source_target_pairs={{0,16},{8,24},{16,0},{24,8},{1,17},{9,25},{17,1},{25,9},{2,18},{10... | collective-permute-start | bytes 786440 | tf_op jit(solution)/shard_map/ppermute | solution.py:389
  15.0 16.0 %collective-permute-start.18 = (f32[2,64,512]{2,1,0:T(8,128)S(1)}, f32[2,64,512]{2,1,0:T(8,128)S(1)}, u32[]{:S(2)}, u32[]{:S(2)}) collective-permute-start(f32[2,64,512]{2,1,0:T(8,128)S(1)} %shard_map.91), channel_id=1, source_target_pairs={{0,8},{8,0},{16,24},{24,16},{1,9},{9,1},{17,25},{25,17},{2,10},{10... | collective-permute-start | bytes 786440 | tf_op jit(solution)/shard_map/ppermute | solution.py:389
  16.8 7.2 %collective-permute-start.5 = (f32[64,512]{1,0:T(8,128)S(1)}, f32[64,512]{1,0:T(8,128)S(1)}, u32[]{:S(2)}, u32[]{:S(2)}) collective-permute-start(f32[64,512]{1,0:T(8,128)S(1)} %get-tuple-element.49), channel_id=1, source_target_pairs={{0,16},{8,24},{16,0},{24,8},{1,17},{9,25},{17,1},{25,9},{2,18},{10... | collective-permute-start | bytes 393224 | tf_op jit(solution)/shard_map/ppermute | solution.py:389
  17.0 8.4 %collective-permute-start.4 = (f32[64,512]{1,0:T(8,128)S(1)}, f32[64,512]{1,0:T(8,128)S(1)}, u32[]{:S(2)}, u32[]{:S(2)}) collective-permute-start(f32[64,512]{1,0:T(8,128)S(1)} %shard_map.85), channel_id=1, source_target_pairs={{0,16},{8,24},{16,0},{24,8},{1,17},{9,25},{17,1},{25,9},{2,18},{10... | collective-permute-start | bytes 393224 | tf_op jit(solution)/shard_map/ppermute | solution.py:389
  18.9 6.5 %collective-permute-start.2 = (f32[64,512]{1,0:T(8,128)S(1)}, f32[64,512]{1,0:T(8,128)S(1)}, u32[]{:S(2)}, u32[]{:S(2)}) collective-permute-start(f32[64,512]{1,0:T(8,128)S(1)} %shard_map.84), channel_id=1, source_target_pairs={{0,8},{8,0},{16,24},{24,16},{1,9},{9,1},{17,25},{25,17},{2,10},{10... | collective-permute-start | bytes 393224 | tf_op jit(solution)/shard_map/ppermute | solution.py:389
  26.6 9.9 %collective-permute-start.6 = (f32[2,64,128]{2,1,0:T(8,128)S(1)}, f32[2,64,128]{2,1,0:T(8,128)S(1)}, u32[]{:S(2)}, u32[]{:S(2)}) collective-permute-start(f32[2,64,128]{2,1,0:T(8,128)S(1)} %get-tuple-element.51), channel_id=1, source_target_pairs={{0,2},{1,3},{2,0},{3,1},{4,6},{5,7},{6,4},{7,5},{8,10},{9,11},{10,... | collective-permute-start | bytes 196616 | tf_op jit(solution)/shard_map/ppermute | solution.py:397
  28.2 8.5 %collective-permute-start.7 = (f32[2,64,128]{2,1,0:T(8,128)S(1)}, f32[2,64,128]{2,1,0:T(8,128)S(1)}, u32[]{:S(2)}, u32[]{:S(2)}) collective-permute-start(f32[2,64,128]{2,1,0:T(8,128)S(1)} %get-tuple-element.52), channel_id=1, source_target_pairs={{0,4},{1,5},{2,6},{3,7},{4,0},{5,1},{6,2},{7,3},{8,12},{9,13},{10,... | collective-permute-start | bytes 196616 | tf_op jit(solution)/shard_map/ppermute | solution.py:397
  30.8 6.2 %collective-permute-start.8 = (f32[2,64,128]{2,1,0:T(8,128)S(1)}, f32[2,64,128]{2,1,0:T(8,128)S(1)}, u32[]{:S(2)}, u32[]{:S(2)}) collective-permute-start(f32[2,64,128]{2,1,0:T(8,128)S(1)} %get-tuple-element.53), channel_id=1, source_target_pairs={{0,6},{1,7},{2,4},{3,5},{4,2},{5,3},{6,0},{7,1},{8,14},{9,15},{10,... | collective-permute-start | bytes 196616 | tf_op jit(solution)/shard_map/ppermute | solution.py:397
  32.2 6.0 %collective-permute-start.20 = (f32[2,64,128]{2,1,0:T(8,128)S(1)}, f32[2,64,128]{2,1,0:T(8,128)S(1)}, u32[]{:S(2)}, u32[]{:S(2)}) collective-permute-start(f32[2,64,128]{2,1,0:T(8,128)S(1)} %get-tuple-element.66), channel_id=1, source_target_pairs={{0,2},{1,3},{2,0},{3,1},{4,6},{5,7},{6,4},{7,5},{8,10},{9,11},{10,... | collective-permute-start | bytes 196616 | tf_op jit(solution)/shard_map/ppermute | solution.py:397
  32.9 7.3 %collective-permute-start.21 = (f32[2,64,128]{2,1,0:T(8,128)S(1)}, f32[2,64,128]{2,1,0:T(8,128)S(1)}, u32[]{:S(2)}, u32[]{:S(2)}) collective-permute-start(f32[2,64,128]{2,1,0:T(8,128)S(1)} %get-tuple-element.67), channel_id=1, source_target_pairs={{0,4},{1,5},{2,6},{3,7},{4,0},{5,1},{6,2},{7,3},{8,12},{9,13},{10,... | collective-permute-start | bytes 196616 | tf_op jit(solution)/shard_map/ppermute | solution.py:397
  36.4 6.1 %collective-permute-start.22 = (f32[2,64,128]{2,1,0:T(8,128)S(1)}, f32[2,64,128]{2,1,0:T(8,128)S(1)}, u32[]{:S(2)}, u32[]{:S(2)}) collective-permute-start(f32[2,64,128]{2,1,0:T(8,128)S(1)} %get-tuple-element.68), channel_id=1, source_target_pairs={{0,6},{1,7},{2,4},{3,5},{4,2},{5,3},{6,0},{7,1},{8,14},{9,15},{10,... | collective-permute-start | bytes 196616 | tf_op jit(solution)/shard_map/ppermute | solution.py:397
  38.2 6.7 %collective-permute-start.9 = (f32[2,64,512]{2,1,0:T(8,128)S(1)}, f32[2,64,512]{2,1,0:T(8,128)S(1)}, u32[]{:S(2)}, u32[]{:S(2)}) collective-permute-start(f32[2,64,512]{2,1,0:T(8,128)S(1)} %get-tuple-element.55), channel_id=1, source_target_pairs={{0,1},{1,0},{2,3},{3,2},{4,5},{5,4},{6,7},{7,6},{8,9},{9,8},{10,11... | collective-permute-start | bytes 786440 | tf_op jit(solution)/shard_map/ppermute | solution.py:401
  43.7 6.8 %collective-permute-start.23 = (f32[2,64,512]{2,1,0:T(8,128)S(1)}, f32[2,64,512]{2,1,0:T(8,128)S(1)}, u32[]{:S(2)}, u32[]{:S(2)}) collective-permute-start(f32[2,64,512]{2,1,0:T(8,128)S(1)} %get-tuple-element.70), channel_id=1, source_target_pairs={{0,1},{1,0},{2,3},{3,2},{4,5},{5,4},{6,7},{7,6},{8,9},{9,8},{10,11... | collective-permute-start | bytes 786440 | tf_op jit(solution)/shard_map/ppermute | solution.py:401
  46.1 7.1 %collective-permute-start.10 = (f32[2,64,128]{2,1,0:T(8,128)S(1)}, f32[2,64,128]{2,1,0:T(8,128)S(1)}, u32[]{:S(2)}, u32[]{:S(2)}) collective-permute-start(f32[2,64,128]{2,1,0:T(8,128)S(1)} %get-tuple-element.57), channel_id=1, source_target_pairs={{0,2},{1,3},{2,0},{3,1},{4,6},{5,7},{6,4},{7,5},{8,10},{9,11},{10,... | collective-permute-start | bytes 196616 | tf_op jit(solution)/shard_map/ppermute | solution.py:397
  46.2 10.0 %collective-permute-start.11 = (f32[2,64,128]{2,1,0:T(8,128)S(1)}, f32[2,64,128]{2,1,0:T(8,128)S(1)}, u32[]{:S(2)}, u32[]{:S(2)}) collective-permute-start(f32[2,64,128]{2,1,0:T(8,128)S(1)} %get-tuple-element.58), channel_id=1, source_target_pairs={{0,4},{1,5},{2,6},{3,7},{4,0},{5,1},{6,2},{7,3},{8,12},{9,13},{10,... | collective-permute-start | bytes 196616 | tf_op jit(solution)/shard_map/ppermute | solution.py:397
  47.5 8.7 %collective-permute-start.12 = (f32[2,64,128]{2,1,0:T(8,128)S(1)}, f32[2,64,128]{2,1,0:T(8,128)S(1)}, u32[]{:S(2)}, u32[]{:S(2)}) collective-permute-start(f32[2,64,128]{2,1,0:T(8,128)S(1)} %get-tuple-element.59), channel_id=1, source_target_pairs={{0,6},{1,7},{2,4},{3,5},{4,2},{5,3},{6,0},{7,1},{8,14},{9,15},{10,... | collective-permute-start | bytes 196616 | tf_op jit(solution)/shard_map/ppermute | solution.py:397
  51.7 5.8 %collective-permute-start.24 = (f32[2,64,128]{2,1,0:T(8,128)S(1)}, f32[2,64,128]{2,1,0:T(8,128)S(1)}, u32[]{:S(2)}, u32[]{:S(2)}) collective-permute-start(f32[2,64,128]{2,1,0:T(8,128)S(1)} %get-tuple-element.72), channel_id=1, source_target_pairs={{0,2},{1,3},{2,0},{3,1},{4,6},{5,7},{6,4},{7,5},{8,10},{9,11},{10,... | collective-permute-start | bytes 196616 | tf_op jit(solution)/shard_map/ppermute | solution.py:397
  51.8 8.7 %collective-permute-start.25 = (f32[2,64,128]{2,1,0:T(8,128)S(1)}, f32[2,64,128]{2,1,0:T(8,128)S(1)}, u32[]{:S(2)}, u32[]{:S(2)}) collective-permute-start(f32[2,64,128]{2,1,0:T(8,128)S(1)} %get-tuple-element.73), channel_id=1, source_target_pairs={{0,4},{1,5},{2,6},{3,7},{4,0},{5,1},{6,2},{7,3},{8,12},{9,13},{10,... | collective-permute-start | bytes 196616 | tf_op jit(solution)/shard_map/ppermute | solution.py:397
  53.2 7.3 %collective-permute-start.26 = (f32[2,64,128]{2,1,0:T(8,128)S(1)}, f32[2,64,128]{2,1,0:T(8,128)S(1)}, u32[]{:S(2)}, u32[]{:S(2)}) collective-permute-start(f32[2,64,128]{2,1,0:T(8,128)S(1)} %get-tuple-element.74), channel_id=1, source_target_pairs={{0,6},{1,7},{2,4},{3,5},{4,2},{5,3},{6,0},{7,1},{8,14},{9,15},{10,... | collective-permute-start | bytes 196616 | tf_op jit(solution)/shard_map/ppermute | solution.py:397
  61.9 9.2 %collective-permute-start.15 = (f32[2,64,512]{2,1,0:T(8,128)S(1)}, f32[2,64,512]{2,1,0:T(8,128)S(1)}, u32[]{:S(2)}, u32[]{:S(2)}) collective-permute-start(f32[2,64,512]{2,1,0:T(8,128)S(1)} %add.161.refs_0_), channel_id=1, source_target_pairs={{0,16},{8,24},{16,0},{24,8},{1,17},{9,25},{17,1},{25,9},{2,18},{10... | collective-permute-start | bytes 786440 | tf_op jit(solution)/shard_map/ppermute | solution.py:389
  63.5 9.2 %collective-permute-start.14 = (f32[2,64,512]{2,1,0:T(8,128)S(1)}, f32[2,64,512]{2,1,0:T(8,128)S(1)}, u32[]{:S(2)}, u32[]{:S(2)}) collective-permute-start(f32[2,64,512]{2,1,0:T(8,128)S(1)} %add.161.refs_0_), channel_id=1, source_target_pairs={{0,8},{8,0},{16,24},{24,16},{1,9},{9,1},{17,25},{25,17},{2,10},{10... | collective-permute-start | bytes 786440 | tf_op jit(solution)/shard_map/ppermute | solution.py:389
  65.0 9.1 %collective-permute-start.31 = (f32[64,512]{1,0:T(8,128)S(1)}, f32[64,512]{1,0:T(8,128)S(1)}, u32[]{:S(2)}, u32[]{:S(2)}) collective-permute-start(f32[64,512]{1,0:T(8,128)S(1)} %get-tuple-element.79), channel_id=1, source_target_pairs={{0,16},{8,24},{16,0},{24,8},{1,17},{9,25},{17,1},{25,9},{2,18},{10... | collective-permute-start | bytes 393224 | tf_op jit(solution)/shard_map/ppermute | solution.py:389
  65.6 9.8 %collective-permute-start.29 = (f32[64,512]{1,0:T(8,128)S(1)}, f32[64,512]{1,0:T(8,128)S(1)}, u32[]{:S(2)}, u32[]{:S(2)}) collective-permute-start(f32[64,512]{1,0:T(8,128)S(1)} %get-tuple-element.79), channel_id=1, source_target_pairs={{0,8},{8,0},{16,24},{24,16},{1,9},{9,1},{17,25},{25,17},{2,10},{10... | collective-permute-start | bytes 393224 | tf_op jit(solution)/shard_map/ppermute | solution.py:389
  66.5 12.5 %collective-permute-start.30 = (f32[64,512]{1,0:T(8,128)S(1)}, f32[64,512]{1,0:T(8,128)S(1)}, u32[]{:S(2)}, u32[]{:S(2)}) collective-permute-start(f32[64,512]{1,0:T(8,128)S(1)} %get-tuple-element.80), channel_id=1, source_target_pairs={{0,16},{8,24},{16,0},{24,8},{1,17},{9,25},{17,1},{25,9},{2,18},{10... | collective-permute-start | bytes 393224 | tf_op jit(solution)/shard_map/ppermute | solution.py:389
  71.1 7.1 %collective-permute-start.28 = (f32[64,512]{1,0:T(8,128)S(1)}, f32[64,512]{1,0:T(8,128)S(1)}, u32[]{:S(2)}, u32[]{:S(2)}) collective-permute-start(f32[64,512]{1,0:T(8,128)S(1)} %get-tuple-element.80), channel_id=1, source_target_pairs={{0,8},{8,0},{16,24},{24,16},{1,9},{9,1},{17,25},{25,17},{2,10},{10... | collective-permute-start | bytes 393224 | tf_op jit(solution)/shard_map/ppermute | solution.py:389
  72.6 8.4 %collective-permute-start.17 = (f32[64,512]{1,0:T(8,128)S(1)}, f32[64,512]{1,0:T(8,128)S(1)}, u32[]{:S(2)}, u32[]{:S(2)}) collective-permute-start(f32[64,512]{1,0:T(8,128)S(1)} %slice_bitcast_fusion.2), channel_id=1, source_target_pairs={{0,8},{8,0},{16,24},{24,16},{1,9},{9,1},{17,25},{25,17},{2,10},{10... | collective-permute-start | bytes 393224 | tf_op jit(solution)/shard_map/ppermute | solution.py:389
  74.2 6.9 %collective-permute-start.16 = (f32[64,512]{1,0:T(8,128)S(1)}, f32[64,512]{1,0:T(8,128)S(1)}, u32[]{:S(2)}, u32[]{:S(2)}) collective-permute-start(f32[64,512]{1,0:T(8,128)S(1)} %slice_bitcast_fusion.3), channel_id=1, source_target_pairs={{0,16},{8,24},{16,0},{24,8},{1,17},{9,25},{17,1},{25,9},{2,18},{10... | collective-permute-start | bytes 393224 | tf_op jit(solution)/shard_map/ppermute | solution.py:389
  75.5 8.5 %collective-permute-start.33 = (f32[64,512]{1,0:T(8,128)S(1)}, f32[64,512]{1,0:T(8,128)S(1)}, u32[]{:S(2)}, u32[]{:S(2)}) collective-permute-start(f32[64,512]{1,0:T(8,128)S(1)} %collective-permute-done.31.refs_9_), channel_id=1, source_target_pairs={{0,8},{8,0},{16,24},{24,16},{1,9},{9,1},{17,25},{25,17},{2,10},{10... | collective-permute-start | bytes 393224 | tf_op jit(solution)/shard_map/ppermute | solution.py:389
  78.3 5.7 %collective-permute-start.32 = (f32[64,512]{1,0:T(8,128)S(1)}, f32[64,512]{1,0:T(8,128)S(1)}, u32[]{:S(2)}, u32[]{:S(2)}) collective-permute-start(f32[64,512]{1,0:T(8,128)S(1)} %collective-permute-done.28.refs_6_), channel_id=1, source_target_pairs={{0,16},{8,24},{16,0},{24,8},{1,17},{9,25},{17,1},{25,9},{2,18},{10... | collective-permute-start | bytes 393224 | tf_op jit(solution)/shard_map/ppermute | solution.py:389
  (7 other events, 64.2 us)

commit v2 on v1

--- a/solution.py
+++ b/solution.py
@@ -13,7 +13,7 @@
 N_IMG = 65536
 FACET_LEN = 5120
 LANES = 128
-CHIP, CORE, FACET = range(3)
+SLOW, FAST = range(2)
 
 
 def mod_product(left, right):
@@ -48,7 +48,9 @@
     def dot(left, right):
         return jnp.dot(left, right, preferred_element_type=jnp.float32)
 
-    return dot(high, high_table) + (dot(low, high_table) + dot(high, low_table))
+    rows = values.shape[0]
+    both = dot(jnp.concatenate([high, low], axis=0), high_table)
+    return both[:rows] + (both[rows:] + dot(high, low_table))
 
 
 def rotate(values, high_table, low_table, sign):
@@ -58,6 +60,11 @@
     real = both[:rows, :length] - sign * both[rows:, length:]
     imag = both[rows:, :length] + sign * both[:rows, length:]
     return real, imag
+
+
+def chip_and_core():
+    team = lax.axis_index("team")
+    return lax.div(team, 2), lax.rem(team, 2)
 
 
 def lane_block(index):
@@ -139,7 +146,7 @@
 
 
 def corner_window_kernel(
-    per_facet, spots, info, offsets_hbm, facet_offsets_hbm, taper_hbm, columns, *refs
+    per_facet, near, keys, offsets_hbm, facet_offsets_hbm, taper_hbm, columns, *refs
 ):
     factor, planes = refs[0], refs[1:-6]
     buffer, sems, offsets, facet_offsets, taper, small_sems = refs[-6:]
@@ -160,16 +167,16 @@
     def prepare():
         small[1].wait()
         small[2].wait()
-        phase_factor(offsets, facet_offsets[info[FACET]], taper[...], factor)
-
-    ids = [info[spot] for spot in spots]
+        phase_factor(offsets, facet_offsets[lax.axis_index("facet")], taper[...], factor)
+
+    ids = [near(*key) for key in keys]
     cut_windows(offsets, ids, columns, outs, buffer, sems, prepare, factor)
 
 
-def window_kernel(layout, spots, info, offsets, columns, factor, *refs):
+def window_kernel(layout, near, keys, offsets, columns, factor, *refs):
     planes, (buffer, sems) = refs[:-2], refs[-2:]
     outs = pairs_of(layout, planes)
-    ids = [info[spot] for spot in spots]
+    ids = [near(*key) for key in keys]
     cut_windows(offsets, ids, columns, outs, buffer, sems, lambda: None, factor)
 
 
@@ -201,12 +208,13 @@
         lax.fori_loop(0, rows, step, 0, unroll=8)
 
 
-def split_out(values, chip, outs):
+def split_out(values, outs):
+    chip, _ = chip_and_core()
     for distance, out in enumerate(outs):
         out[...] = values[:, :, lane_block(jnp.bitwise_xor(chip, distance))]
 
 
-def first_kernel(layout, info, table, *refs):
+def first_kernel(layout, table, *refs):
     scratch = refs[-1]
     chips = scratch.shape[2] // LANES
     terms, outs = refs[: -1 - chips], refs[-1 - chips : -1]
@@ -220,12 +228,12 @@
     real, imag = rotate(jnp.concatenate(sums, axis=0), table[0], table[1], -1.0)
     scratch[0] = real
     scratch[1] = imag
-    split_out(scratch, info[CHIP], outs)
-
-
-def cross_kernel(sign, info, table, *refs):
+    split_out(scratch, outs)
+
+
+def cross_kernel(sign, table, *refs):
     blocks, (keep, send, gathered, partial) = refs[:-4], refs[-4:]
-    chip, core = info[CHIP], info[CORE]
+    chip, core = chip_and_core()
     rows = blocks[0].shape[1]
     for distance, block in enumerate(blocks):
         spot = pl.ds(pl.multiple_of(jnp.bitwise_xor(chip, distance) * rows, rows), rows)
@@ -249,7 +257,7 @@
     send[...] = partial[:, other, :]
 
 
-def correct_kernel(chunk, info, table, keep, received, residuals, chosens, *refs):
+def correct_kernel(chunk, table, keep, received, residuals, chosens, *refs):
     outs, scratch = refs[:-1], refs[-1]
     residual, chosen = residuals.at[chunk], chosens.at[chunk]
     spectrum_real = keep[0] + received[0]
@@ -260,7 +268,7 @@
     real, imag = rotate(values, table[0], table[1], 1.0)
     scratch[0] = real
     scratch[1] = imag
-    split_out(scratch, info[CHIP], outs)
+    split_out(scratch, outs)
 
 
 def turned_pieces(offset, factor, real_ref, imag_ref):
@@ -288,10 +296,10 @@
     return lax.div(begin, LANES), pieces
 
 
-def update_kernel(layout, spots, info, offsets, factor, *refs):
+def update_kernel(layout, near, keys, offsets, factor, *refs):
     arrays, (out, window) = refs[:-2], refs[-2:]
     pairs = pairs_of(layout, arrays)
-    ids = [info[spot] for spot in spots]
+    ids = [near(*key) for key in keys]
     count = len(pairs)
     total = out.shape[3] // LANES
     out[...] = jnp.zeros(out.shape, jnp.float32)
@@ -309,9 +317,9 @@
         window[:, :, pl.ds(piece * LANES, LANES)] = out[0, :, :, spot]
 
 
-def finish_kernel(spot, info, offsets, factor, window, real, imag, whole, out, buffer, sems):
+def finish_kernel(near, key, offsets, factor, window, real, imag, whole, out, buffer, sems):
     total = out.shape[3] // LANES
-    item = info[spot]
+    item = near(*key)
     block, pieces = turned_pieces(offsets[item], factor.at[item], real, imag)
 
     def copy(piece):
@@ -369,13 +377,12 @@
     per_facet = residual.shape[0]
     subgrids = grid_offsets.shape[0]
     slow, fast = grid_of(facet_count)
-    facet = lax.axis_index("facet")
-    team = lax.axis_index("team")
     table = jnp.asarray(split_table(length))
-    down, right = facet // fast, facet % fast
 
     def near(step, chunk):
-        to = (down + step[0]) % slow * fast + (right + step[1]) % fast
+        facet = lax.axis_index("facet")
+        down, right = lax.div(facet, fast), lax.rem(facet, fast)
+        to = lax.rem(down + step[0] % slow, slow) * fast + lax.rem(right + step[1] % fast, fast)
         return to * per_facet + chunk
 
     def move(value, step_slow, step_fast):
@@ -418,21 +425,13 @@
     last = per_facet - 1
     corner_keys = [(step, chunk) for step in corner_steps for chunk in chunks]
     near_keys = [(step, chunk) for chunk in chunks for step in [(0, 0)] + near_steps]
-    gather_keys = [
-        ((-i, -j), chunk) for chunk in chunks for i, j in [(0, 0)] + near_steps + corner_steps
-    ]
-    spots, numbers = {}, [team // 2, team % 2, facet]
-    for key in corner_keys + near_keys + gather_keys:
-        spots[key] = len(numbers)
-        numbers.append(near(*key))
-    info = jnp.stack(numbers).astype(jnp.int32)
 
     def in_hbm(value):
         return pltpu.with_memory_space_constraint(value, pltpu.HBM)
 
     columns = in_hbm(facets)
     factor, *planes = call(
-        functools.partial(corner_window_kernel, per_facet, [spots[key] for key in corner_keys]),
+        functools.partial(corner_window_kernel, per_facet, near, corner_keys),
         [(subgrids, 2, length)] + [(per_facet, rows, length)] * (2 * len(corner_steps)),
         window_scratch(len(corner_keys))
         + [
@@ -441,11 +440,10 @@
             pltpu.VMEM((1, length), jnp.float32),
             pltpu.SemaphoreType.DMA((3,)),
         ],
-        [SMEM, HBM, HBM, HBM, HBM],
+        [HBM, HBM, HBM, HBM],
         8 * MIB,
         matmul_cost // 8,
     )(
-        info,
         in_hbm(grid_offsets),
         in_hbm(facet_offsets),
         in_hbm(taper.reshape(1, length)),
@@ -458,13 +456,13 @@
 
     near_layout = [2 if chunk == 0 and step != (0, 0) else 1 for step, chunk in near_keys]
     outs = call(
-        functools.partial(window_kernel, near_layout, [spots[key] for key in near_keys]),
+        functools.partial(window_kernel, near_layout, near, near_keys),
         [shape for count in near_layout for shape in ([block_shape], [plane] * 2)[count - 1]],
         window_scratch(len(near_keys)),
-        [SMEM, SMEM, HBM, VMEM],
+        [SMEM, HBM, VMEM],
         12 * MIB,
         matmul_cost // 4,
-    )(info, grid_offsets, columns, factor)
+    )(grid_offsets, columns, factor)
     terms = {}
     for key, count in zip(near_keys, near_layout):
         terms[key], outs = tuple(outs[:count]), outs[count:]
@@ -489,13 +487,13 @@
     def scatter(chunk):
         received = [terms[(0, 0), chunk]]
         for i, j in near_steps:
-            axis = "slow" if i else "fast"
+            axis = SLOW if i else FAST
             part = 0 if i else 1
             if i:
                 corners = [by_fast[i, j] for j in fast_steps]
             else:
                 corners = [by_slow[i, j] for i in slow_steps]
-            i, j = (i, 0) if axis == "slow" else (0, j)
+            i, j = (i, 0) if axis == SLOW else (0, j)
             term = terms[(i, j), chunk]
             if len(term) == 1:
                 joined = join(term[0], corners, part, chunk)
@@ -513,10 +511,10 @@
             functools.partial(first_kernel, [len(item) for item in received]),
             [piece_shape] * chips,
             [pltpu.VMEM(block_shape, jnp.float32)],
-            [SMEM, VMEM] + [VMEM] * len(arrays),
+            [VMEM] + [VMEM] * len(arrays),
             8 * MIB,
             matmul_cost,
-        )(info, table, *arrays)
+        )(table, *arrays)
 
     def cross(pieces, sign):
         return call(
@@ -526,20 +524,20 @@
                 pltpu.VMEM((2, chips * rows, LANES), jnp.float32),
                 pltpu.VMEM((2, LANES, length), jnp.float32),
             ],
-            [SMEM, VMEM] + [VMEM] * chips,
+            [VMEM] + [VMEM] * chips,
             8 * MIB,
             matmul_cost,
-        )(info, table, *pieces)
+        )(table, *pieces)
 
     def correct(keep, received, chunk):
         return call(
             functools.partial(correct_kernel, chunk),
             [piece_shape] * chips,
             [pltpu.VMEM(block_shape, jnp.float32)],
-            [SMEM] + [VMEM] * 5,
+            [VMEM] * 5,
             8 * MIB,
             matmul_cost,
-        )(info, table, keep, received, residual, chosen)
+        )(table, keep, received, residual, chosen)
 
     def gather(own, chunk):
         found = {(0, 0): (own,)}
@@ -572,33 +570,33 @@
         keep, sent = halves[chunk]
         own = keep + swap(sent)
         for (i, j), found in gather(own, chunk).items():
-            keys.append(spots[(-i, -j), chunk])
+            keys.append(((-i, -j), chunk))
             items.append(found)
     *first_items, last_item = items
     if len(last_item) == 1:
         last_item = (last_item[0][0], last_item[0][1])
     arrays = [array for item in first_items for array in item]
     whole, window = call(
-        functools.partial(update_kernel, [len(item) for item in first_items], keys),
+        functools.partial(update_kernel, [len(item) for item in first_items], near, keys),
         [(1, 2, rows, facet_len), (2, rows, length + LANES)],
         [],
-        [SMEM, SMEM, VMEM] + [VMEM] * len(arrays),
+        [SMEM, VMEM] + [VMEM] * len(arrays),
         16 * MIB,
         matmul_cost,
-    )(info, grid_offsets, factor, *arrays)
+    )(grid_offsets, factor, *arrays)
     (update,) = call(
-        functools.partial(finish_kernel, keys[-1]),
+        functools.partial(finish_kernel, near, keys[-1]),
         [(1, 2, rows, facet_len)],
         [
             pltpu.VMEM((blocks + 1, 2, rows, LANES), jnp.float32),
             pltpu.SemaphoreType.DMA((blocks + 1,)),
         ],
-        [SMEM, SMEM, VMEM, VMEM, VMEM, VMEM, HBM],
+        [SMEM, VMEM, VMEM, VMEM, VMEM, HBM],
         8 * MIB,
         matmul_cost // 8,
         out_specs=[HBM],
-        input_output_aliases={6: 0},
-    )(info, grid_offsets, factor, window, *last_item, whole)
+        input_output_aliases={5: 0},
+    )(grid_offsets, factor, window, *last_item, whole)
     return update
 
 

time: 85.5 us -> 82.3 us (0.963)
  Pallas kernels: 21 us -> 16.2 us
  waiting for transfers between devices: 21.5 us -> 23.1 us
    pallas_call x4, Pallas kernels: 4.91 us -> 2.79 us  [cross(): call(functools.partial(cross_kernel, sign), [block_shape] * 2, [pltpu.VME...]
    ppermute x12, waiting for transfers between devices: 7.48 us -> 9.1 us  [exchange(): out[distance] = lax.ppermute(pieces[distance], 'team', pairs)]
    pallas_call x2, Pallas kernels: 2.4 us -> 1.29 us  [correct(): call(functools.partial(correct_kernel, chunk), [piece_shape] * chips, [pl...]
    pallas_call x2, Pallas kernels: 2.33 us -> 1.23 us  [first_transform(): call(functools.partial(first_kernel, [len(item) for item in received]), [...]
  transfers between devices with their start and end apart: 34 -> 34, of which waited for: 10 -> 10; matrix products, arithmetic and copies ran while one was open for 0% -> 0% of each run, Pallas kernels for 20% -> 15%
where the time goes in v2:
time: 82.3 us; the launch traced here: 82.1 us
  starting transfers between devices  42.3 us (51%)
  waiting for transfers between devices  23.1 us (28%)
  Pallas kernels  16.2 us (20%)
    ppermute x18, starting transfers between devices, move(): return lax.ppermute(value, 'facet', pairs)  24.3 us
    ppermute x12, starting transfers between devices, exchange(): out[distance] = lax.ppermute(pieces[distance], 'team', pairs)  17.8 us
    ppermute x18, waiting for transfers between devices, move(): return lax.ppermute(value, 'facet', pairs)  14 us
    ppermute x12, waiting for transfers between devices, exchange(): out[distance] = lax.ppermute(pieces[distance], 'team', pairs)  9.1 us
    pallas_call x1, Pallas kernels, tiled_device(): call(functools.partial(window_kernel, near_layout, near, near_keys), [sha...  3.21 us
    pallas_call x1, Pallas kernels, tiled_device(): call(functools.partial(update_kernel, [len(item) for item in first_items]...  2.84 us
    pallas_call x4, Pallas kernels, cross(): call(functools.partial(cross_kernel, sign), [block_shape] * 2, [pltpu.VME...  2.79 us
    pallas_call x1, Pallas kernels, tiled_device(): call(functools.partial(corner_window_kernel, per_facet, near, corner_keys...  2.36 us
  transfers between devices with their start and end apart: 34, of which 10 were waited for; matrix products, arithmetic and copies ran while one was open for 0% of the time, Pallas kernels for 15%

profile of v2, /device:TPU:0, one launch (start us, length us, event | category | flops | bytes accessed | tf_op | source)
XLA Modules:
  0.0 82.1 jit_solution(2253632267057497041)
XLA Ops:
  0.0 2.4 %shard_map.82 = (f32[8,2,512]{2,1,0:T(2,128)S(1)}, f32[2,64,512]{2,1,0:T(8,128)S(1)}, f32[2,64,512]{2,1,0:T(8,128)S(1)}) custom-call(s32[8]{0:T(128)} %offsets.5, s32[4]{0:T(128)} %facet_offsets_hbm.1, f32[1,512]{1,0:T(1,128)} %bitcast.9, f32[1,2,64,5120]{3,2,1,0:T(8,128)} %columns.3), custom_call_target="tpu_custom_call" | custom-call | flops 50331648 | bytes 786432 | tf_op jit(solution)/shard_map/pallas_call | solution.py:433
  2.4 3.0 %collective-permute-start.3 = (f32[2,64,512]{2,1,0:T(8,128)S(1)}, f32[2,64,512]{2,1,0:T(8,128)S(1)}, u32[]{:S(2)}, u32[]{:S(2)}) collective-permute-start(f32[2,64,512]{2,1,0:T(8,128)S(1)} %get-tuple-element.48), channel_id=1, source_target_pairs={{0,8},{8,0},{16,24},{24,16},{1,9},{9,1},{17,25},{25,17},{2,10},{10... | collective-permute-start | bytes 786440 | tf_op jit(solution)/shard_map/ppermute | solution.py:396
  5.4 1.5 %collective-permute-start.1 = (f32[2,64,512]{2,1,0:T(8,128)S(1)}, f32[2,64,512]{2,1,0:T(8,128)S(1)}, u32[]{:S(2)}, u32[]{:S(2)}) collective-permute-start(f32[2,64,512]{2,1,0:T(8,128)S(1)} %get-tuple-element.46), channel_id=1, source_target_pairs={{0,16},{8,24},{16,0},{24,8},{1,17},{9,25},{17,1},{25,9},{2,18},{10... | collective-permute-start | bytes 786440 | tf_op jit(solution)/shard_map/ppermute | solution.py:396
  6.9 3.2 %shard_map.83 = (f32[2,64,512]{2,1,0:T(8,128)S(1)}, f32[64,512]{1,0:T(8,128)S(1)}, f32[64,512]{1,0:T(8,128)S(1)}, f32[64,512]{1,0:T(8,128)S(1)}, f32[64,512]{1,0...) custom-call(s32[8]{0:T(128)S(1)} %copy-done.3, ...), custom_call_target="tpu_custom_call" | custom-call | flops 100663296 | bytes 1572864 | tf_op jit(solution)/shard_map/pallas_call | solution.py:458
  10.7 1.1 %collective-permute-done.3.refs_0_ = f32[2,64,512]{2,1,0:T(8,128)S(1)} collective-permute-done((f32[2,64,512]{2,1,0:T(8,128)S(1)}, f32[2,64,512]{2,1,0:T(8,128)S(1)}, u32[]{:S(2)}, u32[]{:S(2)}) %collective-permute-start.3) | collective-permute-done | bytes 262176 | tf_op jit(solution)/shard_map/ppermute | solution.py:396
  11.8 2.6 %collective-permute-start.19 = (f32[2,64,512]{2,1,0:T(8,128)S(1)}, f32[2,64,512]{2,1,0:T(8,128)S(1)}, u32[]{:S(2)}, u32[]{:S(2)}) collective-permute-start(f32[2,64,512]{2,1,0:T(8,128)S(1)} %shard_map.92), channel_id=1, source_target_pairs={{0,16},{8,24},{16,0},{24,8},{1,17},{9,25},{17,1},{25,9},{2,18},{10... | collective-permute-start | bytes 786440 | tf_op jit(solution)/shard_map/ppermute | solution.py:396
  14.5 1.8 %collective-permute-start.18 = (f32[2,64,512]{2,1,0:T(8,128)S(1)}, f32[2,64,512]{2,1,0:T(8,128)S(1)}, u32[]{:S(2)}, u32[]{:S(2)}) collective-permute-start(f32[2,64,512]{2,1,0:T(8,128)S(1)} %shard_map.91), channel_id=1, source_target_pairs={{0,8},{8,0},{16,24},{24,16},{1,9},{9,1},{17,25},{25,17},{2,10},{10... | collective-permute-start | bytes 786440 | tf_op jit(solution)/shard_map/ppermute | solution.py:396
  16.5 1.9 %collective-permute-start.4 = (f32[64,512]{1,0:T(8,128)S(1)}, f32[64,512]{1,0:T(8,128)S(1)}, u32[]{:S(2)}, u32[]{:S(2)}) collective-permute-start(f32[64,512]{1,0:T(8,128)S(1)} %shard_map.85), channel_id=1, source_target_pairs={{0,16},{8,24},{16,0},{24,8},{1,17},{9,25},{17,1},{25,9},{2,18},{10... | collective-permute-start | bytes 393224 | tf_op jit(solution)/shard_map/ppermute | solution.py:396
  18.8 4.7 %collective-permute-done.5.refs_4_ = f32[64,512]{1,0:T(8,128)S(1)} collective-permute-done((f32[64,512]{1,0:T(8,128)S(1)}, f32[64,512]{1,0:T(8,128)S(1)}, u32[]{:S(2)}, u32[]{:S(2)}) %collective-permute-start.5) | collective-permute-done | bytes 131104 | tf_op jit(solution)/shard_map/ppermute | solution.py:396
  23.5 1.4 %collective-permute-done.4.refs_3_ = f32[64,512]{1,0:T(8,128)S(1)} collective-permute-done((f32[64,512]{1,0:T(8,128)S(1)}, f32[64,512]{1,0:T(8,128)S(1)}, u32[]{:S(2)}, u32[]{:S(2)}) %collective-permute-start.4) | collective-permute-done | bytes 131104 | tf_op jit(solution)/shard_map/ppermute | solution.py:396
  25.5 1.6 %collective-permute-start.6 = (f32[2,64,128]{2,1,0:T(8,128)S(1)}, f32[2,64,128]{2,1,0:T(8,128)S(1)}, u32[]{:S(2)}, u32[]{:S(2)}) collective-permute-start(f32[2,64,128]{2,1,0:T(8,128)S(1)} %get-tuple-element.51), channel_id=1, source_target_pairs={{0,2},{1,3},{2,0},{3,1},{4,6},{5,7},{6,4},{7,5},{8,10},{9,11},{10,... | collective-permute-start | bytes 196616 | tf_op jit(solution)/shard_map/ppermute | solution.py:404
  27.1 2.6 %collective-permute-start.7 = (f32[2,64,128]{2,1,0:T(8,128)S(1)}, f32[2,64,128]{2,1,0:T(8,128)S(1)}, u32[]{:S(2)}, u32[]{:S(2)}) collective-permute-start(f32[2,64,128]{2,1,0:T(8,128)S(1)} %get-tuple-element.52), channel_id=1, source_target_pairs={{0,4},{1,5},{2,6},{3,7},{4,0},{5,1},{6,2},{7,3},{8,12},{9,13},{10,... | collective-permute-start | bytes 196616 | tf_op jit(solution)/shard_map/ppermute | solution.py:404
  31.3 3.5 %collective-permute-start.21 = (f32[2,64,128]{2,1,0:T(8,128)S(1)}, f32[2,64,128]{2,1,0:T(8,128)S(1)}, u32[]{:S(2)}, u32[]{:S(2)}) collective-permute-start(f32[2,64,128]{2,1,0:T(8,128)S(1)} %get-tuple-element.67), channel_id=1, source_target_pairs={{0,4},{1,5},{2,6},{3,7},{4,0},{5,1},{6,2},{7,3},{8,12},{9,13},{10,... | collective-permute-start | bytes 196616 | tf_op jit(solution)/shard_map/ppermute | solution.py:404
  36.9 2.3 %collective-permute-done.21.refs_2_ = f32[2,64,128]{2,1,0:T(8,128)S(1)} collective-permute-done((f32[2,64,128]{2,1,0:T(8,128)S(1)}, f32[2,64,128]{2,1,0:T(8,128)S(1)}, u32[]{:S(2)}, u32[]{:S(2)}) %collective-permute-start.21) | collective-permute-done | bytes 65568 | tf_op jit(solution)/shard_map/ppermute | solution.py:404
  39.2 1.7 %collective-permute-done.22.refs_3_ = f32[2,64,128]{2,1,0:T(8,128)S(1)} collective-permute-done((f32[2,64,128]{2,1,0:T(8,128)S(1)}, f32[2,64,128]{2,1,0:T(8,128)S(1)}, u32[]{:S(2)}, u32[]{:S(2)}) %collective-permute-start.22) | collective-permute-done | bytes 65568 | tf_op jit(solution)/shard_map/ppermute | solution.py:404
  43.5 1.5 %collective-permute-start.11 = (f32[2,64,128]{2,1,0:T(8,128)S(1)}, f32[2,64,128]{2,1,0:T(8,128)S(1)}, u32[]{:S(2)}, u32[]{:S(2)}) collective-permute-start(f32[2,64,128]{2,1,0:T(8,128)S(1)} %get-tuple-element.58), channel_id=1, source_target_pairs={{0,4},{1,5},{2,6},{3,7},{4,0},{5,1},{6,2},{7,3},{8,12},{9,13},{10,... | collective-permute-start | bytes 196616 | tf_op jit(solution)/shard_map/ppermute | solution.py:404
  44.9 2.9 %collective-permute-start.12 = (f32[2,64,128]{2,1,0:T(8,128)S(1)}, f32[2,64,128]{2,1,0:T(8,128)S(1)}, u32[]{:S(2)}, u32[]{:S(2)}) collective-permute-start(f32[2,64,128]{2,1,0:T(8,128)S(1)} %get-tuple-element.59), channel_id=1, source_target_pairs={{0,6},{1,7},{2,4},{3,5},{4,2},{5,3},{6,0},{7,1},{8,14},{9,15},{10,... | collective-permute-start | bytes 196616 | tf_op jit(solution)/shard_map/ppermute | solution.py:404
  48.6 1.5 %collective-permute-start.25 = (f32[2,64,128]{2,1,0:T(8,128)S(1)}, f32[2,64,128]{2,1,0:T(8,128)S(1)}, u32[]{:S(2)}, u32[]{:S(2)}) collective-permute-start(f32[2,64,128]{2,1,0:T(8,128)S(1)} %get-tuple-element.73), channel_id=1, source_target_pairs={{0,4},{1,5},{2,6},{3,7},{4,0},{5,1},{6,2},{7,3},{8,12},{9,13},{10,... | collective-permute-start | bytes 196616 | tf_op jit(solution)/shard_map/ppermute | solution.py:404
  50.1 2.9 %collective-permute-start.26 = (f32[2,64,128]{2,1,0:T(8,128)S(1)}, f32[2,64,128]{2,1,0:T(8,128)S(1)}, u32[]{:S(2)}, u32[]{:S(2)}) collective-permute-start(f32[2,64,128]{2,1,0:T(8,128)S(1)} %get-tuple-element.74), channel_id=1, source_target_pairs={{0,6},{1,7},{2,4},{3,5},{4,2},{5,3},{6,0},{7,1},{8,14},{9,15},{10,... | collective-permute-start | bytes 196616 | tf_op jit(solution)/shard_map/ppermute | solution.py:404
  53.8 4.1 %collective-permute-done.25.refs_2_ = f32[2,64,128]{2,1,0:T(8,128)S(1)} collective-permute-done((f32[2,64,128]{2,1,0:T(8,128)S(1)}, f32[2,64,128]{2,1,0:T(8,128)S(1)}, u32[]{:S(2)}, u32[]{:S(2)}) %collective-permute-start.25) | collective-permute-done | bytes 65568 | tf_op jit(solution)/shard_map/ppermute | solution.py:404
  58.7 1.6 %collective-permute-start.15 = (f32[2,64,512]{2,1,0:T(8,128)S(1)}, f32[2,64,512]{2,1,0:T(8,128)S(1)}, u32[]{:S(2)}, u32[]{:S(2)}) collective-permute-start(f32[2,64,512]{2,1,0:T(8,128)S(1)} %add.6.refs_0_), channel_id=1, source_target_pairs={{0,16},{8,24},{16,0},{24,8},{1,17},{9,25},{17,1},{25,9},{2,18},{10... | collective-permute-start | bytes 786440 | tf_op jit(solution)/shard_map/ppermute | solution.py:396
  60.3 1.5 %collective-permute-start.14 = (f32[2,64,512]{2,1,0:T(8,128)S(1)}, f32[2,64,512]{2,1,0:T(8,128)S(1)}, u32[]{:S(2)}, u32[]{:S(2)}) collective-permute-start(f32[2,64,512]{2,1,0:T(8,128)S(1)} %add.6.refs_0_), channel_id=1, source_target_pairs={{0,8},{8,0},{16,24},{24,16},{1,9},{9,1},{17,25},{25,17},{2,10},{10... | collective-permute-start | bytes 786440 | tf_op jit(solution)/shard_map/ppermute | solution.py:396
  63.3 1.2 %collective-permute-start.30 = (f32[64,512]{1,0:T(8,128)S(1)}, f32[64,512]{1,0:T(8,128)S(1)}, u32[]{:S(2)}, u32[]{:S(2)}) collective-permute-start(f32[64,512]{1,0:T(8,128)S(1)} %get-tuple-element.80), channel_id=1, source_target_pairs={{0,16},{8,24},{16,0},{24,8},{1,17},{9,25},{17,1},{25,9},{2,18},{10... | collective-permute-start | bytes 393224 | tf_op jit(solution)/shard_map/ppermute | solution.py:396
  64.5 3.5 %collective-permute-done.15.refs_2_ = f32[2,64,512]{2,1,0:T(8,128)S(1)} collective-permute-done((f32[2,64,512]{2,1,0:T(8,128)S(1)}, f32[2,64,512]{2,1,0:T(8,128)S(1)}, u32[]{:S(2)}, u32[]{:S(2)}) %collective-permute-start.15) | collective-permute-done | bytes 262176 | tf_op jit(solution)/shard_map/ppermute | solution.py:396
  67.9 1.5 %collective-permute-start.28 = (f32[64,512]{1,0:T(8,128)S(1)}, f32[64,512]{1,0:T(8,128)S(1)}, u32[]{:S(2)}, u32[]{:S(2)}) collective-permute-start(f32[64,512]{1,0:T(8,128)S(1)} %get-tuple-element.80), channel_id=1, source_target_pairs={{0,8},{8,0},{16,24},{24,16},{1,9},{9,1},{17,25},{25,17},{2,10},{10... | collective-permute-start | bytes 393224 | tf_op jit(solution)/shard_map/ppermute | solution.py:396
  69.4 1.5 %collective-permute-start.17 = (f32[64,512]{1,0:T(8,128)S(1)}, f32[64,512]{1,0:T(8,128)S(1)}, u32[]{:S(2)}, u32[]{:S(2)}) collective-permute-start(f32[64,512]{1,0:T(8,128)S(1)} %slice_bitcast_fusion.2), channel_id=1, source_target_pairs={{0,8},{8,0},{16,24},{24,16},{1,9},{9,1},{17,25},{25,17},{2,10},{10... | collective-permute-start | bytes 393224 | tf_op jit(solution)/shard_map/ppermute | solution.py:396
  71.0 1.3 %collective-permute-start.16 = (f32[64,512]{1,0:T(8,128)S(1)}, f32[64,512]{1,0:T(8,128)S(1)}, u32[]{:S(2)}, u32[]{:S(2)}) collective-permute-start(f32[64,512]{1,0:T(8,128)S(1)} %slice_bitcast_fusion.3), channel_id=1, source_target_pairs={{0,16},{8,24},{16,0},{24,8},{1,17},{9,25},{17,1},{25,9},{2,18},{10... | collective-permute-start | bytes 393224 | tf_op jit(solution)/shard_map/ppermute | solution.py:396
  72.3 1.5 %collective-permute-start.33 = (f32[64,512]{1,0:T(8,128)S(1)}, f32[64,512]{1,0:T(8,128)S(1)}, u32[]{:S(2)}, u32[]{:S(2)}) collective-permute-start(f32[64,512]{1,0:T(8,128)S(1)} %collective-permute-done.31.refs_9_), channel_id=1, source_target_pairs={{0,8},{8,0},{16,24},{24,16},{1,9},{9,1},{17,25},{25,17},{2,10},{10... | collective-permute-start | bytes 393224 | tf_op jit(solution)/shard_map/ppermute | solution.py:396
  73.7 1.3 %collective-permute-done.28.refs_6_ = f32[64,512]{1,0:T(8,128)S(1)} collective-permute-done((f32[64,512]{1,0:T(8,128)S(1)}, f32[64,512]{1,0:T(8,128)S(1)}, u32[]{:S(2)}, u32[]{:S(2)}) %collective-permute-start.28) | collective-permute-done | bytes 131104 | tf_op jit(solution)/shard_map/ppermute | solution.py:396
  75.8 2.1 %collective-permute-done.17.refs_4_ = f32[64,512]{1,0:T(8,128)S(1)} collective-permute-done((f32[64,512]{1,0:T(8,128)S(1)}, f32[64,512]{1,0:T(8,128)S(1)}, u32[]{:S(2)}, u32[]{:S(2)}) %collective-permute-start.17) | collective-permute-done | bytes 131104 | tf_op jit(solution)/shard_map/ppermute | solution.py:396
  77.9 2.8 %shard_map.97 = (f32[1,2,64,5120]{3,2,1,0:T(8,128)}, f32[2,64,640]{2,1,0:T(8,128)S(1)}) custom-call(s32[8]{0:T(128)S(1)} %copy-done.3, f32[8,2,512]{2,1,0:T(2,128)S(1)} %get-tuple-element.42.factor, f32[2,64,512]{2,1,0:T(8,128)S(1)} %add.6.refs_0_, f32[2,64,512]{2,1,0:T(8,128)S(1)} %collective-permute-done.14.refs_1_, ...), custom_call_target="tpu_custom_call" | custom-call | flops 402653184 | bytes 6291456 | tf_op jit(solution)/shard_map/pallas_call | solution.py:579
  80.7 1.4 %shard_map.98 = f32[1,2,64,5120]{3,2,1,0:T(8,128)} custom-call(s32[8]{0:T(128)S(1)} %copy-done.3, f32[8,2,512]{2,1,0:T(2,128)S(1)} %get-tuple-element.42.factor, f32[2,64,640]{2,1,0:T(8,128)S(1)} %get-tuple-element.77.window, f32[64,512]{1,0:T(8,128)S(1)} %collective-permute-done.32.real, ...), custom_call_target="tpu_custom_call", output_to_operand_aliasing={{}: (5, {})} | custom-call | flops 50331648 | bytes 786432 | tf_op jit(solution)/shard_map/pallas_call | solution.py:587
  (68 shorter events, 12.7 us)
Async XLA Ops:
  2.4 9.4 %collective-permute-start.3 = (f32[2,64,512]{2,1,0:T(8,128)S(1)}, f32[2,64,512]{2,1,0:T(8,128)S(1)}, u32[]{:S(2)}, u32[]{:S(2)}) collective-permute-start(f32[2,64,512]{2,1,0:T(8,128)S(1)} %get-tuple-element.48), channel_id=1, source_target_pairs={{0,8},{8,0},{16,24},{24,16},{1,9},{9,1},{17,25},{25,17},{2,10},{10... | collective-permute-start | bytes 786440 | tf_op jit(solution)/shard_map/ppermute | solution.py:396
  5.4 9.1 %collective-permute-start.1 = (f32[2,64,512]{2,1,0:T(8,128)S(1)}, f32[2,64,512]{2,1,0:T(8,128)S(1)}, u32[]{:S(2)}, u32[]{:S(2)}) collective-permute-start(f32[2,64,512]{2,1,0:T(8,128)S(1)} %get-tuple-element.46), channel_id=1, source_target_pairs={{0,16},{8,24},{16,0},{24,8},{1,17},{9,25},{17,1},{25,9},{2,18},{10... | collective-permute-start | bytes 786440 | tf_op jit(solution)/shard_map/ppermute | solution.py:396
  10.1 8.3 %collective-permute-start = (f32[64,512]{1,0:T(8,128)S(1)}, f32[64,512]{1,0:T(8,128)S(1)}, u32[]{:S(2)}, u32[]{:S(2)}) collective-permute-start(f32[64,512]{1,0:T(8,128)S(1)} %get-tuple-element.44), channel_id=1, source_target_pairs={{0,8},{8,0},{16,24},{24,16},{1,9},{9,1},{17,25},{25,17},{2,10},{10... | collective-permute-start | bytes 393224 | tf_op jit(solution)/shard_map/ppermute | solution.py:396
  11.8 18.2 %collective-permute-start.19 = (f32[2,64,512]{2,1,0:T(8,128)S(1)}, f32[2,64,512]{2,1,0:T(8,128)S(1)}, u32[]{:S(2)}, u32[]{:S(2)}) collective-permute-start(f32[2,64,512]{2,1,0:T(8,128)S(1)} %shard_map.92), channel_id=1, source_target_pairs={{0,16},{8,24},{16,0},{24,8},{1,17},{9,25},{17,1},{25,9},{2,18},{10... | collective-permute-start | bytes 786440 | tf_op jit(solution)/shard_map/ppermute | solution.py:396
  14.5 15.5 %collective-permute-start.18 = (f32[2,64,512]{2,1,0:T(8,128)S(1)}, f32[2,64,512]{2,1,0:T(8,128)S(1)}, u32[]{:S(2)}, u32[]{:S(2)}) collective-permute-start(f32[2,64,512]{2,1,0:T(8,128)S(1)} %shard_map.91), channel_id=1, source_target_pairs={{0,8},{8,0},{16,24},{24,16},{1,9},{9,1},{17,25},{25,17},{2,10},{10... | collective-permute-start | bytes 786440 | tf_op jit(solution)/shard_map/ppermute | solution.py:396
  16.3 7.2 %collective-permute-start.5 = (f32[64,512]{1,0:T(8,128)S(1)}, f32[64,512]{1,0:T(8,128)S(1)}, u32[]{:S(2)}, u32[]{:S(2)}) collective-permute-start(f32[64,512]{1,0:T(8,128)S(1)} %get-tuple-element.49), channel_id=1, source_target_pairs={{0,16},{8,24},{16,0},{24,8},{1,17},{9,25},{17,1},{25,9},{2,18},{10... | collective-permute-start | bytes 393224 | tf_op jit(solution)/shard_map/ppermute | solution.py:396
  16.5 8.4 %collective-permute-start.4 = (f32[64,512]{1,0:T(8,128)S(1)}, f32[64,512]{1,0:T(8,128)S(1)}, u32[]{:S(2)}, u32[]{:S(2)}) collective-permute-start(f32[64,512]{1,0:T(8,128)S(1)} %shard_map.85), channel_id=1, source_target_pairs={{0,16},{8,24},{16,0},{24,8},{1,17},{9,25},{17,1},{25,9},{2,18},{10... | collective-permute-start | bytes 393224 | tf_op jit(solution)/shard_map/ppermute | solution.py:396
  18.4 6.5 %collective-permute-start.2 = (f32[64,512]{1,0:T(8,128)S(1)}, f32[64,512]{1,0:T(8,128)S(1)}, u32[]{:S(2)}, u32[]{:S(2)}) collective-permute-start(f32[64,512]{1,0:T(8,128)S(1)} %shard_map.84), channel_id=1, source_target_pairs={{0,8},{8,0},{16,24},{24,16},{1,9},{9,1},{17,25},{25,17},{2,10},{10... | collective-permute-start | bytes 393224 | tf_op jit(solution)/shard_map/ppermute | solution.py:396
  25.5 9.3 %collective-permute-start.6 = (f32[2,64,128]{2,1,0:T(8,128)S(1)}, f32[2,64,128]{2,1,0:T(8,128)S(1)}, u32[]{:S(2)}, u32[]{:S(2)}) collective-permute-start(f32[2,64,128]{2,1,0:T(8,128)S(1)} %get-tuple-element.51), channel_id=1, source_target_pairs={{0,2},{1,3},{2,0},{3,1},{4,6},{5,7},{6,4},{7,5},{8,10},{9,11},{10,... | collective-permute-start | bytes 196616 | tf_op jit(solution)/shard_map/ppermute | solution.py:404
  27.1 7.9 %collective-permute-start.7 = (f32[2,64,128]{2,1,0:T(8,128)S(1)}, f32[2,64,128]{2,1,0:T(8,128)S(1)}, u32[]{:S(2)}, u32[]{:S(2)}) collective-permute-start(f32[2,64,128]{2,1,0:T(8,128)S(1)} %get-tuple-element.52), channel_id=1, source_target_pairs={{0,4},{1,5},{2,6},{3,7},{4,0},{5,1},{6,2},{7,3},{8,12},{9,13},{10,... | collective-permute-start | bytes 196616 | tf_op jit(solution)/shard_map/ppermute | solution.py:404
  29.7 6.4 %collective-permute-start.8 = (f32[2,64,128]{2,1,0:T(8,128)S(1)}, f32[2,64,128]{2,1,0:T(8,128)S(1)}, u32[]{:S(2)}, u32[]{:S(2)}) collective-permute-start(f32[2,64,128]{2,1,0:T(8,128)S(1)} %get-tuple-element.53), channel_id=1, source_target_pairs={{0,6},{1,7},{2,4},{3,5},{4,2},{5,3},{6,0},{7,1},{8,14},{9,15},{10,... | collective-permute-start | bytes 196616 | tf_op jit(solution)/shard_map/ppermute | solution.py:404
  30.6 6.3 %collective-permute-start.20 = (f32[2,64,128]{2,1,0:T(8,128)S(1)}, f32[2,64,128]{2,1,0:T(8,128)S(1)}, u32[]{:S(2)}, u32[]{:S(2)}) collective-permute-start(f32[2,64,128]{2,1,0:T(8,128)S(1)} %get-tuple-element.66), channel_id=1, source_target_pairs={{0,2},{1,3},{2,0},{3,1},{4,6},{5,7},{6,4},{7,5},{8,10},{9,11},{10,... | collective-permute-start | bytes 196616 | tf_op jit(solution)/shard_map/ppermute | solution.py:404
  31.3 7.8 %collective-permute-start.21 = (f32[2,64,128]{2,1,0:T(8,128)S(1)}, f32[2,64,128]{2,1,0:T(8,128)S(1)}, u32[]{:S(2)}, u32[]{:S(2)}) collective-permute-start(f32[2,64,128]{2,1,0:T(8,128)S(1)} %get-tuple-element.67), channel_id=1, source_target_pairs={{0,4},{1,5},{2,6},{3,7},{4,0},{5,1},{6,2},{7,3},{8,12},{9,13},{10,... | collective-permute-start | bytes 196616 | tf_op jit(solution)/shard_map/ppermute | solution.py:404
  34.8 6.1 %collective-permute-start.22 = (f32[2,64,128]{2,1,0:T(8,128)S(1)}, f32[2,64,128]{2,1,0:T(8,128)S(1)}, u32[]{:S(2)}, u32[]{:S(2)}) collective-permute-start(f32[2,64,128]{2,1,0:T(8,128)S(1)} %get-tuple-element.68), channel_id=1, source_target_pairs={{0,6},{1,7},{2,4},{3,5},{4,2},{5,3},{6,0},{7,1},{8,14},{9,15},{10,... | collective-permute-start | bytes 196616 | tf_op jit(solution)/shard_map/ppermute | solution.py:404
  36.8 5.9 %collective-permute-start.9 = (f32[2,64,512]{2,1,0:T(8,128)S(1)}, f32[2,64,512]{2,1,0:T(8,128)S(1)}, u32[]{:S(2)}, u32[]{:S(2)}) collective-permute-start(f32[2,64,512]{2,1,0:T(8,128)S(1)} %get-tuple-element.55), channel_id=1, source_target_pairs={{0,1},{1,0},{2,3},{3,2},{4,5},{5,4},{6,7},{7,6},{8,9},{9,8},{10,11... | collective-permute-start | bytes 786440 | tf_op jit(solution)/shard_map/ppermute | solution.py:408
  41.6 6.2 %collective-permute-start.23 = (f32[2,64,512]{2,1,0:T(8,128)S(1)}, f32[2,64,512]{2,1,0:T(8,128)S(1)}, u32[]{:S(2)}, u32[]{:S(2)}) collective-permute-start(f32[2,64,512]{2,1,0:T(8,128)S(1)} %get-tuple-element.70), channel_id=1, source_target_pairs={{0,1},{1,0},{2,3},{3,2},{4,5},{5,4},{6,7},{7,6},{8,9},{9,8},{10,11... | collective-permute-start | bytes 786440 | tf_op jit(solution)/shard_map/ppermute | solution.py:408
  43.4 6.7 %collective-permute-start.10 = (f32[2,64,128]{2,1,0:T(8,128)S(1)}, f32[2,64,128]{2,1,0:T(8,128)S(1)}, u32[]{:S(2)}, u32[]{:S(2)}) collective-permute-start(f32[2,64,128]{2,1,0:T(8,128)S(1)} %get-tuple-element.57), channel_id=1, source_target_pairs={{0,2},{1,3},{2,0},{3,1},{4,6},{5,7},{6,4},{7,5},{8,10},{9,11},{10,... | collective-permute-start | bytes 196616 | tf_op jit(solution)/shard_map/ppermute | solution.py:404
  43.5 9.5 %collective-permute-start.11 = (f32[2,64,128]{2,1,0:T(8,128)S(1)}, f32[2,64,128]{2,1,0:T(8,128)S(1)}, u32[]{:S(2)}, u32[]{:S(2)}) collective-permute-start(f32[2,64,128]{2,1,0:T(8,128)S(1)} %get-tuple-element.58), channel_id=1, source_target_pairs={{0,4},{1,5},{2,6},{3,7},{4,0},{5,1},{6,2},{7,3},{8,12},{9,13},{10,... | collective-permute-start | bytes 196616 | tf_op jit(solution)/shard_map/ppermute | solution.py:404
  44.9 8.0 %collective-permute-start.12 = (f32[2,64,128]{2,1,0:T(8,128)S(1)}, f32[2,64,128]{2,1,0:T(8,128)S(1)}, u32[]{:S(2)}, u32[]{:S(2)}) collective-permute-start(f32[2,64,128]{2,1,0:T(8,128)S(1)} %get-tuple-element.59), channel_id=1, source_target_pairs={{0,6},{1,7},{2,4},{3,5},{4,2},{5,3},{6,0},{7,1},{8,14},{9,15},{10,... | collective-permute-start | bytes 196616 | tf_op jit(solution)/shard_map/ppermute | solution.py:404
  48.5 5.2 %collective-permute-start.24 = (f32[2,64,128]{2,1,0:T(8,128)S(1)}, f32[2,64,128]{2,1,0:T(8,128)S(1)}, u32[]{:S(2)}, u32[]{:S(2)}) collective-permute-start(f32[2,64,128]{2,1,0:T(8,128)S(1)} %get-tuple-element.72), channel_id=1, source_target_pairs={{0,2},{1,3},{2,0},{3,1},{4,6},{5,7},{6,4},{7,5},{8,10},{9,11},{10,... | collective-permute-start | bytes 196616 | tf_op jit(solution)/shard_map/ppermute | solution.py:404
  48.6 9.2 %collective-permute-start.25 = (f32[2,64,128]{2,1,0:T(8,128)S(1)}, f32[2,64,128]{2,1,0:T(8,128)S(1)}, u32[]{:S(2)}, u32[]{:S(2)}) collective-permute-start(f32[2,64,128]{2,1,0:T(8,128)S(1)} %get-tuple-element.73), channel_id=1, source_target_pairs={{0,4},{1,5},{2,6},{3,7},{4,0},{5,1},{6,2},{7,3},{8,12},{9,13},{10,... | collective-permute-start | bytes 196616 | tf_op jit(solution)/shard_map/ppermute | solution.py:404
  50.1 7.8 %collective-permute-start.26 = (f32[2,64,128]{2,1,0:T(8,128)S(1)}, f32[2,64,128]{2,1,0:T(8,128)S(1)}, u32[]{:S(2)}, u32[]{:S(2)}) collective-permute-start(f32[2,64,128]{2,1,0:T(8,128)S(1)} %get-tuple-element.74), channel_id=1, source_target_pairs={{0,6},{1,7},{2,4},{3,5},{4,2},{5,3},{6,0},{7,1},{8,14},{9,15},{10,... | collective-permute-start | bytes 196616 | tf_op jit(solution)/shard_map/ppermute | solution.py:404
  58.7 9.2 %collective-permute-start.15 = (f32[2,64,512]{2,1,0:T(8,128)S(1)}, f32[2,64,512]{2,1,0:T(8,128)S(1)}, u32[]{:S(2)}, u32[]{:S(2)}) collective-permute-start(f32[2,64,512]{2,1,0:T(8,128)S(1)} %add.6.refs_0_), channel_id=1, source_target_pairs={{0,16},{8,24},{16,0},{24,8},{1,17},{9,25},{17,1},{25,9},{2,18},{10... | collective-permute-start | bytes 786440 | tf_op jit(solution)/shard_map/ppermute | solution.py:396
  60.3 9.2 %collective-permute-start.14 = (f32[2,64,512]{2,1,0:T(8,128)S(1)}, f32[2,64,512]{2,1,0:T(8,128)S(1)}, u32[]{:S(2)}, u32[]{:S(2)}) collective-permute-start(f32[2,64,512]{2,1,0:T(8,128)S(1)} %add.6.refs_0_), channel_id=1, source_target_pairs={{0,8},{8,0},{16,24},{24,16},{1,9},{9,1},{17,25},{25,17},{2,10},{10... | collective-permute-start | bytes 786440 | tf_op jit(solution)/shard_map/ppermute | solution.py:396
  61.8 9.1 %collective-permute-start.31 = (f32[64,512]{1,0:T(8,128)S(1)}, f32[64,512]{1,0:T(8,128)S(1)}, u32[]{:S(2)}, u32[]{:S(2)}) collective-permute-start(f32[64,512]{1,0:T(8,128)S(1)} %get-tuple-element.79), channel_id=1, source_target_pairs={{0,16},{8,24},{16,0},{24,8},{1,17},{9,25},{17,1},{25,9},{2,18},{10... | collective-permute-start | bytes 393224 | tf_op jit(solution)/shard_map/ppermute | solution.py:396
  62.4 9.9 %collective-permute-start.29 = (f32[64,512]{1,0:T(8,128)S(1)}, f32[64,512]{1,0:T(8,128)S(1)}, u32[]{:S(2)}, u32[]{:S(2)}) collective-permute-start(f32[64,512]{1,0:T(8,128)S(1)} %get-tuple-element.79), channel_id=1, source_target_pairs={{0,8},{8,0},{16,24},{24,16},{1,9},{9,1},{17,25},{25,17},{2,10},{10... | collective-permute-start | bytes 393224 | tf_op jit(solution)/shard_map/ppermute | solution.py:396
  63.3 12.5 %collective-permute-start.30 = (f32[64,512]{1,0:T(8,128)S(1)}, f32[64,512]{1,0:T(8,128)S(1)}, u32[]{:S(2)}, u32[]{:S(2)}) collective-permute-start(f32[64,512]{1,0:T(8,128)S(1)} %get-tuple-element.80), channel_id=1, source_target_pairs={{0,16},{8,24},{16,0},{24,8},{1,17},{9,25},{17,1},{25,9},{2,18},{10... | collective-permute-start | bytes 393224 | tf_op jit(solution)/shard_map/ppermute | solution.py:396
  67.9 7.1 %collective-permute-start.28 = (f32[64,512]{1,0:T(8,128)S(1)}, f32[64,512]{1,0:T(8,128)S(1)}, u32[]{:S(2)}, u32[]{:S(2)}) collective-permute-start(f32[64,512]{1,0:T(8,128)S(1)} %get-tuple-element.80), channel_id=1, source_target_pairs={{0,8},{8,0},{16,24},{24,16},{1,9},{9,1},{17,25},{25,17},{2,10},{10... | collective-permute-start | bytes 393224 | tf_op jit(solution)/shard_map/ppermute | solution.py:396
  69.4 8.4 %collective-permute-start.17 = (f32[64,512]{1,0:T(8,128)S(1)}, f32[64,512]{1,0:T(8,128)S(1)}, u32[]{:S(2)}, u32[]{:S(2)}) collective-permute-start(f32[64,512]{1,0:T(8,128)S(1)} %slice_bitcast_fusion.2), channel_id=1, source_target_pairs={{0,8},{8,0},{16,24},{24,16},{1,9},{9,1},{17,25},{25,17},{2,10},{10... | collective-permute-start | bytes 393224 | tf_op jit(solution)/shard_map/ppermute | solution.py:396
  71.0 6.9 %collective-permute-start.16 = (f32[64,512]{1,0:T(8,128)S(1)}, f32[64,512]{1,0:T(8,128)S(1)}, u32[]{:S(2)}, u32[]{:S(2)}) collective-permute-start(f32[64,512]{1,0:T(8,128)S(1)} %slice_bitcast_fusion.3), channel_id=1, source_target_pairs={{0,16},{8,24},{16,0},{24,8},{1,17},{9,25},{17,1},{25,9},{2,18},{10... | collective-permute-start | bytes 393224 | tf_op jit(solution)/shard_map/ppermute | solution.py:396
  72.3 8.5 %collective-permute-start.33 = (f32[64,512]{1,0:T(8,128)S(1)}, f32[64,512]{1,0:T(8,128)S(1)}, u32[]{:S(2)}, u32[]{:S(2)}) collective-permute-start(f32[64,512]{1,0:T(8,128)S(1)} %collective-permute-done.31.refs_9_), channel_id=1, source_target_pairs={{0,8},{8,0},{16,24},{24,16},{1,9},{9,1},{17,25},{25,17},{2,10},{10... | collective-permute-start | bytes 393224 | tf_op jit(solution)/shard_map/ppermute | solution.py:396
  75.1 5.7 %collective-permute-start.32 = (f32[64,512]{1,0:T(8,128)S(1)}, f32[64,512]{1,0:T(8,128)S(1)}, u32[]{:S(2)}, u32[]{:S(2)}) collective-permute-start(f32[64,512]{1,0:T(8,128)S(1)} %collective-permute-done.28.refs_6_), channel_id=1, source_target_pairs={{0,16},{8,24},{16,0},{24,8},{1,17},{9,25},{17,1},{25,9},{2,18},{10... | collective-permute-start | bytes 393224 | tf_op jit(solution)/shard_map/ppermute | solution.py:396
  (7 other events, 61.9 us)

commit v3 on v2

--- a/solution.py
+++ b/solution.py
@@ -320,7 +320,9 @@
 def finish_kernel(near, key, offsets, factor, window, real, imag, whole, out, buffer, sems):
     total = out.shape[3] // LANES
     item = near(*key)
-    block, pieces = turned_pieces(offsets[item], factor.at[item], real, imag)
+    spot = lax.broadcasted_iota(jnp.int32, offsets.shape, 1)
+    offset = jnp.sum(jnp.where(spot == item, offsets[...], 0))
+    block, pieces = turned_pieces(offset, factor.at[item], real, imag)
 
     def copy(piece):
         return pltpu.make_async_copy(
@@ -591,12 +593,12 @@
             pltpu.VMEM((blocks + 1, 2, rows, LANES), jnp.float32),
             pltpu.SemaphoreType.DMA((blocks + 1,)),
         ],
-        [SMEM, VMEM, VMEM, VMEM, VMEM, HBM],
+        [VMEM] * 5 + [HBM],
         8 * MIB,
         matmul_cost // 8,
         out_specs=[HBM],
         input_output_aliases={5: 0},
-    )(grid_offsets, factor, window, *last_item, whole)
+    )(grid_offsets.reshape(1, subgrids), factor, window, *last_item, whole)
     return update
 
 

time: 82.3 us -> 81.9 us (level)
  no operation moved by 1% of the time
where the time goes in v3:
time: 81.9 us; the launch traced here: 81.7 us
  starting transfers between devices  42.3 us (52%)
  waiting for transfers between devices  23.1 us (28%)
  Pallas kernels  15.8 us (19%)
    ppermute x18, starting transfers between devices, move(): return lax.ppermute(value, 'facet', pairs)  24.3 us
    ppermute x12, starting transfers between devices, exchange(): out[distance] = lax.ppermute(pieces[distance], 'team', pairs)  17.8 us
    ppermute x18, waiting for transfers between devices, move(): return lax.ppermute(value, 'facet', pairs)  14 us
    ppermute x12, waiting for transfers between devices, exchange(): out[distance] = lax.ppermute(pieces[distance], 'team', pairs)  9.1 us
    pallas_call x1, Pallas kernels, tiled_device(): call(functools.partial(window_kernel, near_layout, near, near_keys), [sha...  3.21 us
    pallas_call x1, Pallas kernels, tiled_device(): call(functools.partial(update_kernel, [len(item) for item in first_items]...  2.84 us
    pallas_call x4, Pallas kernels, cross(): call(functools.partial(cross_kernel, sign), [block_shape] * 2, [pltpu.VME...  2.79 us
    pallas_call x1, Pallas kernels, tiled_device(): call(functools.partial(corner_window_kernel, per_facet, near, corner_keys...  2.36 us
  transfers between devices with their start and end apart: 34, of which 10 were waited for; matrix products, arithmetic and copies ran while one was open for 0% of the time, Pallas kernels for 15%

profile of v3, /device:TPU:0, one launch (start us, length us, event | category | flops | bytes accessed | tf_op | source)
XLA Modules:
  0.0 81.7 jit_solution(14468045557697105107)
XLA Ops:
  0.0 2.4 %shard_map.82 = (f32[8,2,512]{2,1,0:T(2,128)S(1)}, f32[2,64,512]{2,1,0:T(8,128)S(1)}, f32[2,64,512]{2,1,0:T(8,128)S(1)}) custom-call(s32[8]{0:T(128)} %offsets.3, s32[4]{0:T(128)} %facet_offsets_hbm.1, f32[1,512]{1,0:T(1,128)} %bitcast.11, f32[1,2,64,5120]{3,2,1,0:T(8,128)} %columns.3), custom_call_target="tpu_custom_call" | custom-call | flops 50331648 | bytes 786432 | tf_op jit(solution)/shard_map/pallas_call | solution.py:435
  2.4 3.0 %collective-permute-start.3 = (f32[2,64,512]{2,1,0:T(8,128)S(1)}, f32[2,64,512]{2,1,0:T(8,128)S(1)}, u32[]{:S(2)}, u32[]{:S(2)}) collective-permute-start(f32[2,64,512]{2,1,0:T(8,128)S(1)} %get-tuple-element.48), channel_id=1, source_target_pairs={{0,8},{8,0},{16,24},{24,16},{1,9},{9,1},{17,25},{25,17},{2,10},{10... | collective-permute-start | bytes 786440 | tf_op jit(solution)/shard_map/ppermute | solution.py:398
  5.4 1.5 %collective-permute-start.1 = (f32[2,64,512]{2,1,0:T(8,128)S(1)}, f32[2,64,512]{2,1,0:T(8,128)S(1)}, u32[]{:S(2)}, u32[]{:S(2)}) collective-permute-start(f32[2,64,512]{2,1,0:T(8,128)S(1)} %get-tuple-element.46), channel_id=1, source_target_pairs={{0,16},{8,24},{16,0},{24,8},{1,17},{9,25},{17,1},{25,9},{2,18},{10... | collective-permute-start | bytes 786440 | tf_op jit(solution)/shard_map/ppermute | solution.py:398
  6.9 3.2 %shard_map.83 = (f32[2,64,512]{2,1,0:T(8,128)S(1)}, f32[64,512]{1,0:T(8,128)S(1)}, f32[64,512]{1,0:T(8,128)S(1)}, f32[64,512]{1,0:T(8,128)S(1)}, f32[64,512]{1,0...) custom-call(s32[8]{0:T(128)S(1)} %copy-done.3, ...), custom_call_target="tpu_custom_call" | custom-call | flops 100663296 | bytes 1572864 | tf_op jit(solution)/shard_map/pallas_call | solution.py:460
  10.7 1.1 %collective-permute-done.3.refs_0_ = f32[2,64,512]{2,1,0:T(8,128)S(1)} collective-permute-done((f32[2,64,512]{2,1,0:T(8,128)S(1)}, f32[2,64,512]{2,1,0:T(8,128)S(1)}, u32[]{:S(2)}, u32[]{:S(2)}) %collective-permute-start.3) | collective-permute-done | bytes 262176 | tf_op jit(solution)/shard_map/ppermute | solution.py:398
  11.8 2.6 %collective-permute-start.19 = (f32[2,64,512]{2,1,0:T(8,128)S(1)}, f32[2,64,512]{2,1,0:T(8,128)S(1)}, u32[]{:S(2)}, u32[]{:S(2)}) collective-permute-start(f32[2,64,512]{2,1,0:T(8,128)S(1)} %shard_map.92), channel_id=1, source_target_pairs={{0,16},{8,24},{16,0},{24,8},{1,17},{9,25},{17,1},{25,9},{2,18},{10... | collective-permute-start | bytes 786440 | tf_op jit(solution)/shard_map/ppermute | solution.py:398
  14.5 1.8 %collective-permute-start.18 = (f32[2,64,512]{2,1,0:T(8,128)S(1)}, f32[2,64,512]{2,1,0:T(8,128)S(1)}, u32[]{:S(2)}, u32[]{:S(2)}) collective-permute-start(f32[2,64,512]{2,1,0:T(8,128)S(1)} %shard_map.91), channel_id=1, source_target_pairs={{0,8},{8,0},{16,24},{24,16},{1,9},{9,1},{17,25},{25,17},{2,10},{10... | collective-permute-start | bytes 786440 | tf_op jit(solution)/shard_map/ppermute | solution.py:398
  16.5 1.9 %collective-permute-start.4 = (f32[64,512]{1,0:T(8,128)S(1)}, f32[64,512]{1,0:T(8,128)S(1)}, u32[]{:S(2)}, u32[]{:S(2)}) collective-permute-start(f32[64,512]{1,0:T(8,128)S(1)} %shard_map.85), channel_id=1, source_target_pairs={{0,16},{8,24},{16,0},{24,8},{1,17},{9,25},{17,1},{25,9},{2,18},{10... | collective-permute-start | bytes 393224 | tf_op jit(solution)/shard_map/ppermute | solution.py:398
  18.8 4.7 %collective-permute-done.5.refs_4_ = f32[64,512]{1,0:T(8,128)S(1)} collective-permute-done((f32[64,512]{1,0:T(8,128)S(1)}, f32[64,512]{1,0:T(8,128)S(1)}, u32[]{:S(2)}, u32[]{:S(2)}) %collective-permute-start.5) | collective-permute-done | bytes 131104 | tf_op jit(solution)/shard_map/ppermute | solution.py:398
  23.5 1.4 %collective-permute-done.4.refs_3_ = f32[64,512]{1,0:T(8,128)S(1)} collective-permute-done((f32[64,512]{1,0:T(8,128)S(1)}, f32[64,512]{1,0:T(8,128)S(1)}, u32[]{:S(2)}, u32[]{:S(2)}) %collective-permute-start.4) | collective-permute-done | bytes 131104 | tf_op jit(solution)/shard_map/ppermute | solution.py:398
  25.5 1.6 %collective-permute-start.6 = (f32[2,64,128]{2,1,0:T(8,128)S(1)}, f32[2,64,128]{2,1,0:T(8,128)S(1)}, u32[]{:S(2)}, u32[]{:S(2)}) collective-permute-start(f32[2,64,128]{2,1,0:T(8,128)S(1)} %get-tuple-element.51), channel_id=1, source_target_pairs={{0,2},{1,3},{2,0},{3,1},{4,6},{5,7},{6,4},{7,5},{8,10},{9,11},{10,... | collective-permute-start | bytes 196616 | tf_op jit(solution)/shard_map/ppermute | solution.py:406
  27.1 2.6 %collective-permute-start.7 = (f32[2,64,128]{2,1,0:T(8,128)S(1)}, f32[2,64,128]{2,1,0:T(8,128)S(1)}, u32[]{:S(2)}, u32[]{:S(2)}) collective-permute-start(f32[2,64,128]{2,1,0:T(8,128)S(1)} %get-tuple-element.52), channel_id=1, source_target_pairs={{0,4},{1,5},{2,6},{3,7},{4,0},{5,1},{6,2},{7,3},{8,12},{9,13},{10,... | collective-permute-start | bytes 196616 | tf_op jit(solution)/shard_map/ppermute | solution.py:406
  31.3 3.5 %collective-permute-start.21 = (f32[2,64,128]{2,1,0:T(8,128)S(1)}, f32[2,64,128]{2,1,0:T(8,128)S(1)}, u32[]{:S(2)}, u32[]{:S(2)}) collective-permute-start(f32[2,64,128]{2,1,0:T(8,128)S(1)} %get-tuple-element.67), channel_id=1, source_target_pairs={{0,4},{1,5},{2,6},{3,7},{4,0},{5,1},{6,2},{7,3},{8,12},{9,13},{10,... | collective-permute-start | bytes 196616 | tf_op jit(solution)/shard_map/ppermute | solution.py:406
  35.1 1.0 %collective-permute-done.8.refs_3_ = f32[2,64,128]{2,1,0:T(8,128)S(1)} collective-permute-done((f32[2,64,128]{2,1,0:T(8,128)S(1)}, f32[2,64,128]{2,1,0:T(8,128)S(1)}, u32[]{:S(2)}, u32[]{:S(2)}) %collective-permute-start.8) | collective-permute-done | bytes 65568 | tf_op jit(solution)/shard_map/ppermute | solution.py:406
  36.9 2.3 %collective-permute-done.21.refs_2_ = f32[2,64,128]{2,1,0:T(8,128)S(1)} collective-permute-done((f32[2,64,128]{2,1,0:T(8,128)S(1)}, f32[2,64,128]{2,1,0:T(8,128)S(1)}, u32[]{:S(2)}, u32[]{:S(2)}) %collective-permute-start.21) | collective-permute-done | bytes 65568 | tf_op jit(solution)/shard_map/ppermute | solution.py:406
  39.2 1.7 %collective-permute-done.22.refs_3_ = f32[2,64,128]{2,1,0:T(8,128)S(1)} collective-permute-done((f32[2,64,128]{2,1,0:T(8,128)S(1)}, f32[2,64,128]{2,1,0:T(8,128)S(1)}, u32[]{:S(2)}, u32[]{:S(2)}) %collective-permute-start.22) | collective-permute-done | bytes 65568 | tf_op jit(solution)/shard_map/ppermute | solution.py:406
  43.5 1.5 %collective-permute-start.11 = (f32[2,64,128]{2,1,0:T(8,128)S(1)}, f32[2,64,128]{2,1,0:T(8,128)S(1)}, u32[]{:S(2)}, u32[]{:S(2)}) collective-permute-start(f32[2,64,128]{2,1,0:T(8,128)S(1)} %get-tuple-element.58), channel_id=1, source_target_pairs={{0,4},{1,5},{2,6},{3,7},{4,0},{5,1},{6,2},{7,3},{8,12},{9,13},{10,... | collective-permute-start | bytes 196616 | tf_op jit(solution)/shard_map/ppermute | solution.py:406
  44.9 2.9 %collective-permute-start.12 = (f32[2,64,128]{2,1,0:T(8,128)S(1)}, f32[2,64,128]{2,1,0:T(8,128)S(1)}, u32[]{:S(2)}, u32[]{:S(2)}) collective-permute-start(f32[2,64,128]{2,1,0:T(8,128)S(1)} %get-tuple-element.59), channel_id=1, source_target_pairs={{0,6},{1,7},{2,4},{3,5},{4,2},{5,3},{6,0},{7,1},{8,14},{9,15},{10,... | collective-permute-start | bytes 196616 | tf_op jit(solution)/shard_map/ppermute | solution.py:406
  48.6 1.5 %collective-permute-start.25 = (f32[2,64,128]{2,1,0:T(8,128)S(1)}, f32[2,64,128]{2,1,0:T(8,128)S(1)}, u32[]{:S(2)}, u32[]{:S(2)}) collective-permute-start(f32[2,64,128]{2,1,0:T(8,128)S(1)} %get-tuple-element.73), channel_id=1, source_target_pairs={{0,4},{1,5},{2,6},{3,7},{4,0},{5,1},{6,2},{7,3},{8,12},{9,13},{10,... | collective-permute-start | bytes 196616 | tf_op jit(solution)/shard_map/ppermute | solution.py:406
  50.1 2.9 %collective-permute-start.26 = (f32[2,64,128]{2,1,0:T(8,128)S(1)}, f32[2,64,128]{2,1,0:T(8,128)S(1)}, u32[]{:S(2)}, u32[]{:S(2)}) collective-permute-start(f32[2,64,128]{2,1,0:T(8,128)S(1)} %get-tuple-element.74), channel_id=1, source_target_pairs={{0,6},{1,7},{2,4},{3,5},{4,2},{5,3},{6,0},{7,1},{8,14},{9,15},{10,... | collective-permute-start | bytes 196616 | tf_op jit(solution)/shard_map/ppermute | solution.py:406
  53.8 4.1 %collective-permute-done.25.refs_2_ = f32[2,64,128]{2,1,0:T(8,128)S(1)} collective-permute-done((f32[2,64,128]{2,1,0:T(8,128)S(1)}, f32[2,64,128]{2,1,0:T(8,128)S(1)}, u32[]{:S(2)}, u32[]{:S(2)}) %collective-permute-start.25) | collective-permute-done | bytes 65568 | tf_op jit(solution)/shard_map/ppermute | solution.py:406
  58.7 1.6 %collective-permute-start.15 = (f32[2,64,512]{2,1,0:T(8,128)S(1)}, f32[2,64,512]{2,1,0:T(8,128)S(1)}, u32[]{:S(2)}, u32[]{:S(2)}) collective-permute-start(f32[2,64,512]{2,1,0:T(8,128)S(1)} %add.6.refs_0_), channel_id=1, source_target_pairs={{0,16},{8,24},{16,0},{24,8},{1,17},{9,25},{17,1},{25,9},{2,18},{10... | collective-permute-start | bytes 786440 | tf_op jit(solution)/shard_map/ppermute | solution.py:398
  60.3 1.5 %collective-permute-start.14 = (f32[2,64,512]{2,1,0:T(8,128)S(1)}, f32[2,64,512]{2,1,0:T(8,128)S(1)}, u32[]{:S(2)}, u32[]{:S(2)}) collective-permute-start(f32[2,64,512]{2,1,0:T(8,128)S(1)} %add.6.refs_0_), channel_id=1, source_target_pairs={{0,8},{8,0},{16,24},{24,16},{1,9},{9,1},{17,25},{25,17},{2,10},{10... | collective-permute-start | bytes 786440 | tf_op jit(solution)/shard_map/ppermute | solution.py:398
  63.3 1.2 %collective-permute-start.30 = (f32[64,512]{1,0:T(8,128)S(1)}, f32[64,512]{1,0:T(8,128)S(1)}, u32[]{:S(2)}, u32[]{:S(2)}) collective-permute-start(f32[64,512]{1,0:T(8,128)S(1)} %get-tuple-element.80), channel_id=1, source_target_pairs={{0,16},{8,24},{16,0},{24,8},{1,17},{9,25},{17,1},{25,9},{2,18},{10... | collective-permute-start | bytes 393224 | tf_op jit(solution)/shard_map/ppermute | solution.py:398
  64.5 3.5 %collective-permute-done.15.refs_2_ = f32[2,64,512]{2,1,0:T(8,128)S(1)} collective-permute-done((f32[2,64,512]{2,1,0:T(8,128)S(1)}, f32[2,64,512]{2,1,0:T(8,128)S(1)}, u32[]{:S(2)}, u32[]{:S(2)}) %collective-permute-start.15) | collective-permute-done | bytes 262176 | tf_op jit(solution)/shard_map/ppermute | solution.py:398
  67.9 1.5 %collective-permute-start.28 = (f32[64,512]{1,0:T(8,128)S(1)}, f32[64,512]{1,0:T(8,128)S(1)}, u32[]{:S(2)}, u32[]{:S(2)}) collective-permute-start(f32[64,512]{1,0:T(8,128)S(1)} %get-tuple-element.80), channel_id=1, source_target_pairs={{0,8},{8,0},{16,24},{24,16},{1,9},{9,1},{17,25},{25,17},{2,10},{10... | collective-permute-start | bytes 393224 | tf_op jit(solution)/shard_map/ppermute | solution.py:398
  69.4 1.5 %collective-permute-start.17 = (f32[64,512]{1,0:T(8,128)S(1)}, f32[64,512]{1,0:T(8,128)S(1)}, u32[]{:S(2)}, u32[]{:S(2)}) collective-permute-start(f32[64,512]{1,0:T(8,128)S(1)} %slice_bitcast_fusion.2), channel_id=1, source_target_pairs={{0,8},{8,0},{16,24},{24,16},{1,9},{9,1},{17,25},{25,17},{2,10},{10... | collective-permute-start | bytes 393224 | tf_op jit(solution)/shard_map/ppermute | solution.py:398
  71.0 1.3 %collective-permute-start.16 = (f32[64,512]{1,0:T(8,128)S(1)}, f32[64,512]{1,0:T(8,128)S(1)}, u32[]{:S(2)}, u32[]{:S(2)}) collective-permute-start(f32[64,512]{1,0:T(8,128)S(1)} %slice_bitcast_fusion.3), channel_id=1, source_target_pairs={{0,16},{8,24},{16,0},{24,8},{1,17},{9,25},{17,1},{25,9},{2,18},{10... | collective-permute-start | bytes 393224 | tf_op jit(solution)/shard_map/ppermute | solution.py:398
  72.3 1.5 %collective-permute-start.33 = (f32[64,512]{1,0:T(8,128)S(1)}, f32[64,512]{1,0:T(8,128)S(1)}, u32[]{:S(2)}, u32[]{:S(2)}) collective-permute-start(f32[64,512]{1,0:T(8,128)S(1)} %collective-permute-done.31.refs_9_), channel_id=1, source_target_pairs={{0,8},{8,0},{16,24},{24,16},{1,9},{9,1},{17,25},{25,17},{2,10},{10... | collective-permute-start | bytes 393224 | tf_op jit(solution)/shard_map/ppermute | solution.py:398
  73.7 1.3 %collective-permute-done.28.refs_6_ = f32[64,512]{1,0:T(8,128)S(1)} collective-permute-done((f32[64,512]{1,0:T(8,128)S(1)}, f32[64,512]{1,0:T(8,128)S(1)}, u32[]{:S(2)}, u32[]{:S(2)}) %collective-permute-start.28) | collective-permute-done | bytes 131104 | tf_op jit(solution)/shard_map/ppermute | solution.py:398
  75.8 2.1 %collective-permute-done.17.refs_4_ = f32[64,512]{1,0:T(8,128)S(1)} collective-permute-done((f32[64,512]{1,0:T(8,128)S(1)}, f32[64,512]{1,0:T(8,128)S(1)}, u32[]{:S(2)}, u32[]{:S(2)}) %collective-permute-start.17) | collective-permute-done | bytes 131104 | tf_op jit(solution)/shard_map/ppermute | solution.py:398
  77.9 2.8 %shard_map.97 = (f32[1,2,64,5120]{3,2,1,0:T(8,128)}, f32[2,64,640]{2,1,0:T(8,128)S(1)}) custom-call(s32[8]{0:T(128)S(1)} %copy-done.3, f32[8,2,512]{2,1,0:T(2,128)S(1)} %get-tuple-element.42.factor, f32[2,64,512]{2,1,0:T(8,128)S(1)} %add.6.refs_0_, f32[2,64,512]{2,1,0:T(8,128)S(1)} %collective-permute-done.14.refs_1_, ...), custom_call_target="tpu_custom_call" | custom-call | flops 402653184 | bytes 6291456 | tf_op jit(solution)/shard_map/pallas_call | solution.py:581
  (68 shorter events, 12.7 us)
Async XLA Ops:
  2.4 9.4 %collective-permute-start.3 = (f32[2,64,512]{2,1,0:T(8,128)S(1)}, f32[2,64,512]{2,1,0:T(8,128)S(1)}, u32[]{:S(2)}, u32[]{:S(2)}) collective-permute-start(f32[2,64,512]{2,1,0:T(8,128)S(1)} %get-tuple-element.48), channel_id=1, source_target_pairs={{0,8},{8,0},{16,24},{24,16},{1,9},{9,1},{17,25},{25,17},{2,10},{10... | collective-permute-start | bytes 786440 | tf_op jit(solution)/shard_map/ppermute | solution.py:398
  5.4 9.1 %collective-permute-start.1 = (f32[2,64,512]{2,1,0:T(8,128)S(1)}, f32[2,64,512]{2,1,0:T(8,128)S(1)}, u32[]{:S(2)}, u32[]{:S(2)}) collective-permute-start(f32[2,64,512]{2,1,0:T(8,128)S(1)} %get-tuple-element.46), channel_id=1, source_target_pairs={{0,16},{8,24},{16,0},{24,8},{1,17},{9,25},{17,1},{25,9},{2,18},{10... | collective-permute-start | bytes 786440 | tf_op jit(solution)/shard_map/ppermute | solution.py:398
  10.1 8.3 %collective-permute-start = (f32[64,512]{1,0:T(8,128)S(1)}, f32[64,512]{1,0:T(8,128)S(1)}, u32[]{:S(2)}, u32[]{:S(2)}) collective-permute-start(f32[64,512]{1,0:T(8,128)S(1)} %get-tuple-element.44), channel_id=1, source_target_pairs={{0,8},{8,0},{16,24},{24,16},{1,9},{9,1},{17,25},{25,17},{2,10},{10... | collective-permute-start | bytes 393224 | tf_op jit(solution)/shard_map/ppermute | solution.py:398
  11.8 18.2 %collective-permute-start.19 = (f32[2,64,512]{2,1,0:T(8,128)S(1)}, f32[2,64,512]{2,1,0:T(8,128)S(1)}, u32[]{:S(2)}, u32[]{:S(2)}) collective-permute-start(f32[2,64,512]{2,1,0:T(8,128)S(1)} %shard_map.92), channel_id=1, source_target_pairs={{0,16},{8,24},{16,0},{24,8},{1,17},{9,25},{17,1},{25,9},{2,18},{10... | collective-permute-start | bytes 786440 | tf_op jit(solution)/shard_map/ppermute | solution.py:398
  14.5 15.5 %collective-permute-start.18 = (f32[2,64,512]{2,1,0:T(8,128)S(1)}, f32[2,64,512]{2,1,0:T(8,128)S(1)}, u32[]{:S(2)}, u32[]{:S(2)}) collective-permute-start(f32[2,64,512]{2,1,0:T(8,128)S(1)} %shard_map.91), channel_id=1, source_target_pairs={{0,8},{8,0},{16,24},{24,16},{1,9},{9,1},{17,25},{25,17},{2,10},{10... | collective-permute-start | bytes 786440 | tf_op jit(solution)/shard_map/ppermute | solution.py:398
  16.3 7.2 %collective-permute-start.5 = (f32[64,512]{1,0:T(8,128)S(1)}, f32[64,512]{1,0:T(8,128)S(1)}, u32[]{:S(2)}, u32[]{:S(2)}) collective-permute-start(f32[64,512]{1,0:T(8,128)S(1)} %get-tuple-element.49), channel_id=1, source_target_pairs={{0,16},{8,24},{16,0},{24,8},{1,17},{9,25},{17,1},{25,9},{2,18},{10... | collective-permute-start | bytes 393224 | tf_op jit(solution)/shard_map/ppermute | solution.py:398
  16.5 8.4 %collective-permute-start.4 = (f32[64,512]{1,0:T(8,128)S(1)}, f32[64,512]{1,0:T(8,128)S(1)}, u32[]{:S(2)}, u32[]{:S(2)}) collective-permute-start(f32[64,512]{1,0:T(8,128)S(1)} %shard_map.85), channel_id=1, source_target_pairs={{0,16},{8,24},{16,0},{24,8},{1,17},{9,25},{17,1},{25,9},{2,18},{10... | collective-permute-start | bytes 393224 | tf_op jit(solution)/shard_map/ppermute | solution.py:398
  18.4 6.5 %collective-permute-start.2 = (f32[64,512]{1,0:T(8,128)S(1)}, f32[64,512]{1,0:T(8,128)S(1)}, u32[]{:S(2)}, u32[]{:S(2)}) collective-permute-start(f32[64,512]{1,0:T(8,128)S(1)} %shard_map.84), channel_id=1, source_target_pairs={{0,8},{8,0},{16,24},{24,16},{1,9},{9,1},{17,25},{25,17},{2,10},{10... | collective-permute-start | bytes 393224 | tf_op jit(solution)/shard_map/ppermute | solution.py:398
  25.5 9.3 %collective-permute-start.6 = (f32[2,64,128]{2,1,0:T(8,128)S(1)}, f32[2,64,128]{2,1,0:T(8,128)S(1)}, u32[]{:S(2)}, u32[]{:S(2)}) collective-permute-start(f32[2,64,128]{2,1,0:T(8,128)S(1)} %get-tuple-element.51), channel_id=1, source_target_pairs={{0,2},{1,3},{2,0},{3,1},{4,6},{5,7},{6,4},{7,5},{8,10},{9,11},{10,... | collective-permute-start | bytes 196616 | tf_op jit(solution)/shard_map/ppermute | solution.py:406
  27.1 7.9 %collective-permute-start.7 = (f32[2,64,128]{2,1,0:T(8,128)S(1)}, f32[2,64,128]{2,1,0:T(8,128)S(1)}, u32[]{:S(2)}, u32[]{:S(2)}) collective-permute-start(f32[2,64,128]{2,1,0:T(8,128)S(1)} %get-tuple-element.52), channel_id=1, source_target_pairs={{0,4},{1,5},{2,6},{3,7},{4,0},{5,1},{6,2},{7,3},{8,12},{9,13},{10,... | collective-permute-start | bytes 196616 | tf_op jit(solution)/shard_map/ppermute | solution.py:406
  29.7 6.4 %collective-permute-start.8 = (f32[2,64,128]{2,1,0:T(8,128)S(1)}, f32[2,64,128]{2,1,0:T(8,128)S(1)}, u32[]{:S(2)}, u32[]{:S(2)}) collective-permute-start(f32[2,64,128]{2,1,0:T(8,128)S(1)} %get-tuple-element.53), channel_id=1, source_target_pairs={{0,6},{1,7},{2,4},{3,5},{4,2},{5,3},{6,0},{7,1},{8,14},{9,15},{10,... | collective-permute-start | bytes 196616 | tf_op jit(solution)/shard_map/ppermute | solution.py:406
  30.6 6.3 %collective-permute-start.20 = (f32[2,64,128]{2,1,0:T(8,128)S(1)}, f32[2,64,128]{2,1,0:T(8,128)S(1)}, u32[]{:S(2)}, u32[]{:S(2)}) collective-permute-start(f32[2,64,128]{2,1,0:T(8,128)S(1)} %get-tuple-element.66), channel_id=1, source_target_pairs={{0,2},{1,3},{2,0},{3,1},{4,6},{5,7},{6,4},{7,5},{8,10},{9,11},{10,... | collective-permute-start | bytes 196616 | tf_op jit(solution)/shard_map/ppermute | solution.py:406
  31.3 7.8 %collective-permute-start.21 = (f32[2,64,128]{2,1,0:T(8,128)S(1)}, f32[2,64,128]{2,1,0:T(8,128)S(1)}, u32[]{:S(2)}, u32[]{:S(2)}) collective-permute-start(f32[2,64,128]{2,1,0:T(8,128)S(1)} %get-tuple-element.67), channel_id=1, source_target_pairs={{0,4},{1,5},{2,6},{3,7},{4,0},{5,1},{6,2},{7,3},{8,12},{9,13},{10,... | collective-permute-start | bytes 196616 | tf_op jit(solution)/shard_map/ppermute | solution.py:406
  34.8 6.1 %collective-permute-start.22 = (f32[2,64,128]{2,1,0:T(8,128)S(1)}, f32[2,64,128]{2,1,0:T(8,128)S(1)}, u32[]{:S(2)}, u32[]{:S(2)}) collective-permute-start(f32[2,64,128]{2,1,0:T(8,128)S(1)} %get-tuple-element.68), channel_id=1, source_target_pairs={{0,6},{1,7},{2,4},{3,5},{4,2},{5,3},{6,0},{7,1},{8,14},{9,15},{10,... | collective-permute-start | bytes 196616 | tf_op jit(solution)/shard_map/ppermute | solution.py:406
  36.8 5.9 %collective-permute-start.9 = (f32[2,64,512]{2,1,0:T(8,128)S(1)}, f32[2,64,512]{2,1,0:T(8,128)S(1)}, u32[]{:S(2)}, u32[]{:S(2)}) collective-permute-start(f32[2,64,512]{2,1,0:T(8,128)S(1)} %get-tuple-element.55), channel_id=1, source_target_pairs={{0,1},{1,0},{2,3},{3,2},{4,5},{5,4},{6,7},{7,6},{8,9},{9,8},{10,11... | collective-permute-start | bytes 786440 | tf_op jit(solution)/shard_map/ppermute | solution.py:410
  41.6 6.2 %collective-permute-start.23 = (f32[2,64,512]{2,1,0:T(8,128)S(1)}, f32[2,64,512]{2,1,0:T(8,128)S(1)}, u32[]{:S(2)}, u32[]{:S(2)}) collective-permute-start(f32[2,64,512]{2,1,0:T(8,128)S(1)} %get-tuple-element.70), channel_id=1, source_target_pairs={{0,1},{1,0},{2,3},{3,2},{4,5},{5,4},{6,7},{7,6},{8,9},{9,8},{10,11... | collective-permute-start | bytes 786440 | tf_op jit(solution)/shard_map/ppermute | solution.py:410
  43.4 6.7 %collective-permute-start.10 = (f32[2,64,128]{2,1,0:T(8,128)S(1)}, f32[2,64,128]{2,1,0:T(8,128)S(1)}, u32[]{:S(2)}, u32[]{:S(2)}) collective-permute-start(f32[2,64,128]{2,1,0:T(8,128)S(1)} %get-tuple-element.57), channel_id=1, source_target_pairs={{0,2},{1,3},{2,0},{3,1},{4,6},{5,7},{6,4},{7,5},{8,10},{9,11},{10,... | collective-permute-start | bytes 196616 | tf_op jit(solution)/shard_map/ppermute | solution.py:406
  43.5 9.5 %collective-permute-start.11 = (f32[2,64,128]{2,1,0:T(8,128)S(1)}, f32[2,64,128]{2,1,0:T(8,128)S(1)}, u32[]{:S(2)}, u32[]{:S(2)}) collective-permute-start(f32[2,64,128]{2,1,0:T(8,128)S(1)} %get-tuple-element.58), channel_id=1, source_target_pairs={{0,4},{1,5},{2,6},{3,7},{4,0},{5,1},{6,2},{7,3},{8,12},{9,13},{10,... | collective-permute-start | bytes 196616 | tf_op jit(solution)/shard_map/ppermute | solution.py:406
  44.9 8.0 %collective-permute-start.12 = (f32[2,64,128]{2,1,0:T(8,128)S(1)}, f32[2,64,128]{2,1,0:T(8,128)S(1)}, u32[]{:S(2)}, u32[]{:S(2)}) collective-permute-start(f32[2,64,128]{2,1,0:T(8,128)S(1)} %get-tuple-element.59), channel_id=1, source_target_pairs={{0,6},{1,7},{2,4},{3,5},{4,2},{5,3},{6,0},{7,1},{8,14},{9,15},{10,... | collective-permute-start | bytes 196616 | tf_op jit(solution)/shard_map/ppermute | solution.py:406
  48.5 5.2 %collective-permute-start.24 = (f32[2,64,128]{2,1,0:T(8,128)S(1)}, f32[2,64,128]{2,1,0:T(8,128)S(1)}, u32[]{:S(2)}, u32[]{:S(2)}) collective-permute-start(f32[2,64,128]{2,1,0:T(8,128)S(1)} %get-tuple-element.72), channel_id=1, source_target_pairs={{0,2},{1,3},{2,0},{3,1},{4,6},{5,7},{6,4},{7,5},{8,10},{9,11},{10,... | collective-permute-start | bytes 196616 | tf_op jit(solution)/shard_map/ppermute | solution.py:406
  48.6 9.2 %collective-permute-start.25 = (f32[2,64,128]{2,1,0:T(8,128)S(1)}, f32[2,64,128]{2,1,0:T(8,128)S(1)}, u32[]{:S(2)}, u32[]{:S(2)}) collective-permute-start(f32[2,64,128]{2,1,0:T(8,128)S(1)} %get-tuple-element.73), channel_id=1, source_target_pairs={{0,4},{1,5},{2,6},{3,7},{4,0},{5,1},{6,2},{7,3},{8,12},{9,13},{10,... | collective-permute-start | bytes 196616 | tf_op jit(solution)/shard_map/ppermute | solution.py:406
  50.1 7.8 %collective-permute-start.26 = (f32[2,64,128]{2,1,0:T(8,128)S(1)}, f32[2,64,128]{2,1,0:T(8,128)S(1)}, u32[]{:S(2)}, u32[]{:S(2)}) collective-permute-start(f32[2,64,128]{2,1,0:T(8,128)S(1)} %get-tuple-element.74), channel_id=1, source_target_pairs={{0,6},{1,7},{2,4},{3,5},{4,2},{5,3},{6,0},{7,1},{8,14},{9,15},{10,... | collective-permute-start | bytes 196616 | tf_op jit(solution)/shard_map/ppermute | solution.py:406
  58.7 9.2 %collective-permute-start.15 = (f32[2,64,512]{2,1,0:T(8,128)S(1)}, f32[2,64,512]{2,1,0:T(8,128)S(1)}, u32[]{:S(2)}, u32[]{:S(2)}) collective-permute-start(f32[2,64,512]{2,1,0:T(8,128)S(1)} %add.6.refs_0_), channel_id=1, source_target_pairs={{0,16},{8,24},{16,0},{24,8},{1,17},{9,25},{17,1},{25,9},{2,18},{10... | collective-permute-start | bytes 786440 | tf_op jit(solution)/shard_map/ppermute | solution.py:398
  60.3 9.2 %collective-permute-start.14 = (f32[2,64,512]{2,1,0:T(8,128)S(1)}, f32[2,64,512]{2,1,0:T(8,128)S(1)}, u32[]{:S(2)}, u32[]{:S(2)}) collective-permute-start(f32[2,64,512]{2,1,0:T(8,128)S(1)} %add.6.refs_0_), channel_id=1, source_target_pairs={{0,8},{8,0},{16,24},{24,16},{1,9},{9,1},{17,25},{25,17},{2,10},{10... | collective-permute-start | bytes 786440 | tf_op jit(solution)/shard_map/ppermute | solution.py:398
  61.8 9.1 %collective-permute-start.31 = (f32[64,512]{1,0:T(8,128)S(1)}, f32[64,512]{1,0:T(8,128)S(1)}, u32[]{:S(2)}, u32[]{:S(2)}) collective-permute-start(f32[64,512]{1,0:T(8,128)S(1)} %get-tuple-element.79), channel_id=1, source_target_pairs={{0,16},{8,24},{16,0},{24,8},{1,17},{9,25},{17,1},{25,9},{2,18},{10... | collective-permute-start | bytes 393224 | tf_op jit(solution)/shard_map/ppermute | solution.py:398
  62.4 9.9 %collective-permute-start.29 = (f32[64,512]{1,0:T(8,128)S(1)}, f32[64,512]{1,0:T(8,128)S(1)}, u32[]{:S(2)}, u32[]{:S(2)}) collective-permute-start(f32[64,512]{1,0:T(8,128)S(1)} %get-tuple-element.79), channel_id=1, source_target_pairs={{0,8},{8,0},{16,24},{24,16},{1,9},{9,1},{17,25},{25,17},{2,10},{10... | collective-permute-start | bytes 393224 | tf_op jit(solution)/shard_map/ppermute | solution.py:398
  63.3 12.5 %collective-permute-start.30 = (f32[64,512]{1,0:T(8,128)S(1)}, f32[64,512]{1,0:T(8,128)S(1)}, u32[]{:S(2)}, u32[]{:S(2)}) collective-permute-start(f32[64,512]{1,0:T(8,128)S(1)} %get-tuple-element.80), channel_id=1, source_target_pairs={{0,16},{8,24},{16,0},{24,8},{1,17},{9,25},{17,1},{25,9},{2,18},{10... | collective-permute-start | bytes 393224 | tf_op jit(solution)/shard_map/ppermute | solution.py:398
  67.9 7.1 %collective-permute-start.28 = (f32[64,512]{1,0:T(8,128)S(1)}, f32[64,512]{1,0:T(8,128)S(1)}, u32[]{:S(2)}, u32[]{:S(2)}) collective-permute-start(f32[64,512]{1,0:T(8,128)S(1)} %get-tuple-element.80), channel_id=1, source_target_pairs={{0,8},{8,0},{16,24},{24,16},{1,9},{9,1},{17,25},{25,17},{2,10},{10... | collective-permute-start | bytes 393224 | tf_op jit(solution)/shard_map/ppermute | solution.py:398
  69.4 8.4 %collective-permute-start.17 = (f32[64,512]{1,0:T(8,128)S(1)}, f32[64,512]{1,0:T(8,128)S(1)}, u32[]{:S(2)}, u32[]{:S(2)}) collective-permute-start(f32[64,512]{1,0:T(8,128)S(1)} %slice_bitcast_fusion.2), channel_id=1, source_target_pairs={{0,8},{8,0},{16,24},{24,16},{1,9},{9,1},{17,25},{25,17},{2,10},{10... | collective-permute-start | bytes 393224 | tf_op jit(solution)/shard_map/ppermute | solution.py:398
  71.0 6.9 %collective-permute-start.16 = (f32[64,512]{1,0:T(8,128)S(1)}, f32[64,512]{1,0:T(8,128)S(1)}, u32[]{:S(2)}, u32[]{:S(2)}) collective-permute-start(f32[64,512]{1,0:T(8,128)S(1)} %slice_bitcast_fusion.3), channel_id=1, source_target_pairs={{0,16},{8,24},{16,0},{24,8},{1,17},{9,25},{17,1},{25,9},{2,18},{10... | collective-permute-start | bytes 393224 | tf_op jit(solution)/shard_map/ppermute | solution.py:398
  72.3 8.5 %collective-permute-start.33 = (f32[64,512]{1,0:T(8,128)S(1)}, f32[64,512]{1,0:T(8,128)S(1)}, u32[]{:S(2)}, u32[]{:S(2)}) collective-permute-start(f32[64,512]{1,0:T(8,128)S(1)} %collective-permute-done.31.refs_9_), channel_id=1, source_target_pairs={{0,8},{8,0},{16,24},{24,16},{1,9},{9,1},{17,25},{25,17},{2,10},{10... | collective-permute-start | bytes 393224 | tf_op jit(solution)/shard_map/ppermute | solution.py:398
  75.1 5.7 %collective-permute-start.32 = (f32[64,512]{1,0:T(8,128)S(1)}, f32[64,512]{1,0:T(8,128)S(1)}, u32[]{:S(2)}, u32[]{:S(2)}) collective-permute-start(f32[64,512]{1,0:T(8,128)S(1)} %collective-permute-done.28.refs_6_), channel_id=1, source_target_pairs={{0,16},{8,24},{16,0},{24,8},{1,17},{9,25},{17,1},{25,9},{2,18},{10... | collective-permute-start | bytes 393224 | tf_op jit(solution)/shard_map/ppermute | solution.py:398
  (7 other events, 61.9 us)
